TPU v7x, 32 devices: a whole 2x2x4 slice. The times are simulated.
32 devices in a mesh: near: 16 (over z, y, x), far: 2 (over core).
Axes of the slice: x: 2, y: 2, z: 4, core: 2. Of those that a mesh axis runs over, the one named last changes fastest.
Arguments:
- vectors: bfloat16 [128, 4, 480], P('near'), may hold values from -6 to 6
- near_blocks: bfloat16 [128, 16, 2, 240, 240], P('near', 'far'), may hold values from -0.09375 to 0.09375
- neighbours: int32 [128, 16], P('near', 'far'), may hold values from 0 to 127, as said below
- live_counts: int32 [128], P('near'), may hold values from 4 to 16, as said below
- tmatrix: float32 [128, 2, 240], P('near'), may hold values from -0.8 to 0.8
- agg_matrix: bfloat16 [480, 512], replicated, may hold values from -0.25 to 0.25
- sphere_box: int32 [128], P('near'), may hold values from 0 to 15, never falling along the last dimension, each value on 1 to 24 neighbouring positions
- agg_angle: float32 [128, 256], P('near'), may hold values from -3.140625 to 3.140625
- far_list: int32 [16, 16], P('far'), may hold values from 0 to 15, as said below
- far_factors: float32 [16, 16, 2, 256], P('far', None, None, 'near'), may hold values from -0.6 to 0.6
- dis_matrix: bfloat16 [512, 480], replicated, may hold values from -0.25 to 0.25
Outputs:
- first_image: bfloat16 [128, 4, 480], P('near')
- second_image: bfloat16 [128, 4, 480], P('near')
Inputs may be any that keep to these rules, and one draw needn't show every extreme that they name: `neighbours`: each entry differs from its row's sphere number by 1 to 8. `live_counts`: slots at or above a sphere's count are padding; some sphere has all 16 slots live. `sphere_box`: box numbers never fall along the spheres; every box holds 1 to 24 spheres. `far_list`: a box's far list names neither the box nor the boxes numbered one above or below it, counted around.
All inputs are finite; a program needn't handle non-finite values.
Results may differ from a plain program's by a relative error of at most 0.0052.
Values may be sent and summed in bfloat16 or wider, within the bound.
No kernel may reach another device: no remote copies, remote signals or barrier semaphores. Data moves between devices by JAX's collectives and lax.ppermute only.
A program may use at most 64 MiB of HBM per device.

v0:
```python
import jax
import jax.numpy as jnp
from jax import lax
from jax.sharding import PartitionSpec as P


def with_halo(block, sides, width):
    for axis, dim in sides:
        count = lax.axis_size(axis)
        forward = [(i, i + 1) for i in range(count - 1)]
        backward = [(target, source) for source, target in forward]
        low = lax.ppermute(
            lax.slice_in_dim(block, block.shape[dim] - width, None, axis=dim), axis, forward
        )
        high = lax.ppermute(lax.slice_in_dim(block, 0, width, axis=dim), axis, backward)
        block = jnp.concatenate([low, block, high], axis=dim)
    return block


def complex_mul(left_re, left_im, right_re, right_im):
    return (left_re * right_re - left_im * right_im, left_re * right_im + left_im * right_re)


def outgoing_of(rows_vec, cos_rows, sin_rows, agg_matrix):
    count, newton, width = rows_vec.shape
    waves = agg_matrix.shape[1] // 2
    product = jnp.dot(
        rows_vec.reshape(count * newton, width), agg_matrix, preferred_element_type=jnp.float32
    )
    product = product.reshape(count, newton, 2, waves)
    out_re, out_im = complex_mul(
        product[:, :, 0], product[:, :, 1], cos_rows[:, None, :], sin_rows[:, None, :]
    )
    return jnp.stack([out_re, out_im], axis=2)


def apply_operator(
    current,
    near_blocks,
    neighbours,
    live_counts,
    tmatrix,
    agg_matrix,
    sphere_box,
    agg_angle,
    far_list,
    far_factors,
    dis_matrix,
):
    sph_count, newton, width = current.shape
    coeffs = width // 2
    slots = neighbours.shape[1]
    own_boxes = far_list.shape[0]
    far_count = lax.axis_size("far")
    all_boxes = own_boxes * far_count
    waves = agg_matrix.shape[1] // 2
    near_pos = lax.axis_index("near")
    far_pos = lax.axis_index("far")
    padded = with_halo(current, (("near", 0),), sph_count)
    local_index = neighbours - (near_pos - 1) * sph_count
    gathered = padded[local_index]
    alive = (far_pos * slots + jnp.arange(slots, dtype=jnp.int32))[None, :] < live_counts[:, None]
    gathered = jnp.where(alive[:, :, None, None], gathered, jnp.zeros_like(gathered))
    both_parts = jnp.concatenate([gathered[..., :coeffs], gathered[..., coeffs:]], axis=2)
    with_real = jnp.einsum(
        "nkrc,nkcd->nrd", both_parts, near_blocks[:, :, 0], preferred_element_type=jnp.float32
    )
    with_imag = jnp.einsum(
        "nkrc,nkcd->nrd", both_parts, near_blocks[:, :, 1], preferred_element_type=jnp.float32
    )
    near_re = with_real[:, :newton] - with_imag[:, newton:]
    near_im = with_imag[:, :newton] + with_real[:, newton:]
    near_field = jnp.concatenate([near_re, near_im], axis=-1)
    cosine = jnp.cos(agg_angle)
    sine = jnp.sin(agg_angle)
    stacked = outgoing_of(current, cosine, sine, agg_matrix)
    member = (
        sphere_box[None, :] == far_pos * own_boxes + jnp.arange(own_boxes, dtype=jnp.int32)[:, None]
    ).astype(jnp.float32)
    partial_value = jnp.einsum("bn,nrtq->brtq", member, stacked, precision=lax.Precision.HIGHEST)
    box_waves = lax.psum_scatter(partial_value, "near", scatter_dimension=3, tiled=True)
    all_waves = lax.all_gather(box_waves, "far", axis=0, tiled=True)
    selector = (
        far_list[:, :, None] == jnp.arange(all_boxes, dtype=jnp.int32)[None, None, :]
    ).astype(jnp.float32)
    picked = jnp.einsum("gfb,brtq->gfrtq", selector, all_waves, precision=lax.Precision.HIGHEST)
    in_re, in_im = complex_mul(
        far_factors[:, :, None, 0, :],
        far_factors[:, :, None, 1, :],
        picked[:, :, :, 0],
        picked[:, :, :, 1],
    )
    incoming = jnp.stack([jnp.sum(in_re, axis=1), jnp.sum(in_im, axis=1)], axis=2)
    full_waves = lax.all_gather(incoming, "near", axis=3, tiled=True)
    owner = (
        sphere_box[:, None] == far_pos * own_boxes + jnp.arange(own_boxes, dtype=jnp.int32)[None, :]
    ).astype(jnp.float32)
    sphere_waves = jnp.einsum("nb,brtq->nrtq", owner, full_waves, precision=lax.Precision.HIGHEST)
    local_re, local_im = complex_mul(
        sphere_waves[:, :, 0], sphere_waves[:, :, 1], cosine[:, None, :], -sine[:, None, :]
    )
    local_waves = jnp.concatenate([local_re, local_im], axis=-1).astype(jnp.bfloat16)
    far_field = jnp.dot(
        local_waves.reshape(sph_count * newton, 2 * waves),
        dis_matrix,
        preferred_element_type=jnp.float32,
    )
    far_field = far_field.reshape(sph_count, newton, width)
    field = lax.psum(near_field + far_field, "far")
    scat_re, scat_im = complex_mul(
        tmatrix[:, None, 0, :], tmatrix[:, None, 1, :], field[..., :coeffs], field[..., coeffs:]
    )
    image = current.astype(jnp.float32) - jnp.concatenate([scat_re, scat_im], axis=-1)
    return image.astype(jnp.bfloat16)


def shards(
    vectors,
    near_blocks,
    neighbours,
    live_counts,
    tmatrix,
    agg_matrix,
    sphere_box,
    agg_angle,
    far_list,
    far_factors,
    dis_matrix,
):
    first_image = apply_operator(
        vectors,
        near_blocks,
        neighbours,
        live_counts,
        tmatrix,
        agg_matrix,
        sphere_box,
        agg_angle,
        far_list,
        far_factors,
        dis_matrix,
    )
    second_image = apply_operator(
        first_image,
        near_blocks,
        neighbours,
        live_counts,
        tmatrix,
        agg_matrix,
        sphere_box,
        agg_angle,
        far_list,
        far_factors,
        dis_matrix,
    )
    return (first_image, second_image)


def solution(mesh):
    return jax.shard_map(
        shards,
        mesh=mesh,
        in_specs=(
            P("near", None, None),
            P("near", "far", None, None, None),
            P("near", "far"),
            P("near"),
            P("near", None, None),
            P(),
            P("near"),
            P("near", None),
            P("far", None),
            P("far", None, None, "near"),
            P(),
        ),
        out_specs=(P("near", None, None), P("near", None, None)),
        check_vma=False,
    )
```

profile of v0, /device:TPU:0, one launch (start us, length us, event | category | flops | bytes accessed | tf_op | source)
XLA Modules:
  0.0 290.1 jit_solution(10729382742883723635)
XLA Ops:
  7.3 5.0 %collective-permute-start = (bf16[8,4,480]{2,1,0:T(4,128)(2,1)}, bf16[8,4,480]{2,1,0:T(4,128)(2,1)S(1)}, u32[]{:S(2)}, u32[]{:S(2)}) collective-permute-start(bf16[8,4,480]{2,1,0:T(4,128)(2,1)} %param.11), channel_id=1, source_target_pairs={{0,2},{2,4},{4,6},{6,8},{8,10},{10,12},{12,14},{14,16},{16,18},{18... | collective-permute-start | bytes 92168 | tf_op jit(solution)/shard_map/ppermute | solution.py:12
  12.3 1.3 collective-permute-start.1
  13.6 0.7 fusion.80
  14.4 1.2 fusion.29
  15.6 0.9 fusion.34
  16.5 0.7 copy.86
  17.2 1.9 reshape.112
  19.3 1.1 fusion.78
  20.4 0.7 broadcast_compare_fusion
  21.9 0.8 fusion.79
  22.7 0.8 pad_maximum_fusion.6
  23.6 0.8 gather_fusion
  24.7 4.4 %fusion.12 = f32[8,8,240]{2,1,0:T(8,128)S(1)} fusion(bf16[8,8,2,240,240]{4,3,2,1,0:T(8,128)(2,1)} %param.12, bf16[8,8,4,240]{3,2,1,0:T(4,128)(2,1)S(1)} %get-tuple-element.9, bf16[8,8,4,240]{3,2,1,0:T(4,128)(2,1)S(1)} %get-tuple-element.8), kind=kOutput, calls=%fused_computation.14 | convolution fusion | flops 59473920 | bytes 8171520 | tf_op jit(solution)/shard_map/nkrc,nkcd->nrd/dot_general | solution.py:65
  29.2 4.4 %fusion.18 = f32[8,8,240]{2,1,0:T(8,128)S(1)} fusion(bf16[8,8,2,240,240]{4,3,2,1,0:T(8,128)(2,1)} %param.12, bf16[8,8,4,240]{3,2,1,0:T(4,128)(2,1)S(1)} %get-tuple-element.9, bf16[8,8,4,240]{3,2,1,0:T(4,128)(2,1)S(1)} %get-tuple-element.8), kind=kOutput, calls=%fused_computation.16 | convolution fusion | flops 59473920 | bytes 8171520 | tf_op jit(solution)/shard_map/nkrc,nkcd->nrd/dot_general | solution.py:68
  33.6 65.1 %reduce-scatter.7.cloned.1.call-done = f32[16,64]{1,0:T(8,128)} async-done(((f32[256,64]{1,0:T(8,128)}), f32[16,64]{1,0:T(8,128)}) %reduce-scatter.7.cloned.1.call-update) | async-done | bytes 4112
  98.7 0.8 reshape.113
  99.6 1.8 all_gather.12
  102.2 41.7 %all_gather.13 = f32[8,4,2,256]{0,1,2,3:T(4,128)S(1)} all-gather(f32[8,4,2,16]{0,1,2,3:T(4,128)S(1)} %copy.49), channel_id=1, replica_groups=mesh['near'=16,'far'=2] {'near'}, dimensions={3}, use_global_device_ids=true | all-gather | bytes 69632 | tf_op jit(solution)/shard_map/all_gather | solution.py:94
  144.9 3.6 %psum.14 = f32[8,4,480]{2,1,0:T(4,128)S(1)} all-reduce(f32[8,4,480]{2,1,0:T(4,128)S(1)} %convolution_add_fusion.1), channel_id=1, replica_groups=mesh['near'=16,'far'=2] {'far'}, use_global_device_ids=true, to_apply=%region_3.4 | all-reduce | flops 15360 | bytes 122880 | tf_op jit(solution)/shard_map/psum | solution.py:109
  148.7 4.0 %collective-permute-start.2 = (bf16[8,4,480]{2,1,0:T(4,128)(2,1)S(1)}, bf16[8,4,480]{2,1,0:T(4,128)(2,1)S(1)}, u32[]{:S(2)}, u32[]{:S(2)}) collective-permute-start(bf16[8,4,480]{2,1,0:T(4,128)(2,1)S(1)} %fusion.38), channel_id=1, source_target_pairs={{0,2},{2,4},{4,6},{6,8},{8,10},{10,12},{12,14},{14,16},{16,18},{18... | collective-permute-start | bytes 92168 | tf_op jit(solution)/shard_map/ppermute | solution.py:12
  152.8 1.3 collective-permute-start.3
  154.5 0.7 copy.88
  155.3 1.9 reshape.114
  157.3 1.3 collective-permute-done.3
  158.7 0.8 gather_fusion.1
  159.8 4.4 %fusion.15 = f32[8,8,240]{2,1,0:T(8,128)S(1)} fusion(bf16[8,8,2,240,240]{4,3,2,1,0:T(8,128)(2,1)} %param.12, bf16[8,8,4,240]{3,2,1,0:T(4,128)(2,1)S(1)} %get-tuple-element.7, bf16[8,8,4,240]{3,2,1,0:T(4,128)(2,1)S(1)} %get-tuple-element.6), kind=kOutput, calls=%fused_computation.15 | convolution fusion | flops 59473920 | bytes 8171520 | tf_op jit(solution)/shard_map/nkrc,nkcd->nrd/dot_general | solution.py:65
  164.3 4.4 %fusion.21 = f32[8,8,240]{2,1,0:T(8,128)S(1)} fusion(bf16[8,8,2,240,240]{4,3,2,1,0:T(8,128)(2,1)} %param.12, bf16[8,8,4,240]{3,2,1,0:T(4,128)(2,1)S(1)} %get-tuple-element.7, bf16[8,8,4,240]{3,2,1,0:T(4,128)(2,1)S(1)} %get-tuple-element.6), kind=kOutput, calls=%fused_computation.17 | convolution fusion | flops 59473920 | bytes 8171520 | tf_op jit(solution)/shard_map/nkrc,nkcd->nrd/dot_general | solution.py:68
  168.7 64.0 %reduce-scatter.9.cloned.1.call-done = f32[16,64]{1,0:T(8,128)} async-done(((f32[256,64]{1,0:T(8,128)}), f32[16,64]{1,0:T(8,128)}) %reduce-scatter.9.cloned.1.call-update) | async-done | bytes 4112
  232.7 0.8 reshape.115
  233.6 1.8 all_gather.14
  236.2 41.7 %all_gather.15 = f32[8,4,2,256]{0,1,2,3:T(4,128)S(1)} all-gather(f32[8,4,2,16]{0,1,2,3:T(4,128)S(1)} %copy.58), channel_id=1, replica_groups=mesh['near'=16,'far'=2] {'near'}, dimensions={3}, use_global_device_ids=true | all-gather | bytes 69632 | tf_op jit(solution)/shard_map/all_gather | solution.py:94
  278.9 3.6 %psum.15 = f32[8,4,480]{2,1,0:T(4,128)S(1)} all-reduce(f32[8,4,480]{2,1,0:T(4,128)S(1)} %convolution_add_fusion), channel_id=1, replica_groups=mesh['near'=16,'far'=2] {'far'}, use_global_device_ids=true, to_apply=%region_7.8 | all-reduce | flops 15360 | bytes 122880 | tf_op jit(solution)/shard_map/psum | solution.py:109
  (58 shorter events, 6.7 us)
Async XLA Ops:
  7.2 137.5 %copy-start = (bf16[512,480]{0,1:T(8,128)(2,1)S(1)}, bf16[512,480]{0,1:T(8,128)(2,1)}, u32[]{:S(2)}) copy-start(bf16[512,480]{0,1:T(8,128)(2,1)} %param.21) | copy-start | bytes 1474564
  7.2 141.4 %copy-start.3 = (bf16[8,4,480]{2,1,0:T(4,128)(2,1)S(1)}, bf16[8,4,480]{2,1,0:T(4,128)(2,1)}, u32[]{:S(2)}) copy-start(bf16[8,4,480]{2,1,0:T(4,128)(2,1)} %param.11) | copy-start | bytes 92164
  7.2 146.9 %copy-start.1 = (bf16[480,512]{1,0:T(8,128)(2,1)S(1)}, bf16[480,512]{1,0:T(8,128)(2,1)}, u32[]{:S(2)}) copy-start(bf16[480,512]{1,0:T(8,128)(2,1)} %param.16) | copy-start | bytes 1474564
  7.2 136.7 %copy-start.5 = (s32[8]{0:T(128)S(1)}, s32[8]{0:T(128)}, u32[]{:S(2)}) copy-start(s32[8]{0:T(128)} %param.17) | copy-start | bytes 100
  7.2 94.3 %copy-start.4 = (s32[8,16]{1,0:T(8,128)S(1)}, s32[8,16]{1,0:T(8,128)}, u32[]{:S(2)}) copy-start(s32[8,16]{1,0:T(8,128)} %param.19) | copy-start | bytes 1540
  7.2 91.5 %reduce-scatter.7.cloned.1.call-start = ((), (), s32[]{:S(2)}) async-start(), calls=%async_computation.2 | async-start | bytes 139264
  7.3 15.5 %collective-permute-start = (bf16[8,4,480]{2,1,0:T(4,128)(2,1)}, bf16[8,4,480]{2,1,0:T(4,128)(2,1)S(1)}, u32[]{:S(2)}, u32[]{:S(2)}) collective-permute-start(bf16[8,4,480]{2,1,0:T(4,128)(2,1)} %param.11), channel_id=1, source_target_pairs={{0,2},{2,4},{4,6},{6,8},{8,10},{10,12},{12,14},{14,16},{16,18},{18... | collective-permute-start | bytes 92168 | tf_op jit(solution)/shard_map/ppermute | solution.py:12
  12.3 10.5 %collective-permute-start.1 = (bf16[8,4,480]{2,1,0:T(4,128)(2,1)}, bf16[8,4,480]{2,1,0:T(4,128)(2,1)S(1)}, u32[]{:S(2)}, u32[]{:S(2)}) collective-permute-start(bf16[8,4,480]{2,1,0:T(4,128)(2,1)} %param.11), channel_id=1, source_target_pairs={{2,0},{4,2},{6,4},{8,6},{10,8},{12,10},{14,12},{16,14},{18,16},{20... | collective-permute-start | bytes 92168 | tf_op jit(solution)/shard_map/ppermute | solution.py:15
  19.2 213.5 %reduce-scatter.9.cloned.1.call-start = ((), (), s32[]{:S(2)}) async-start(), calls=%async_computation.3 | async-start | bytes 139264
  148.7 134.5 %copy-start.2 = (bf16[8,4,480]{2,1,0:T(4,128)(2,1)}, bf16[8,4,480]{2,1,0:T(4,128)(2,1)S(1)}, u32[]{:S(2)}) copy-start(bf16[8,4,480]{2,1,0:T(4,128)(2,1)S(1)} %fusion.38) | copy-start | bytes 92164
  148.7 8.5 %collective-permute-start.2 = (bf16[8,4,480]{2,1,0:T(4,128)(2,1)S(1)}, bf16[8,4,480]{2,1,0:T(4,128)(2,1)S(1)}, u32[]{:S(2)}, u32[]{:S(2)}) collective-permute-start(bf16[8,4,480]{2,1,0:T(4,128)(2,1)S(1)} %fusion.38), channel_id=1, source_target_pairs={{0,2},{2,4},{4,6},{6,8},{8,10},{10,12},{12,14},{14,16},{16,18},{18... | collective-permute-start | bytes 92168 | tf_op jit(solution)/shard_map/ppermute | solution.py:12
  152.8 5.8 %collective-permute-start.3 = (bf16[8,4,480]{2,1,0:T(4,128)(2,1)S(1)}, bf16[8,4,480]{2,1,0:T(4,128)(2,1)S(1)}, u32[]{:S(2)}, u32[]{:S(2)}) collective-permute-start(bf16[8,4,480]{2,1,0:T(4,128)(2,1)S(1)} %fusion.38), channel_id=1, source_target_pairs={{2,0},{4,2},{6,4},{8,6},{10,8},{12,10},{14,12},{16,14},{18,16},{20... | collective-permute-start | bytes 92168 | tf_op jit(solution)/shard_map/ppermute | solution.py:15
Sparse Core Ops, SparseCore 0:
  19.3 79.3 reduce-scatter.6
  157.4 75.2 reduce-scatter.8
where the time goes:
time: 291 us; the launch traced here: 290 us
  waiting for transfers between devices  130 us (45%)
  blocking collectives  94.3 us (32%)
  matrix products  22.9 us (8%)
  between operations  14.5 us (5%)
  local copies, waits for them, and re-layouts  12.1 us (4%)
  starting transfers between devices  11.7 us (4%)
  other arithmetic  4.22 us (1%)
    unnamed x4, waiting for transfers between devices  129 us
    all_gather x2, blocking collectives, apply_operator(): full_waves = lax.all_gather(incoming, 'near', axis=3, tiled=True)  83.4 us
    ppermute x2, starting transfers between devices, with_halo(): lax.ppermute(lax.slice_in_dim(block, block.shape[dim] - width, None, axis...  9.03 us
    dot_general x2, matrix products, apply_operator(): jnp.einsum('nkrc,nkcd->nrd', both_parts, near_blocks[:, :, 0], preferred_...  8.88 us
    dot_general x2, matrix products, apply_operator(): jnp.einsum('nkrc,nkcd->nrd', both_parts, near_blocks[:, :, 1], preferred_...  8.84 us
    unnamed x20, local copies, waits for them, and re-layouts  7.23 us
    psum x2, blocking collectives, apply_operator(): field = lax.psum(near_field + far_field, 'far')  7.18 us
  transfers between devices with their start and end apart: 6, of which 3 were waited for; matrix products, arithmetic and copies ran while one was open for 11% of the time, Pallas kernels for 0%

commit v1 on v0

v1 whole, which is shorter than its diff:
```python
import jax
import jax.numpy as jnp
from jax import lax
from jax.sharding import PartitionSpec as P

F32 = jnp.float32
BF16 = jnp.bfloat16
RADIX = 4


def complex_mul(left_re, left_im, right_re, right_im):
    return (left_re * right_re - left_im * right_im, left_re * right_im + left_im * right_re)


def swap_near(block, mask):
    count = lax.axis_size("near")
    return lax.ppermute(block, "near", [(i, i ^ mask) for i in range(count)])


def phase_masks():
    count = lax.axis_size("near")
    phases, step = [], 1
    while step < count:
        radix = min(RADIX, count // step)
        phases.append([step * j for j in range(1, radix)])
        step *= radix
    return phases


def xor_gather(block, masks):
    return [block] + [swap_near(block, mask) for mask in masks]


def in_order(parts, masks):
    step = masks[0]
    digit = lax.axis_index("near") // step % len(parts)
    stacked = jnp.stack(parts)
    return jnp.take(stacked, jnp.arange(len(parts)) ^ digit, axis=0)


def edge_rows(block):
    count = lax.axis_size("near")
    pairs = []
    for low in range(RADIX, count, RADIX):
        pairs.append((low - 1, low))
        pairs.append((low, low - 1))
    return lax.ppermute(block, "near", pairs) if pairs else jnp.zeros_like(block)


def over_far(block):
    count = lax.axis_size("far")
    if count == 2:
        other = lax.ppermute(block, "far", [(0, 1), (1, 0)])
        first = lax.axis_index("far") == 0
        return jnp.stack([jnp.where(first, block, other), jnp.where(first, other, block)])
    return lax.all_gather(block, "far", axis=0)


def near_share(partial, share):
    count = lax.axis_size("far")
    far_pos = lax.axis_index("far")
    mine = lax.dynamic_slice_in_dim(partial, far_pos % (partial.shape[1] // share) * share, share, 1)
    if count == 2:
        theirs = lax.dynamic_slice_in_dim(partial, (1 - far_pos) * share, share, 1)
        return mine + lax.ppermute(theirs, "far", [(0, 1), (1, 0)])
    total = lax.psum(partial, "far")
    return lax.dynamic_slice_in_dim(total, far_pos % (partial.shape[1] // share) * share, share, 1)


def shards(
    vectors,
    near_blocks,
    neighbours,
    live_counts,
    tmatrix,
    agg_matrix,
    sphere_box,
    agg_angle,
    far_list,
    far_factors,
    dis_matrix,
):
    spheres, newton, width = vectors.shape
    coeffs = width // 2
    slots = neighbours.shape[1]
    far_count = lax.axis_size("far")
    near_count = lax.axis_size("near")
    own_boxes, listed = far_list.shape
    boxes = own_boxes * far_count
    waves = agg_matrix.shape[1] // 2
    share = newton // min(far_count, newton)
    splits = newton // share
    near_pos = lax.axis_index("near")
    far_pos = lax.axis_index("far")
    phases = phase_masks()
    rows = spheres * share

    def own_share(block):
        return lax.dynamic_slice_in_dim(block, far_pos % splits * share, share, 1)

    hi = agg_angle.astype(BF16)
    low = (agg_angle - hi.astype(F32)).astype(BF16)
    factors = far_factors.astype(BF16).reshape(-1, far_factors.shape[-1]).T
    per_part = factors.size
    lists = over_far_lists(far_list)
    extra = jnp.concatenate(
        [
            jnp.repeat(sphere_box, share).astype(BF16)[:, None],
            jnp.stack([hi, low]).reshape(rows, -1),
            factors.reshape(rows, -1),
        ],
        axis=1,
    )
    angle_width = 2 * spheres * waves // rows

    cosine = jnp.cos(agg_angle)
    sine = jnp.sin(agg_angle)
    alive = (far_pos * slots + jnp.arange(slots, dtype=jnp.int32))[None, :] < live_counts[:, None]
    chip = neighbours // spheres
    place = jnp.where(chip // RADIX == near_pos // RADIX, chip ^ near_pos, RADIX)
    local_index = place * spheres + neighbours % spheres

    state = {}
    images = []
    current = own_share(vectors)
    whole = vectors
    for step in range(2):
        flat = current.reshape(rows, width)
        edge = edge_rows(current)
        message = jnp.concatenate([flat, extra], axis=1) if step == 0 else flat
        parts = xor_gather(message, phases[0])
        group = len(parts)
        around = [p[:, :width].reshape(spheres, share, width) for p in parts]
        full = over_far(jnp.stack(around + [edge]))[:splits]
        full = jnp.moveaxis(full, 0, 2).reshape((group + 1) * spheres, newton, width)
        if step == 1:
            images.append(full[:spheres])
        if step == 0:
            box_ids = jnp.concatenate([p[:, width].reshape(spheres, share)[:, 0] for p in parts])
            angles = jnp.stack(
                [
                    p[:, width + 1 : width + 1 + angle_width].reshape(2, spheres, waves)
                    for p in parts
                ]
            ).astype(F32)
            angles = (angles[:, 0] + angles[:, 1]).reshape(group * spheres, waves)
            state["cos"], state["sin"] = jnp.cos(angles), jnp.sin(angles)
            state["member"] = (
                box_ids.astype(jnp.int32)[None, :] == jnp.arange(boxes, dtype=jnp.int32)[:, None]
            ).astype(F32)
            table = in_order([p[:, width + 1 + angle_width :] for p in parts], phases[0])
        product = jnp.dot(
            jnp.concatenate(around).reshape(group * rows, width),
            agg_matrix,
            preferred_element_type=F32,
        ).reshape(group * spheres, share, 2, waves)
        out_re, out_im = complex_mul(
            product[:, :, 0], product[:, :, 1], state["cos"][:, None], state["sin"][:, None]
        )
        stacked = jnp.concatenate([out_re, out_im], axis=-1)
        sums = jnp.einsum("bn,nrq->brq", state["member"], stacked, precision=lax.Precision.HIGHEST)
        for masks in phases[1:]:
            block = sums.astype(BF16).reshape(boxes * share, 2 * waves)
            if step == 0:
                block = jnp.concatenate([block, table.reshape(boxes * share, -1)], axis=1)
            pieces = xor_gather(block, masks)
            sums = sum(p[:, : 2 * waves].astype(F32) for p in pieces)
            sums = sums.reshape(boxes, share, 2 * waves)
            if step == 0:
                table = in_order([p[:, 2 * waves :] for p in pieces], masks)
        if step == 0:
            table = over_far(table.reshape(waves, own_boxes, listed, 2))
            table = table.transpose(0, 2, 3, 4, 1).reshape(boxes, listed, 2, waves)
            state["factors"] = table[sphere_box].astype(F32)
            state["sources"] = (
                lists[sphere_box][:, :, None] == jnp.arange(boxes, dtype=jnp.int32)
            ).astype(F32)
        gathered = jnp.where(alive[:, :, None, None], full[local_index], jnp.zeros((), BF16))
        both = jnp.concatenate([gathered[..., :coeffs], gathered[..., coeffs:]], axis=2)
        with_real = jnp.einsum(
            "nkrc,nkcd->nrd", both, near_blocks[:, :, 0], preferred_element_type=F32
        )
        with_imag = jnp.einsum(
            "nkrc,nkcd->nrd", both, near_blocks[:, :, 1], preferred_element_type=F32
        )
        near_re = with_real[:, :newton] - with_imag[:, newton:]
        near_im = with_imag[:, :newton] + with_real[:, newton:]
        near_field = near_share(jnp.concatenate([near_re, near_im], axis=-1), share)
        picked = jnp.einsum(
            "nfb,brq->nfrq", state["sources"], sums, precision=lax.Precision.HIGHEST
        )
        fac = state["factors"]
        in_re, in_im = complex_mul(
            fac[:, :, None, 0], fac[:, :, None, 1], picked[..., :waves], picked[..., waves:]
        )
        in_re, in_im = jnp.sum(in_re, axis=1), jnp.sum(in_im, axis=1)
        local_re, local_im = complex_mul(in_re, in_im, cosine[:, None], -sine[:, None])
        local_waves = jnp.concatenate([local_re, local_im], axis=-1).astype(BF16)
        far_field = jnp.dot(
            local_waves.reshape(rows, 2 * waves), dis_matrix, preferred_element_type=F32
        ).reshape(spheres, share, width)
        field = near_field + far_field
        scat_re, scat_im = complex_mul(
            tmatrix[:, None, 0], tmatrix[:, None, 1], field[..., :coeffs], field[..., coeffs:]
        )
        current = (current.astype(F32) - jnp.concatenate([scat_re, scat_im], axis=-1)).astype(BF16)
    last = over_far(current)[:splits]
    images.append(jnp.moveaxis(last, 0, 1).reshape(spheres, newton, width))
    return tuple(images)


def over_far_lists(far_list):
    gathered = over_far(far_list)
    return gathered.reshape(-1, far_list.shape[1])


def solution(mesh):
    return jax.shard_map(
        shards,
        mesh=mesh,
        in_specs=(
            P("near", None, None),
            P("near", "far", None, None, None),
            P("near", "far"),
            P("near"),
            P("near", None, None),
            P(),
            P("near"),
            P("near", None),
            P("far", None),
            P("far", None, None, "near"),
            P(),
        ),
        out_specs=(P("near", None, None), P("near", None, None)),
        check_vma=False,
    )
```

time: 291 us -> 152 us (0.52)
  waiting for transfers between devices: 130 us -> 12.1 us
  blocking collectives: 94.3 us -> 0 us
  local copies, waits for them, and re-layouts: 12.1 us -> 73.6 us
  other arithmetic: 4.22 us -> 19.3 us
  between operations: 14.5 us -> 1.5 us
  starting transfers between devices: 11.7 us -> 23.5 us
    unnamed x4 -> x0, waiting for transfers between devices: 129 us -> none
    all_gather x4 -> x0, blocking collectives: 87.1 us -> none  [the longest x2 83.4 us: apply_operator(): full_waves = lax.all_gather(incoming, 'near', axis=3, tiled=True)]
    select_n x0 -> x4, local copies, waits for them, and re-layouts: none -> 29.6 us  [in_order(): return jnp.take(stacked, jnp.arange(len(parts)) ^ digit, axis=0)]
    another operation x2 -> x19, local copies, waits for them, and re-layouts: 0.2 us -> 21.3 us  [the longest x2 20.6 us: over_far(): jnp.stack([jnp.where(first, block, other), jnp.where(first, other, block)])]
    ppermute x0 -> x1, local copies, waits for them, and re-layouts: none -> 13.8 us  [over_far(): other = lax.ppermute(block, 'far', [(0, 1), (1, 0)])]
    another operation x4 -> x11, other arithmetic: 0.06 us -> 12.4 us  [the longest x6 12.4 us: over_far(): jnp.stack([jnp.where(first, block, other), jnp.where(first, other, block)])]
    ppermute x4 -> x21, starting transfers between devices: 11.6 us -> 23.5 us  [the longest x12 20.9 us: swap_near(): return lax.ppermute(block, 'near', [(i, i ^ mask) for i in range(count)])]
    ppermute x4 -> x21, waiting for transfers between devices: 1.34 us -> 12.1 us  [the longest x12 10.7 us: swap_near(): return lax.ppermute(block, 'near', [(i, i ^ mask) for i in range(count)])]
  transfers between devices with their start and end apart: 6 -> 21, of which waited for: 3 -> 8; matrix products, arithmetic and copies ran while one was open for 11% -> 65% of each run, Pallas kernels for 0% -> 0%
where the time goes in v1:
time: 152 us; the launch traced here: 151 us
  local copies, waits for them, and re-layouts  73.6 us (48%)
  starting transfers between devices  23.5 us (15%)
  matrix products  20.7 us (14%)
  other arithmetic  19.3 us (13%)
  waiting for transfers between devices  12.1 us (8%)
    select_n x4, local copies, waits for them, and re-layouts, in_order(): return jnp.take(stacked, jnp.arange(len(parts)) ^ digit, axis=0)  29.6 us
    ppermute x12, starting transfers between devices, swap_near(): return lax.ppermute(block, 'near', [(i, i ^ mask) for i in range(count)])  20.9 us
    another operation x2, local copies, waits for them, and re-layouts, over_far(): jnp.stack([jnp.where(first, block, other), jnp.where(first, other, block)])  20.6 us
    ppermute x1, local copies, waits for them, and re-layouts, over_far(): other = lax.ppermute(block, 'far', [(0, 1), (1, 0)])  13.8 us
    another operation x6, other arithmetic, over_far(): jnp.stack([jnp.where(first, block, other), jnp.where(first, other, block)])  12.4 us
    ppermute x12, waiting for transfers between devices, swap_near(): return lax.ppermute(block, 'near', [(i, i ^ mask) for i in range(count)])  10.7 us
    dot_general x2, matrix products, shards(): jnp.einsum('nkrc,nkcd->nrd', both, near_blocks[:, :, 1], preferred_elemen...  8.84 us
    dot_general x2, matrix products, shards(): jnp.einsum('nkrc,nkcd->nrd', both, near_blocks[:, :, 0], preferred_elemen...  8.84 us
  transfers between devices with their start and end apart: 21, of which 8 were waited for; matrix products, arithmetic and copies ran while one was open for 65% of the time, Pallas kernels for 0%

profile of v1, /device:TPU:0, one launch (start us, length us, event | category | flops | bytes accessed | tf_op | source)
XLA Modules:
  0.0 150.7 jit_solution(3371983806514256342)
XLA Ops:
  0.7 0.8 constant_dynamic-update-slice_fusion.4
  1.5 0.8 fusion.102
  2.4 0.7 compare_select_fusion.1
  3.2 1.0 convert_element_type.97
  4.4 3.0 %collective-permute-start = (bf16[16,993]{1,0:T(8,128)(2,1)S(1)}, bf16[16,993]{1,0:T(8,128)(2,1)S(1)}, u32[]{:S(2)}, u32[]{:S(2)}) collective-permute-start(bf16[16,993]{1,0:T(8,128)(2,1)S(1)} %pad_maximum_fusion.9), channel_id=1, source_target_pairs={{0,2},{2,0},{4,6},{6,4},{8,10},{10,8},{12,14},{14,12},{16,18},{18,... | collective-permute-start | bytes 95336 | tf_op jit(solution)/shard_map/ppermute | solution.py:17
  7.4 1.5 %collective-permute-start.1 = (bf16[16,993]{1,0:T(8,128)(2,1)S(1)}, bf16[16,993]{1,0:T(8,128)(2,1)S(1)}, u32[]{:S(2)}, u32[]{:S(2)}) collective-permute-start(bf16[16,993]{1,0:T(8,128)(2,1)S(1)} %pad_maximum_fusion.9), channel_id=1, source_target_pairs={{0,4},{2,6},{4,0},{6,2},{8,12},{10,14},{12,8},{14,10},{16,20},{18,... | collective-permute-start | bytes 95336 | tf_op jit(solution)/shard_map/ppermute | solution.py:17
  10.6 0.8 fusion.101
  15.2 1.2 fusion.24
  17.6 7.5 %collective-permute-start.8 = (bf16[32,1024]{1,0:T(8,128)(2,1)S(1)}, bf16[32,1024]{1,0:T(8,128)(2,1)S(1)}, u32[]{:S(2)}, u32[]{:S(2)}) collective-permute-start(bf16[32,1024]{1,0:T(8,128)(2,1)S(1)} %constant_dynamic-update-slice_fusion.5), channel_id=1, source_target_pairs={{0,24},{2,26},{4,28},{6,30},{8,16},{10,18},{12,20},{14,22},{16,8},... | collective-permute-start | bytes 196616 | tf_op jit(solution)/shard_map/ppermute | solution.py:17
  26.0 2.0 %collective-permute-done.8 = bf16[32,1024]{1,0:T(8,128)(2,1)S(1)} collective-permute-done((bf16[32,1024]{1,0:T(8,128)(2,1)S(1)}, bf16[32,1024]{1,0:T(8,128)(2,1)S(1)}, u32[]{:S(2)}, u32[]{:S(2)}) %collective-permute-start.8) | collective-permute-done | bytes 65568 | tf_op jit(solution)/shard_map/ppermute | solution.py:17
  28.0 3.2 %collective-permute-done.7 = bf16[32,1024]{1,0:T(8,128)(2,1)S(1)} collective-permute-done((bf16[32,1024]{1,0:T(8,128)(2,1)S(1)}, bf16[32,1024]{1,0:T(8,128)(2,1)S(1)}, u32[]{:S(2)}, u32[]{:S(2)}) %collective-permute-start.7) | collective-permute-done | bytes 65568 | tf_op jit(solution)/shard_map/ppermute | solution.py:17
  31.9 19.2 %select_n.204 = bf16[256,8,16,2]{3,2,1,0:T(8,128)(2,1)} reshape(bf16[4,32,512]{2,1,0:T(8,128)(2,1)S(1)} %broadcast_select_fusion.6) | data formatting | bytes 262144 | tf_op jit(solution)/shard_map/jit(_take)/select_n | solution.py:38
  51.1 10.3 %copy.101 = bf16[256,8,16,2]{0,2,3,1:T(8,128)(2,1)S(1)} copy(bf16[256,8,16,2]{3,2,1,0:T(8,128)(2,1)} %select_n.204) | data formatting | bytes 262144 | tf_op jit(solution)/shard_map/jit(_take)/select_n | solution.py:38
  62.5 0.8 gather_fusion
  63.7 4.4 %fusion.18 = f32[8,8,240]{2,1,0:T(8,128)S(1)} fusion(bf16[8,8,2,240,240]{4,3,2,1,0:T(8,128)(2,1)} %param.12, bf16[8,8,4,240]{3,2,1,0:T(4,128)(2,1)S(1)} %get-tuple-element.23, bf16[8,8,4,240]{3,2,1,0:T(4,128)(2,1)S(1)} %get-tuple-element.22), kind=kOutput, calls=%fused_computation.22 | convolution fusion | flops 59473920 | bytes 8171520 | tf_op jit(solution)/shard_map/nkrc,nkcd->nrd/dot_general | solution.py:183
  68.1 4.4 %fusion.12 = f32[8,8,240]{2,1,0:T(8,128)S(1)} fusion(bf16[8,8,2,240,240]{4,3,2,1,0:T(8,128)(2,1)} %param.12, bf16[8,8,4,240]{3,2,1,0:T(4,128)(2,1)S(1)} %get-tuple-element.23, bf16[8,8,4,240]{3,2,1,0:T(4,128)(2,1)S(1)} %get-tuple-element.22), kind=kOutput, calls=%fused_computation.20 | convolution fusion | flops 59473920 | bytes 8171520 | tf_op jit(solution)/shard_map/nkrc,nkcd->nrd/dot_general | solution.py:180
  73.2 13.8 %copy.102 = bf16[256,8,16,2]{3,2,1,0:T(8,128)(2,1)} copy(bf16[256,8,16,2]{0,2,3,1:T(8,128)(2,1)S(1)} %collective-permute-done.9) | data formatting | bytes 262144 | tf_op jit(solution)/shard_map/ppermute | solution.py:53
  87.0 11.3 %select_bitcast_fusion.1 = (bf16[1,256,8,16,2]{4,3,2,1,0:T(8,128)(2,1)}, bf16[1,256,8,16,2]{4,3,2,1,0:T(8,128)(2,1)}) fusion(bf16[256,8,16,2]{3,2,1,0:T(8,128)(2,1)} %select_n.204, bf16[256,8,16,2]{3,2,1,0:T(8,128)(2,1)} %copy.102, pred[]{:T(512)S(6)} %eq.47), kind=kLoop, calls=%fused_computation.7 | loop fusion | flops 131072 | bytes 524289 | tf_op jit(solution)/shard_map/stack | solution.py:55
  98.3 10.3 %copy.104 = bf16[1,256,8,16,2]{1,3,4,2,0:T(8,128)(2,1)S(1)} copy(bf16[1,256,8,16,2]{4,3,2,1,0:T(8,128)(2,1)} %get-tuple-element.16) | data formatting | bytes 262144 | tf_op jit(solution)/shard_map/stack | solution.py:55
  108.7 10.3 %copy.105 = bf16[1,256,8,16,2]{1,3,4,2,0:T(8,128)(2,1)S(1)} copy(bf16[1,256,8,16,2]{4,3,2,1,0:T(8,128)(2,1)} %get-tuple-element.17) | data formatting | bytes 262144 | tf_op jit(solution)/shard_map/stack | solution.py:55
  120.4 2.2 %collective-permute-start.12 = (bf16[16,480]{1,0:T(8,128)(2,1)S(1)}, bf16[16,480]{1,0:T(8,128)(2,1)S(1)}, u32[]{:S(2)}, u32[]{:S(2)}) collective-permute-start(bf16[16,480]{1,0:T(8,128)(2,1)S(1)} %reshape.278), channel_id=1, source_target_pairs={{0,4},{2,6},{4,0},{6,2},{8,12},{10,14},{12,8},{14,10},{16,20},{18,... | collective-permute-start | bytes 46088 | tf_op jit(solution)/shard_map/ppermute | solution.py:17
  122.6 1.3 collective-permute-start.13
  124.0 0.9 collective-permute-start.14
  125.0 2.2 %collective-permute-done.13 = bf16[16,480]{1,0:T(8,128)(2,1)S(1)} collective-permute-done((bf16[16,480]{1,0:T(8,128)(2,1)S(1)}, bf16[16,480]{1,0:T(8,128)(2,1)S(1)}, u32[]{:S(2)}, u32[]{:S(2)}) %collective-permute-start.13) | collective-permute-done | bytes 15392 | tf_op jit(solution)/shard_map/ppermute | solution.py:17
  127.8 2.2 %collective-permute-start.17 = (bf16[32,512]{1,0:T(8,128)(2,1)S(1)}, bf16[32,512]{1,0:T(8,128)(2,1)S(1)}, u32[]{:S(2)}, u32[]{:S(2)}) collective-permute-start(bf16[32,512]{1,0:T(8,128)(2,1)S(1)} %reshape.283), channel_id=1, source_target_pairs={{0,8},{2,10},{4,12},{6,14},{8,0},{10,2},{12,4},{14,6},{16,24},{18,... | collective-permute-start | bytes 98312 | tf_op jit(solution)/shard_map/ppermute | solution.py:17
  130.1 2.3 %collective-permute-start.19 = (bf16[32,512]{1,0:T(8,128)(2,1)S(1)}, bf16[32,512]{1,0:T(8,128)(2,1)S(1)}, u32[]{:S(2)}, u32[]{:S(2)}) collective-permute-start(bf16[32,512]{1,0:T(8,128)(2,1)S(1)} %reshape.283), channel_id=1, source_target_pairs={{0,24},{2,26},{4,28},{6,30},{8,16},{10,18},{12,20},{14,22},{16,8},... | collective-permute-start | bytes 98312 | tf_op jit(solution)/shard_map/ppermute | solution.py:17
  132.7 2.1 %collective-permute-done.18 = bf16[32,512]{1,0:T(8,128)(2,1)S(1)} collective-permute-done((bf16[32,512]{1,0:T(8,128)(2,1)S(1)}, bf16[32,512]{1,0:T(8,128)(2,1)S(1)}, u32[]{:S(2)}, u32[]{:S(2)}) %collective-permute-start.18) | collective-permute-done | bytes 32800 | tf_op jit(solution)/shard_map/ppermute | solution.py:17
  134.8 1.0 collective-permute-done.19
  137.0 0.8 gather_fusion.5
  138.2 4.4 %fusion.21 = f32[8,8,240]{2,1,0:T(8,128)S(1)} fusion(bf16[8,8,2,240,240]{4,3,2,1,0:T(8,128)(2,1)} %param.12, bf16[8,8,4,240]{3,2,1,0:T(4,128)(2,1)S(1)} %get-tuple-element.19, bf16[8,8,4,240]{3,2,1,0:T(4,128)(2,1)S(1)} %get-tuple-element.18), kind=kOutput, calls=%fused_computation.23 | convolution fusion | flops 59473920 | bytes 8171520 | tf_op jit(solution)/shard_map/nkrc,nkcd->nrd/dot_general | solution.py:183
  142.6 4.4 %fusion.15 = f32[8,8,240]{2,1,0:T(8,128)S(1)} fusion(bf16[8,8,2,240,240]{4,3,2,1,0:T(8,128)(2,1)} %param.12, bf16[8,8,4,240]{3,2,1,0:T(4,128)(2,1)S(1)} %get-tuple-element.19, bf16[8,8,4,240]{3,2,1,0:T(4,128)(2,1)S(1)} %get-tuple-element.18), kind=kOutput, calls=%fused_computation.21 | convolution fusion | flops 59473920 | bytes 8171520 | tf_op jit(solution)/shard_map/nkrc,nkcd->nrd/dot_general | solution.py:180
  147.5 1.0 collective-permute-done.16
  (161 shorter events, 16.9 us)
Async XLA Ops:
  0.6 119.1 %copy-start = (bf16[512,480]{0,1:T(8,128)(2,1)S(1)}, bf16[512,480]{0,1:T(8,128)(2,1)}, u32[]{:S(2)}) copy-start(bf16[512,480]{0,1:T(8,128)(2,1)} %param.21) | copy-start | bytes 1474564
  4.4 9.1 %collective-permute-start = (bf16[16,993]{1,0:T(8,128)(2,1)S(1)}, bf16[16,993]{1,0:T(8,128)(2,1)S(1)}, u32[]{:S(2)}, u32[]{:S(2)}) collective-permute-start(bf16[16,993]{1,0:T(8,128)(2,1)S(1)} %pad_maximum_fusion.9), channel_id=1, source_target_pairs={{0,2},{2,0},{4,6},{6,4},{8,10},{10,8},{12,14},{14,12},{16,18},{18,... | collective-permute-start | bytes 95336 | tf_op jit(solution)/shard_map/ppermute | solution.py:17
  7.4 6.1 %collective-permute-start.1 = (bf16[16,993]{1,0:T(8,128)(2,1)S(1)}, bf16[16,993]{1,0:T(8,128)(2,1)S(1)}, u32[]{:S(2)}, u32[]{:S(2)}) collective-permute-start(bf16[16,993]{1,0:T(8,128)(2,1)S(1)} %pad_maximum_fusion.9), channel_id=1, source_target_pairs={{0,4},{2,6},{4,0},{6,2},{8,12},{10,14},{12,8},{14,10},{16,20},{18,... | collective-permute-start | bytes 95336 | tf_op jit(solution)/shard_map/ppermute | solution.py:17
  8.9 4.8 %collective-permute-start.2 = (bf16[16,993]{1,0:T(8,128)(2,1)S(1)}, bf16[16,993]{1,0:T(8,128)(2,1)S(1)}, u32[]{:S(2)}, u32[]{:S(2)}) collective-permute-start(bf16[16,993]{1,0:T(8,128)(2,1)S(1)} %pad_maximum_fusion.9), channel_id=1, source_target_pairs={{0,6},{2,4},{4,2},{6,0},{8,14},{10,12},{12,10},{14,8},{16,22},{18,... | collective-permute-start | bytes 95336 | tf_op jit(solution)/shard_map/ppermute | solution.py:17
  8.9 17.0 %collective-permute-start.3 = (bf16[8,2,480]{2,1,0:T(2,128)(2,1)S(1)}, bf16[8,2,480]{2,1,0:T(2,128)(2,1)S(1)}, u32[]{:S(2)}, u32[]{:S(2)}) collective-permute-start(bf16[8,2,480]{2,1,0:T(2,128)(2,1)S(1)} %get-tuple-element.15), channel_id=1, source_target_pairs={{6,8},{8,6},{14,16},{16,14},{22,24},{24,22},{7,9},{9,7},{15,17},{1... | collective-permute-start | bytes 46088 | tf_op jit(solution)/shard_map/ppermute | solution.py:47
  9.6 2.6 %collective-permute-start.10 = (s32[8,16]{1,0:T(8,128)}, s32[8,16]{1,0:T(8,128)S(1)}, u32[]{:S(2)}, u32[]{:S(2)}) collective-permute-start(s32[8,16]{1,0:T(8,128)} %param.19), channel_id=1, source_target_pairs={{0,1},{1,0},{2,3},{3,2},{4,5},{5,4},{6,7},{7,6},{8,9},{9,8},{10,11... | collective-permute-start | bytes 1544 | tf_op jit(solution)/shard_map/ppermute | solution.py:53
  17.6 10.4 %collective-permute-start.8 = (bf16[32,1024]{1,0:T(8,128)(2,1)S(1)}, bf16[32,1024]{1,0:T(8,128)(2,1)S(1)}, u32[]{:S(2)}, u32[]{:S(2)}) collective-permute-start(bf16[32,1024]{1,0:T(8,128)(2,1)S(1)} %constant_dynamic-update-slice_fusion.5), channel_id=1, source_target_pairs={{0,24},{2,26},{4,28},{6,30},{8,16},{10,18},{12,20},{14,22},{16,8},... | collective-permute-start | bytes 196616 | tf_op jit(solution)/shard_map/ppermute | solution.py:17
  25.1 6.1 %collective-permute-start.7 = (bf16[32,1024]{1,0:T(8,128)(2,1)S(1)}, bf16[32,1024]{1,0:T(8,128)(2,1)S(1)}, u32[]{:S(2)}, u32[]{:S(2)}) collective-permute-start(bf16[32,1024]{1,0:T(8,128)(2,1)S(1)} %constant_dynamic-update-slice_fusion.5), channel_id=1, source_target_pairs={{0,16},{2,18},{4,20},{6,22},{8,24},{10,26},{12,28},{14,30},{16,0},... | collective-permute-start | bytes 196616 | tf_op jit(solution)/shard_map/ppermute | solution.py:17
  25.1 6.1 %collective-permute-start.6 = (bf16[32,1024]{1,0:T(8,128)(2,1)S(1)}, bf16[32,1024]{1,0:T(8,128)(2,1)S(1)}, u32[]{:S(2)}, u32[]{:S(2)}) collective-permute-start(bf16[32,1024]{1,0:T(8,128)(2,1)S(1)} %constant_dynamic-update-slice_fusion.5), channel_id=1, source_target_pairs={{0,8},{2,10},{4,12},{6,14},{8,0},{10,2},{12,4},{14,6},{16,24},{18,... | collective-permute-start | bytes 196616 | tf_op jit(solution)/shard_map/ppermute | solution.py:17
  26.0 36.0 %collective-permute-start.4 = (bf16[5,8,2,480]{3,2,1,0:T(2,128)(2,1)S(1)}, bf16[5,8,2,480]{3,2,1,0:T(2,128)(2,1)S(1)}, u32[]{:S(2)}, u32[]{:S(2)}) collective-permute-start(bf16[5,8,2,480]{3,2,1,0:T(2,128)(2,1)S(1)} %constant_dynamic-update-slice_fusion), channel_id=1, source_target_pairs={{0,1},{1,0},{2,3},{3,2},{4,5},{5,4},{6,7},{7,6},{8,9},{9,8},{10,11... | collective-permute-start | bytes 230408 | tf_op jit(solution)/shard_map/ppermute | solution.py:53
  61.4 11.8 %collective-permute-start.9 = (bf16[256,8,16,2]{0,2,3,1:T(8,128)(2,1)S(1)}, bf16[256,8,16,2]{0,2,3,1:T(8,128)(2,1)S(1)}, u32[]{:S(2)}, u32[]{:S(2)}) collective-permute-start(bf16[256,8,16,2]{0,2,3,1:T(8,128)(2,1)S(1)} %copy.101), channel_id=1, source_target_pairs={{0,1},{1,0},{2,3},{3,2},{4,5},{5,4},{6,7},{7,6},{8,9},{9,8},{10,11... | collective-permute-start | bytes 393224 | tf_op jit(solution)/shard_map/ppermute | solution.py:53
  72.6 47.4 %collective-permute-start.5 = (f32[8,2,480]{2,1,0:T(2,128)S(1)}, f32[8,2,480]{2,1,0:T(2,128)S(1)}, u32[]{:S(2)}, u32[]{:S(2)}) collective-permute-start(f32[8,2,480]{2,1,0:T(2,128)S(1)} %fusion.58), channel_id=1, source_target_pairs={{0,1},{1,0},{2,3},{3,2},{4,5},{5,4},{6,7},{7,6},{8,9},{9,8},{10,11... | collective-permute-start | bytes 92168 | tf_op jit(solution)/shard_map/ppermute | solution.py:65
  98.3 25.6 %copy-start.1 = (bf16[480,512]{1,0:T(8,128)(2,1)S(1)}, bf16[480,512]{1,0:T(8,128)(2,1)}, u32[]{:S(2)}) copy-start(bf16[480,512]{1,0:T(8,128)(2,1)} %param.16) | copy-start | bytes 1474564
  120.4 4.6 %collective-permute-start.11 = (bf16[16,480]{1,0:T(8,128)(2,1)S(1)}, bf16[16,480]{1,0:T(8,128)(2,1)S(1)}, u32[]{:S(2)}, u32[]{:S(2)}) collective-permute-start(bf16[16,480]{1,0:T(8,128)(2,1)S(1)} %reshape.278), channel_id=1, source_target_pairs={{0,2},{2,0},{4,6},{6,4},{8,10},{10,8},{12,14},{14,12},{16,18},{18,... | collective-permute-start | bytes 46088 | tf_op jit(solution)/shard_map/ppermute | solution.py:17
  120.4 4.5 %collective-permute-start.12 = (bf16[16,480]{1,0:T(8,128)(2,1)S(1)}, bf16[16,480]{1,0:T(8,128)(2,1)S(1)}, u32[]{:S(2)}, u32[]{:S(2)}) collective-permute-start(bf16[16,480]{1,0:T(8,128)(2,1)S(1)} %reshape.278), channel_id=1, source_target_pairs={{0,4},{2,6},{4,0},{6,2},{8,12},{10,14},{12,8},{14,10},{16,20},{18,... | collective-permute-start | bytes 46088 | tf_op jit(solution)/shard_map/ppermute | solution.py:17
  122.6 4.6 %collective-permute-start.13 = (bf16[16,480]{1,0:T(8,128)(2,1)S(1)}, bf16[16,480]{1,0:T(8,128)(2,1)S(1)}, u32[]{:S(2)}, u32[]{:S(2)}) collective-permute-start(bf16[16,480]{1,0:T(8,128)(2,1)S(1)} %reshape.278), channel_id=1, source_target_pairs={{0,6},{2,4},{4,2},{6,0},{8,14},{10,12},{12,10},{14,8},{16,22},{18,... | collective-permute-start | bytes 46088 | tf_op jit(solution)/shard_map/ppermute | solution.py:17
  124.0 8.5 %collective-permute-start.14 = (bf16[8,2,480]{2,1,0:T(2,128)(2,1)S(1)}, bf16[8,2,480]{2,1,0:T(2,128)(2,1)S(1)}, u32[]{:S(2)}, u32[]{:S(2)}) collective-permute-start(bf16[8,2,480]{2,1,0:T(2,128)(2,1)S(1)} %get-tuple-element.13), channel_id=1, source_target_pairs={{6,8},{8,6},{14,16},{16,14},{22,24},{24,22},{7,9},{9,7},{15,17},{1... | collective-permute-start | bytes 46088 | tf_op jit(solution)/shard_map/ppermute | solution.py:47
  127.8 4.8 %collective-permute-start.17 = (bf16[32,512]{1,0:T(8,128)(2,1)S(1)}, bf16[32,512]{1,0:T(8,128)(2,1)S(1)}, u32[]{:S(2)}, u32[]{:S(2)}) collective-permute-start(bf16[32,512]{1,0:T(8,128)(2,1)S(1)} %reshape.283), channel_id=1, source_target_pairs={{0,8},{2,10},{4,12},{6,14},{8,0},{10,2},{12,4},{14,6},{16,24},{18,... | collective-permute-start | bytes 98312 | tf_op jit(solution)/shard_map/ppermute | solution.py:17
  130.0 4.8 %collective-permute-start.18 = (bf16[32,512]{1,0:T(8,128)(2,1)S(1)}, bf16[32,512]{1,0:T(8,128)(2,1)S(1)}, u32[]{:S(2)}, u32[]{:S(2)}) collective-permute-start(bf16[32,512]{1,0:T(8,128)(2,1)S(1)} %reshape.283), channel_id=1, source_target_pairs={{0,16},{2,18},{4,20},{6,22},{8,24},{10,26},{12,28},{14,30},{16,0},... | collective-permute-start | bytes 98312 | tf_op jit(solution)/shard_map/ppermute | solution.py:17
  130.1 5.7 %collective-permute-start.19 = (bf16[32,512]{1,0:T(8,128)(2,1)S(1)}, bf16[32,512]{1,0:T(8,128)(2,1)S(1)}, u32[]{:S(2)}, u32[]{:S(2)}) collective-permute-start(bf16[32,512]{1,0:T(8,128)(2,1)S(1)} %reshape.283), channel_id=1, source_target_pairs={{0,24},{2,26},{4,28},{6,30},{8,16},{10,18},{12,20},{14,22},{16,8},... | collective-permute-start | bytes 98312 | tf_op jit(solution)/shard_map/ppermute | solution.py:17
  132.6 3.9 %collective-permute-start.15 = (bf16[5,8,2,480]{3,2,1,0:T(2,128)(2,1)S(1)}, bf16[5,8,2,480]{3,2,1,0:T(2,128)(2,1)S(1)}, u32[]{:S(2)}, u32[]{:S(2)}) collective-permute-start(bf16[5,8,2,480]{3,2,1,0:T(2,128)(2,1)S(1)} %constant_dynamic-update-slice_fusion.7), channel_id=1, source_target_pairs={{0,1},{1,0},{2,3},{3,2},{4,5},{5,4},{6,7},{7,6},{8,9},{9,8},{10,11... | collective-permute-start | bytes 230408 | tf_op jit(solution)/shard_map/ppermute | solution.py:53
  147.1 1.3 collective-permute-start.16
  148.7 1.2 collective-permute-start.20

commit v2 on v1

--- a/solution.py
+++ b/solution.py
@@ -1,6 +1,10 @@
+import functools
+
 import jax
 import jax.numpy as jnp
 from jax import lax
+from jax.experimental import pallas as pl
+from jax.experimental.pallas import tpu as pltpu
 from jax.sharding import PartitionSpec as P
 
 F32 = jnp.float32
@@ -67,7 +71,7 @@
     return lax.dynamic_slice_in_dim(total, far_pos % (partial.shape[1] // share) * share, share, 1)
 
 
-def shards(
+def plain_shards(
     vectors,
     near_blocks,
     neighbours,
@@ -98,8 +102,8 @@
     def own_share(block):
         return lax.dynamic_slice_in_dim(block, far_pos % splits * share, share, 1)
 
-    hi = agg_angle.astype(BF16)
-    low = (agg_angle - hi.astype(F32)).astype(BF16)
+    rounded = lax.reduce_precision(agg_angle, 8, 7)
+    hi, low = rounded.astype(BF16), (agg_angle - rounded).astype(BF16)
     factors = far_factors.astype(BF16).reshape(-1, far_factors.shape[-1]).T
     per_part = factors.size
     lists = over_far_lists(far_list)
@@ -214,6 +218,356 @@
     return gathered.reshape(-1, far_list.shape[1])
 
 
+VM = pl.BlockSpec(memory_space=pltpu.VMEM)
+SM = pl.BlockSpec(memory_space=pltpu.SMEM)
+
+
+def call(kernel, outs, specs, args, scratch=(), flops=0, moved=0):
+    return pl.pallas_call(
+        kernel,
+        out_shape=tuple(jax.ShapeDtypeStruct(shape, kind) for shape, kind in outs),
+        in_specs=list(specs),
+        out_specs=(VM,) * len(outs),
+        scratch_shapes=list(scratch),
+        cost_estimate=pl.CostEstimate(flops=flops, bytes_accessed=moved, transcendentals=0),
+    )(*args)
+
+
+def pack_kernel(place, box, vectors, angle, factors, out):
+    spheres, newton, width = vectors.shape
+    share = newton // 2
+    waves = angle.shape[1]
+    first = place[0] == 0
+    values = vectors[...].astype(F32)
+    for r in range(share):
+        low, high = values[:, r], values[:, share + r]
+        rows = pl.ds(r * spheres, spheres)
+        out[rows, pl.ds(0, width)] = jnp.where(first, low, high).astype(BF16)
+        out[rows, pl.ds(512, width)] = jnp.where(first, high, low).astype(BF16)
+    lane = lax.broadcasted_iota(jnp.int32, (spheres * share, 512 - width), 0) % spheres
+    ids = jnp.zeros((spheres * share, 512 - width), F32)
+    for n in range(spheres):
+        ids = jnp.where(lane == n, box[n].astype(F32), ids)
+    out[:, pl.ds(width, 512 - width)] = ids.astype(BF16)
+    hi = angle[...].astype(BF16)
+    low = (angle[...] - hi.astype(F32)).astype(BF16)
+    out[pl.ds(0, spheres), pl.ds(1024, waves)] = hi
+    out[pl.ds(spheres, spheres), pl.ds(1024, waves)] = low
+    out[:, pl.ds(1024 + waves, factors.shape[0])] = factors[...].T.astype(BF16)
+
+
+def sum_rows(member, waves):
+    dims = (((0,), (0,)), ((), ()))
+    hi = waves.astype(BF16)
+    low = (waves - hi.astype(F32)).astype(BF16)
+    return lax.dot_general(member, hi, dims, preferred_element_type=F32) + lax.dot_general(
+        member, low, dims, preferred_element_type=F32
+    )
+
+
+def turned(product, turn, waves):
+    cosine, sine = turn[:, :waves], turn[:, waves:]
+    re, im = product[:, :waves], product[:, waves:]
+    return jnp.concatenate([re * cosine - im * sine, re * sine + im * cosine], axis=1)
+
+
+def first_waves_kernel(boxes, place, p0, p1, p2, p3, agg, out, turn, member, table):
+    parts = (p0, p1, p2, p3)
+    width = agg.shape[0]
+    waves = agg.shape[1] // 2
+    rows = p0.shape[0]
+    half = rows // 2
+    held = table.shape[0] // 4
+    for j, part in enumerate(parts):
+        angle = part[pl.ds(0, half), pl.ds(1024, waves)].astype(F32)
+        angle += part[pl.ds(half, half), pl.ds(1024, waves)].astype(F32)
+        both = jnp.concatenate([jnp.cos(angle), jnp.sin(angle)], axis=1)
+        turn[pl.ds(j * rows, half), :] = both
+        turn[pl.ds(j * rows + half, half), :] = both
+        ids = part[:, pl.ds(width, 1)].astype(F32)
+        row = lax.broadcasted_iota(jnp.int32, (rows, 2 * boxes), 0) // half
+        col = lax.broadcasted_iota(jnp.int32, (rows, 2 * boxes), 1)
+        hit = (ids == (col % boxes).astype(F32)) & (row == col // boxes)
+        member[pl.ds(j * rows, rows), :] = jnp.where(hit, 1.0, 0.0).astype(BF16)
+        at = pl.multiple_of((place[1] ^ j) * held, held)
+        table[pl.ds(at, held), :] = part[:, pl.ds(1024 + waves, table.shape[1])].astype(F32)
+    flat = jnp.concatenate([p[:, pl.ds(0, width)] for p in parts], axis=0)
+    product = jnp.dot(flat, agg[...], preferred_element_type=F32)
+    sums = sum_rows(member[...], turned(product, turn[...], waves))
+    out[:, pl.ds(0, 2 * waves)] = sums.astype(BF16)
+    lines = out.shape[0]
+    span = table.shape[1]
+    for j in range(table.shape[0] // lines):
+        out[:, pl.ds(2 * waves + j * span, span)] = table[pl.ds(j * lines, lines), :].astype(BF16)
+
+
+def next_waves_kernel(p0, p1, p2, p3, agg, turn, member, out):
+    waves = agg.shape[1] // 2
+    flat = jnp.concatenate([p0[...], p1[...], p2[...], p3[...]], axis=0)
+    product = jnp.dot(flat, agg[...], preferred_element_type=F32)
+    out[...] = sum_rows(member[...], turned(product, turn[...], waves)).astype(BF16)
+
+
+def table_kernel(waves, place, z0, z1, z2, z3, out, held):
+    lines = z0.shape[0]
+    span = held.shape[1]
+    pieces = (z0.shape[1] - 2 * waves) // span
+    for j, part in enumerate((z0, z1, z2, z3)):
+        for i in range(pieces):
+            at = pl.multiple_of(((place[2] ^ j) * pieces + i) * lines, lines)
+            held[pl.ds(at, lines), :] = part[:, pl.ds(2 * waves + i * span, span)].astype(F32)
+    out[...] = held[...].T.astype(BF16)
+
+
+def near_kernel(starts, emit, place, neighbours, live, *refs):
+    mine, theirs = refs[:5], refs[5 : 5 + (5 if starts[1] is not None else 1)]
+    refs = refs[5 + len(theirs) :]
+    blocks = refs[0]
+    out_mine, out_theirs = refs[1], refs[2]
+    image = refs[3] if emit else None
+    held = refs[-1]
+    n = pl.program_id(0)
+    spheres = out_mine.shape[0] // 2
+    slots = blocks.shape[1]
+    coeffs = blocks.shape[3]
+
+    @pl.when(n == 0)
+    def _():
+        for j in range(5):
+            for side in range(2):
+                for r in range(2):
+                    rows = pl.ds(r * spheres, spheres)
+                    if side == 0:
+                        value = mine[j][rows, pl.ds(0, 2 * coeffs)]
+                    elif starts[1] is not None:
+                        value = theirs[j][rows, pl.ds(starts[1], 2 * coeffs)]
+                    else:
+                        value = theirs[0][pl.ds((2 * j + r) * spheres, spheres), :]
+                    value = value.astype(F32)
+                    at = pl.ds(j * spheres, spheres)
+                    held[at, side * 2 + r, :] = value[:, :coeffs]
+                    held[at, 4 + side * 2 + r, :] = value[:, coeffs:]
+        if emit:
+            first = place[0] == 0
+            for r in range(2):
+                own = mine[0][pl.ds(r * spheres, spheres), :].astype(F32)
+                other = theirs[0][pl.ds(r * spheres, spheres), :].astype(F32)
+                image[:, r, :] = jnp.where(first, own, other).astype(BF16)
+                image[:, 2 + r, :] = jnp.where(first, other, own).astype(BF16)
+
+    real = jnp.zeros((8, coeffs), F32)
+    imag = jnp.zeros((8, coeffs), F32)
+    for k in range(slots):
+        source = neighbours[n, k]
+        chip = source // spheres
+        near = jnp.where(chip // 4 == place[3] // 4, chip ^ place[3], 4)
+        value = held[near * spheres + source % spheres]
+        alive = place[0] * slots + k < live[n]
+        value = jnp.where(alive, value, 0.0).astype(BF16)
+        real += jnp.dot(value, blocks[0, k, 0], preferred_element_type=F32)
+        imag += jnp.dot(value, blocks[0, k, 1], preferred_element_type=F32)
+    near_re = real[:4] - imag[4:]
+    near_im = imag[:4] + real[4:]
+    for r in range(2):
+        row = pl.ds(r * spheres + n, 1)
+        out_mine[row, pl.ds(0, coeffs)] = near_re[r : r + 1]
+        out_mine[row, pl.ds(coeffs, coeffs)] = near_im[r : r + 1]
+        out_theirs[row, pl.ds(0, coeffs)] = near_re[2 + r : 3 + r]
+        out_theirs[row, pl.ds(coeffs, coeffs)] = near_im[2 + r : 3 + r]
+
+
+def near_call(starts, emit, place, neighbours, live, mine, theirs, blocks):
+    spheres, slots, _, coeffs, _ = blocks.shape
+    rows = 2 * spheres
+    outs = [jax.ShapeDtypeStruct((rows, 2 * coeffs), F32)] * 2
+    if emit:
+        outs.append(jax.ShapeDtypeStruct((spheres, 4, 2 * coeffs), BF16))
+    full = [VM] * (len(mine) + len(theirs))
+    return pl.pallas_call(
+        functools.partial(near_kernel, starts, emit),
+        grid=(spheres,),
+        out_shape=tuple(outs),
+        in_specs=[SM] * 3
+        + full
+        + [pl.BlockSpec((1, slots, 2, coeffs, coeffs), lambda n: (n, 0, 0, 0, 0))],
+        out_specs=(VM,) * len(outs),
+        scratch_shapes=[pltpu.VMEM((5 * spheres, 8, coeffs), F32)],
+        cost_estimate=pl.CostEstimate(
+            flops=2 * 8 * 2 * coeffs * coeffs * spheres * slots,
+            bytes_accessed=blocks.size * 2,
+            transcendentals=0,
+        ),
+    )(place, neighbours, live, *mine, *theirs, blocks)
+
+
+def finish_kernel(
+    place, box, list_mine, list_theirs, z0, z1, z2, z3, table_mine, table_theirs, turn, dis,
+    near_mine, near_got, tmatrix, current, out, source, factor, field, local
+):
+    own_boxes, listed = list_mine.shape
+    boxes = 2 * own_boxes
+    waves = source.shape[2]
+    spheres = tmatrix.shape[0]
+    coeffs = tmatrix.shape[2]
+    first = place[0] == 0
+    total = jnp.zeros((2 * boxes, 2 * waves), F32)
+    for part in (z0, z1, z2, z3):
+        total += part[:, pl.ds(0, 2 * waves)].astype(F32)
+    for r in range(2):
+        re = total[r * boxes : (r + 1) * boxes, :waves]
+        im = total[r * boxes : (r + 1) * boxes, waves:]
+        source[:, r, :] = re
+        source[:, 2 + r, :] = im
+        source[:, 4 + r, :] = -im
+        source[:, 6 + r, :] = re
+    size = table_mine.shape[0]
+    mine, theirs = table_mine[...].astype(F32), table_theirs[...].astype(F32)
+    factor[pl.ds(0, size), :] = jnp.where(first, mine, theirs)
+    factor[pl.ds(size, size), :] = jnp.where(first, theirs, mine)
+    upper = lax.broadcasted_iota(jnp.int32, (8, waves), 0) < 4
+
+    def one_box(b, carry):
+        row = b % own_boxes
+        is_mine = b // own_boxes == place[0]
+        sums = [jnp.zeros((8, waves), F32) for _ in range(2)]
+        for f in range(listed):
+            which = jnp.where(is_mine, list_mine[row, f], list_theirs[row, f])
+            at = (b * listed + f) * 2
+            weight = jnp.where(upper, factor[pl.ds(at, 1), :], factor[pl.ds(at + 1, 1), :])
+            sums[f % 2] = sums[f % 2] + weight * source[which]
+        both = sums[0] + sums[1]
+        field[b] = both[:4] + both[4:]
+        return carry
+
+    lax.fori_loop(box[0], box[spheres - 1] + 1, one_box, 0)
+    for n in range(spheres):
+        local[:, n, :] = field[box[n]]
+    re = local[pl.ds(0, 2)].reshape(2 * spheres, waves)
+    im = local[pl.ds(2, 2)].reshape(2 * spheres, waves)
+    cosine = turn[pl.ds(0, 2 * spheres), pl.ds(0, waves)]
+    sine = turn[pl.ds(0, 2 * spheres), pl.ds(waves, waves)]
+    shifted = jnp.concatenate([re * cosine + im * sine, im * cosine - re * sine], axis=1)
+    total = jnp.dot(shifted.astype(BF16), dis[...], preferred_element_type=F32)
+    total += near_mine[...] + near_got[...]
+    t_re = jnp.concatenate([tmatrix[:, 0], tmatrix[:, 0]], axis=0)
+    t_im = jnp.concatenate([tmatrix[:, 1], tmatrix[:, 1]], axis=0)
+    f_re, f_im = total[:, :coeffs], total[:, coeffs:]
+    start = current[:, pl.ds(0, 2 * coeffs)].astype(F32)
+    out[:, pl.ds(0, coeffs)] = (start[:, :coeffs] - (t_re * f_re - t_im * f_im)).astype(BF16)
+    out[:, pl.ds(coeffs, coeffs)] = (start[:, coeffs:] - (t_re * f_im + t_im * f_re)).astype(BF16)
+
+
+def join_kernel(place, mine, theirs, out):
+    spheres = out.shape[0]
+    first = place[0] == 0
+    for r in range(2):
+        own = mine[pl.ds(r * spheres, spheres), :].astype(F32)
+        other = theirs[pl.ds(r * spheres, spheres), :].astype(F32)
+        out[:, r, :] = jnp.where(first, own, other).astype(BF16)
+        out[:, 2 + r, :] = jnp.where(first, other, own).astype(BF16)
+
+
+def swap_far(block):
+    return lax.ppermute(block, "far", [(0, 1), (1, 0)])
+
+
+def kernel_shards(
+    vectors, near_blocks, neighbours, live_counts, tmatrix, agg_matrix, sphere_box, agg_angle,
+    far_list, far_factors, dis_matrix
+):
+    spheres, newton, width = vectors.shape
+    coeffs = width // 2
+    own_boxes, listed = far_list.shape
+    boxes = 2 * own_boxes
+    waves = agg_matrix.shape[1] // 2
+    rows = spheres * newton // 2
+    near_pos = lax.axis_index("near")
+    place = jnp.stack([lax.axis_index("far"), near_pos % 4, near_pos // 4, near_pos])
+    place = place.astype(jnp.int32)
+    entries = own_boxes * listed * 2
+    message = call(
+        pack_kernel,
+        [((rows, 1024 + waves + entries), BF16)],
+        [SM, SM, VM, VM, VM],
+        (place, sphere_box, vectors, agg_angle, far_factors.reshape(entries, -1)),
+    )[0]
+    list_theirs = swap_far(far_list)
+    current, edge = message, edge_rows(message[:, :1024])
+    table = None
+    for step in range(2):
+        if step == 0:
+            parts = xor_gather(message, (1, 2, 3))
+            block, turn, member, _ = call(
+                functools.partial(first_waves_kernel, boxes),
+                [
+                    ((2 * boxes, 2 * waves + waves // 4 * entries // (2 * boxes)), BF16),
+                    ((4 * rows, 2 * waves), F32),
+                    ((4 * rows, 2 * boxes), BF16),
+                    ((waves // 4, entries), F32),
+                ],
+                [SM] + [VM] * 5,
+                (place, *parts, agg_matrix),
+            )
+        else:
+            edge = edge_rows(current)
+            parts = xor_gather(current, (1, 2, 3))
+            block = call(
+                next_waves_kernel,
+                [((2 * boxes, 2 * waves), BF16)],
+                [VM] * 7,
+                (*parts, agg_matrix, turn, member),
+            )[0]
+        pieces = xor_gather(block, (4, 8, 12))
+        mine = (*parts, edge)
+        if step == 0:
+            near_mine, near_theirs = near_call(
+                (0, 512), False, place, neighbours, live_counts, mine, mine, near_blocks
+            )
+        else:
+            theirs = swap_far(jnp.concatenate(mine, axis=0))
+            near_mine, near_theirs, first_image = near_call(
+                (0, None), True, place, neighbours, live_counts, mine, (theirs,), near_blocks
+            )
+        near_got = swap_far(near_theirs)
+        if step == 0:
+            table = call(
+                functools.partial(table_kernel, waves),
+                [((entries, waves), BF16)],
+                [SM] + [VM] * 4,
+                (place, *pieces),
+                [pltpu.VMEM((waves, entries), F32)],
+            )[0]
+            table = (table, swap_far(table))
+        current = call(
+            finish_kernel,
+            [((rows, width), BF16)],
+            [SM] * 4 + [VM] * 12,
+            (
+                place, sphere_box, far_list, list_theirs, *pieces, *table, turn, dis_matrix,
+                near_mine, near_got, tmatrix, current
+            ),
+            [
+                pltpu.VMEM((boxes, 8, waves), F32),
+                pltpu.VMEM((2 * entries, waves), F32),
+                pltpu.VMEM((boxes, 4, waves), F32),
+                pltpu.VMEM((4, spheres, waves), F32),
+            ],
+        )[0]
+    second_image = call(
+        join_kernel,
+        [((spheres, newton, width), BF16)],
+        [SM, VM, VM],
+        (place, current, swap_far(current)),
+    )[0]
+    return first_image, second_image
+
+
+def shards(*args):
+    if lax.axis_size("near") == 16 and lax.axis_size("far") == 2:
+        return kernel_shards(*args)
+    return plain_shards(*args)
+
+
 def solution(mesh):
     return jax.shard_map(
         shards,

time: 152 us -> 85.2 us (0.56)
  local copies, waits for them, and re-layouts: 73.6 us -> 8.06 us
  Pallas kernels: 0 us -> 34.4 us
  matrix products: 20.7 us -> 0 us
  other arithmetic: 19.3 us -> 0.66 us
  starting transfers between devices: 23.5 us -> 26.5 us
  waiting for transfers between devices: 12.1 us -> 14.2 us
    pallas_call x0 -> x9, Pallas kernels: none -> 34.4 us  [the longest x2 20.3 us: near_call(): pl.pallas_call(functools.partial(near_kernel, starts, emit), grid=(sphere...]
    select_n x4 -> x0, local copies, waits for them, and re-layouts: 29.6 us -> none  [in_order(): return jnp.take(stacked, jnp.arange(len(parts)) ^ digit, axis=0)]
    another operation x19 -> x0, local copies, waits for them, and re-layouts: 21.3 us -> none  [the longest x2 20.6 us: over_far(): jnp.stack([jnp.where(first, block, other), jnp.where(first, other, block)])]
    dot_general x12 -> x0, matrix products: 20.7 us -> none  [the longest x2 8.84 us: shards(): jnp.einsum('nkrc,nkcd->nrd', both, near_blocks[:, :, 1], preferred_elemen...]
    ppermute x1 -> x0, local copies, waits for them, and re-layouts: 13.8 us -> none  [over_far(): other = lax.ppermute(block, 'far', [(0, 1), (1, 0)])]
    another operation x11 -> x1, other arithmetic: 12.4 us -> 0.66 us  [kernel_shards(): jnp.stack([lax.axis_index('far'), near_pos % 4, near_pos // 4, near_pos])]
    unnamed x14 -> x49, local copies, waits for them, and re-layouts: 2.24 us -> 7.3 us
    gather x6 -> x0, local copies, waits for them, and re-layouts: 3.8 us -> none  [the longest x2 1.59 us: shards(): full[local_index]]
  transfers between devices with their start and end apart: 21 -> 20, of which waited for: 8 -> 9; matrix products, arithmetic and copies ran while one was open for 65% -> 3% of each run, Pallas kernels for 0% -> 26%
where the time goes in v2:
time: 85.2 us; the launch traced here: 84.6 us
  Pallas kernels  34.4 us (40%)
  starting transfers between devices  26.5 us (31%)
  waiting for transfers between devices  14.2 us (17%)
  local copies, waits for them, and re-layouts  8.06 us (9%)
  between operations  0.88 us (1%)
    ppermute x12, starting transfers between devices, swap_near(): return lax.ppermute(block, 'near', [(i, i ^ mask) for i in range(count)])  24.3 us
    pallas_call x2, Pallas kernels, near_call(): pl.pallas_call(functools.partial(near_kernel, starts, emit), grid=(sphere...  20.3 us
    pallas_call x7, Pallas kernels, call(): pl.pallas_call(kernel, out_shape=tuple((jax.ShapeDtypeStruct(shape, kind)...  14.1 us
    ppermute x12, waiting for transfers between devices, swap_near(): return lax.ppermute(block, 'near', [(i, i ^ mask) for i in range(count)])  11.5 us
    unnamed x49, local copies, waits for them, and re-layouts  7.3 us
    ppermute x6, waiting for transfers between devices, swap_far(): return lax.ppermute(block, 'far', [(0, 1), (1, 0)])  2.66 us
  transfers between devices with their start and end apart: 20, of which 9 were waited for; matrix products, arithmetic and copies ran while one was open for 3% of the time, Pallas kernels for 26%

profile of v2, /device:TPU:0, one launch (start us, length us, event | category | flops | bytes accessed | tf_op | source)
XLA Modules:
  0.0 84.6 jit_solution(265007977533270092)
XLA Ops:
  0.7 0.7 pad_add_fusion.place
  1.3 1.7 %shard_map.122.p0.refs_0_.refs_5_.current = bf16[16,1536]{1,0:T(8,128)(2,1)} custom-call(s32[4]{0:T(128)} %pad_add_fusion.place, s32[8]{0:T(128)} %box.5, bf16[8,4,480]{2,1,0:T(4,128)(2,1)} %vectors.1, f32[8,256]{1,0:T(8,128)} %angle.1, f32[256,16]{1,0:T(8,128)} %bitcast.5), custom_call_target="tpu_custom_call" | custom-call | tf_op jit(solution)/shard_map/pallas_call | solution.py:226
  3.0 3.9 %collective-permute-start.3 = (bf16[16,1536]{1,0:T(8,128)(2,1)}, bf16[16,1536]{1,0:T(8,128)(2,1)S(1)}, u32[]{:S(2)}, u32[]{:S(2)}) collective-permute-start(bf16[16,1536]{1,0:T(8,128)(2,1)} %shard_map.122.p0.refs_0_.refs_5_.current), channel_id=1, source_target_pairs={{0,6},{2,4},{4,2},{6,0},{8,14},{10,12},{12,10},{14,8},{16,22},{18,... | collective-permute-start | bytes 147464 | tf_op jit(solution)/shard_map/ppermute | solution.py:21
  7.5 1.7 %collective-permute-done.3.p3.refs_3_.refs_8_ = bf16[16,1536]{1,0:T(8,128)(2,1)S(1)} collective-permute-done((bf16[16,1536]{1,0:T(8,128)(2,1)}, bf16[16,1536]{1,0:T(8,128)(2,1)S(1)}, u32[]{:S(2)}, u32[]{:S(2)}) %collective-permute-start.3) | collective-permute-done | bytes 49184 | tf_op jit(solution)/shard_map/ppermute | solution.py:21
  9.2 2.0 %collective-permute-done.2.p2.refs_2_.refs_7_ = bf16[16,1536]{1,0:T(8,128)(2,1)S(1)} collective-permute-done((bf16[16,1536]{1,0:T(8,128)(2,1)}, bf16[16,1536]{1,0:T(8,128)(2,1)S(1)}, u32[]{:S(2)}, u32[]{:S(2)}) %collective-permute-start.2) | collective-permute-done | bytes 49184 | tf_op jit(solution)/shard_map/ppermute | solution.py:21
  12.5 2.2 %shard_map.123 = (bf16[32,1024]{1,0:T(8,128)(2,1)}, f32[64,512]{1,0:T(8,128)}, bf16[64,32]{1,0:T(8,128)(2,1)}, f32[64,256]{1,0:T(8,128)}) custom-call(s32[4]{0:T(128)} %pad_add_fusion.place, bf16[16,1536]{1,0:T(8,128)(2,1)} %shard_map.122.p0.refs_0_.refs_5_.current, bf16[16,1536]{1,0:T(8,128)(2,1)} %copy-done.4, bf16[16,1536]{1,0:T(8,128)(2,1)} %copy-done.3, ...), custom_call_target="tpu_custom_call" | custom-call | tf_op jit(solution)/shard_map/pallas_call | solution.py:226
  14.6 3.6 %collective-permute-start.6 = (bf16[32,1024]{1,0:T(8,128)(2,1)}, bf16[32,1024]{1,0:T(8,128)(2,1)S(1)}, u32[]{:S(2)}, u32[]{:S(2)}) collective-permute-start(bf16[32,1024]{1,0:T(8,128)(2,1)} %get-tuple-element.10.z0), channel_id=1, source_target_pairs={{0,24},{2,26},{4,28},{6,30},{8,16},{10,18},{12,20},{14,22},{16,8},... | collective-permute-start | bytes 196616 | tf_op jit(solution)/shard_map/ppermute | solution.py:21
  18.2 0.8 collective-permute-start.4
  19.0 1.9 %collective-permute-done.6.z3 = bf16[32,1024]{1,0:T(8,128)(2,1)S(1)} collective-permute-done((bf16[32,1024]{1,0:T(8,128)(2,1)}, bf16[32,1024]{1,0:T(8,128)(2,1)S(1)}, u32[]{:S(2)}, u32[]{:S(2)}) %collective-permute-start.6) | collective-permute-done | bytes 65568 | tf_op jit(solution)/shard_map/ppermute | solution.py:21
  21.0 2.8 %collective-permute-done.5.z2 = bf16[32,1024]{1,0:T(8,128)(2,1)S(1)} collective-permute-done((bf16[32,1024]{1,0:T(8,128)(2,1)}, bf16[32,1024]{1,0:T(8,128)(2,1)S(1)}, u32[]{:S(2)}, u32[]{:S(2)}) %collective-permute-start.5) | collective-permute-done | bytes 65568 | tf_op jit(solution)/shard_map/ppermute | solution.py:21
  24.4 0.6 copy-done.7
  25.0 1.7 %shard_map.124.table_mine = bf16[256,256]{1,0:T(8,128)(2,1)} custom-call(s32[4]{0:T(128)} %pad_add_fusion.place, bf16[32,1024]{1,0:T(8,128)(2,1)} %get-tuple-element.10.z0, bf16[32,1024]{1,0:T(8,128)(2,1)} %copy-done.7, bf16[32,1024]{1,0:T(8,128)(2,1)} %copy-done.6, bf16[32,1024]{1,0:T(8,128)(2,1)} %copy-done.5), custom_call_target="tpu_custom_call" | custom-call | tf_op jit(solution)/shard_map/pallas_call | solution.py:226
  26.7 0.8 slice.4
  27.5 0.7 collective-permute-start.8
  28.8 10.4 %shard_map.125 = (f32[16,480]{1,0:T(8,128)}, f32[16,480]{1,0:T(8,128)}) custom-call(s32[4]{0:T(128)} %pad_add_fusion.place, s32[8,8]{1,0:T(8,128)} %neighbours.3, s32[8]{0:T(128)} %live.3, bf16[16,1536]{1,0:T(8,128)(2,1)} %shard_map.122.p0.refs_0_.refs_5_.current, bf16[16,1536]{1,0:T(8,128)(2,1)} %copy-done.4, bf16[16,1536]{1,0:T(8,128)(2,1)} %copy-done.3, ...), custom_call_target="tpu_custom_call" | custom-call | flops 117964800 | bytes 14745600 | tf_op jit(solution)/shard_map/pallas_call | solution.py:386
  39.7 1.0 %copy.13.dis = bf16[512,480]{1,0:T(8,128)(2,1)} copy(bf16[512,480]{0,1:T(8,128)(2,1)S(1)} %copy-done.1) | data formatting | bytes 983040 | tf_op args[10]
  41.5 2.5 %shard_map.126.refs_0_.p0.current = bf16[16,480]{1,0:T(8,128)(2,1)} custom-call(s32[4]{0:T(128)} %pad_add_fusion.place, s32[8]{0:T(128)} %box.5, s32[8,16]{1,0:T(8,128)} %list_mine.3, s32[8,16]{1,0:T(8,128)} %copy-done.20, bf16[32,1024]{1,0:T(8,128)(2,1)} %get-tuple-element.10.z0, bf16[32,1024]{1,0:T(8,128)(2,1)} %copy-done.7, bf16[32,1024]{1,0:T(8,128)(2,1)} %copy-done.6, ...), custom_call_target="tpu_custom_call" | custom-call | tf_op jit(solution)/shard_map/pallas_call | solution.py:226
  44.0 0.7 collective-permute-start.13
  44.6 10.4 %collective-permute-start.12 = (bf16[16,480]{1,0:T(8,128)(2,1)}, bf16[16,480]{1,0:T(8,128)(2,1)S(1)}, u32[]{:S(2)}, u32[]{:S(2)}) collective-permute-start(bf16[16,480]{1,0:T(8,128)(2,1)} %shard_map.126.refs_0_.p0.current), channel_id=1, source_target_pairs={{0,6},{2,4},{4,2},{6,0},{8,14},{10,12},{12,10},{14,8},{16,22},{18,... | collective-permute-start | bytes 46088 | tf_op jit(solution)/shard_map/ppermute | solution.py:21
  55.1 0.6 collective-permute-start.10
  55.7 0.8 constant_dynamic-update-slice_fusion.4
  56.5 2.6 %collective-permute-done.10.refs_1_.p1 = bf16[16,480]{1,0:T(8,128)(2,1)S(1)} collective-permute-done((bf16[16,480]{1,0:T(8,128)(2,1)}, bf16[16,480]{1,0:T(8,128)(2,1)S(1)}, u32[]{:S(2)}, u32[]{:S(2)}) %collective-permute-start.10) | collective-permute-done | bytes 15392 | tf_op jit(solution)/shard_map/ppermute | solution.py:21
  59.7 2.1 %shard_map.128.z0 = bf16[32,512]{1,0:T(8,128)(2,1)} custom-call(bf16[16,480]{1,0:T(8,128)(2,1)} %shard_map.126.refs_0_.p0.current, bf16[16,480]{1,0:T(8,128)(2,1)} %copy-done.10, bf16[16,480]{1,0:T(8,128)(2,1)} %copy-done.9, bf16[16,480]{1,0:T(8,128)(2,1)} %copy-done.8, bf16[480,512]{1,0:T(8,128)(2,1)} %agg.3, f32[64,512]{1,0:T(8,128)} %get-tuple-element.11.turn, ...), custom_call_target="tpu_custom_call" | custom-call | tf_op jit(solution)/shard_map/pallas_call | solution.py:226
  61.8 2.6 %collective-permute-start.17 = (bf16[32,512]{1,0:T(8,128)(2,1)}, bf16[32,512]{1,0:T(8,128)(2,1)S(1)}, u32[]{:S(2)}, u32[]{:S(2)}) collective-permute-start(bf16[32,512]{1,0:T(8,128)(2,1)} %shard_map.128.z0), channel_id=1, source_target_pairs={{0,24},{2,26},{4,28},{6,30},{8,16},{10,18},{12,20},{14,22},{16,8},... | collective-permute-start | bytes 98312 | tf_op jit(solution)/shard_map/ppermute | solution.py:21
  64.4 0.9 %collective-permute-start.16 = (bf16[32,512]{1,0:T(8,128)(2,1)}, bf16[32,512]{1,0:T(8,128)(2,1)S(1)}, u32[]{:S(2)}, u32[]{:S(2)}) collective-permute-start(bf16[32,512]{1,0:T(8,128)(2,1)} %shard_map.128.z0), channel_id=1, source_target_pairs={{0,16},{2,18},{4,20},{6,22},{8,24},{10,26},{12,28},{14,30},{16,0},... | collective-permute-start | bytes 98312 | tf_op jit(solution)/shard_map/ppermute | solution.py:21
  65.3 0.9 %collective-permute-start.15 = (bf16[32,512]{1,0:T(8,128)(2,1)}, bf16[32,512]{1,0:T(8,128)(2,1)S(1)}, u32[]{:S(2)}, u32[]{:S(2)}) collective-permute-start(bf16[32,512]{1,0:T(8,128)(2,1)} %shard_map.128.z0), channel_id=1, source_target_pairs={{0,8},{2,10},{4,12},{6,14},{8,0},{10,2},{12,4},{14,6},{16,24},{18,... | collective-permute-start | bytes 98312 | tf_op jit(solution)/shard_map/ppermute | solution.py:21
  66.2 0.6 copy-done.12
  66.8 9.9 %shard_map.127 = (f32[16,480]{1,0:T(8,128)}, f32[16,480]{1,0:T(8,128)}, bf16[8,4,480]{2,1,0:T(4,128)(2,1)}) custom-call(s32[4]{0:T(128)} %pad_add_fusion.place, s32[8,8]{1,0:T(8,128)} %neighbours.3, s32[8]{0:T(128)} %live.3, bf16[16,480]{1,0:T(8,128)(2,1)} %shard_map.126.refs_0_.p0.current, bf16[16,480]{1,0:T(8,128)(2,1)} %copy-done.10, ...), custom_call_target="tpu_custom_call" | custom-call | flops 117964800 | bytes 14745600 | tf_op jit(solution)/shard_map/pallas_call | solution.py:386
  76.8 1.3 %collective-permute-done.18.near_got = f32[16,480]{1,0:T(8,128)S(1)} collective-permute-done((f32[16,480]{1,0:T(8,128)}, f32[16,480]{1,0:T(8,128)S(1)}, u32[]{:S(2)}, u32[]{:S(2)}) %collective-permute-start.18) | collective-permute-done | bytes 30752 | tf_op jit(solution)/shard_map/ppermute | solution.py:471
  78.8 2.5 %shard_map.129.mine = bf16[16,480]{1,0:T(8,128)(2,1)} custom-call(s32[4]{0:T(128)} %pad_add_fusion.place, s32[8]{0:T(128)} %box.5, s32[8,16]{1,0:T(8,128)} %list_mine.3, s32[8,16]{1,0:T(8,128)} %copy-done.20, bf16[32,512]{1,0:T(8,128)(2,1)} %shard_map.128.z0, bf16[32,512]{1,0:T(8,128)(2,1)} %copy-done.16, bf16[32,512]{1,0:T(8,128)(2,1)} %copy-done.15, ...), custom_call_target="tpu_custom_call" | custom-call | tf_op jit(solution)/shard_map/pallas_call | solution.py:226
  81.4 1.2 %collective-permute-done.19.theirs = bf16[16,480]{1,0:T(8,128)(2,1)S(1)} collective-permute-done((bf16[16,480]{1,0:T(8,128)(2,1)}, bf16[16,480]{1,0:T(8,128)(2,1)S(1)}, u32[]{:S(2)}, u32[]{:S(2)}) %collective-permute-start.19) | collective-permute-done | bytes 15392 | tf_op jit(solution)/shard_map/ppermute | solution.py:471
  83.2 1.4 %shard_map.130 = bf16[8,4,480]{2,1,0:T(4,128)(2,1)} custom-call(s32[4]{0:T(128)} %pad_add_fusion.place, bf16[16,480]{1,0:T(8,128)(2,1)} %shard_map.129.mine, bf16[16,480]{1,0:T(8,128)(2,1)} %copy-done.21), custom_call_target="tpu_custom_call" | custom-call | tf_op jit(solution)/shard_map/pallas_call | solution.py:226
  (69 shorter events, 6.3 us)
Async XLA Ops:
  0.6 39.0 %copy-start.19 = (s32[8,16]{1,0:T(8,128)S(1)}, s32[8,16]{1,0:T(8,128)}, u32[]{:S(2)}) copy-start(s32[8,16]{1,0:T(8,128)} %list_mine.3) | copy-start | bytes 1540
  0.6 39.1 %copy-start.1 = (bf16[512,480]{0,1:T(8,128)(2,1)S(1)}, bf16[512,480]{0,1:T(8,128)(2,1)}, u32[]{:S(2)}) copy-start(bf16[512,480]{0,1:T(8,128)(2,1)} %param.21) | copy-start | bytes 1474564
  3.0 6.2 %collective-permute-start.3 = (bf16[16,1536]{1,0:T(8,128)(2,1)}, bf16[16,1536]{1,0:T(8,128)(2,1)S(1)}, u32[]{:S(2)}, u32[]{:S(2)}) collective-permute-start(bf16[16,1536]{1,0:T(8,128)(2,1)} %shard_map.122.p0.refs_0_.refs_5_.current), channel_id=1, source_target_pairs={{0,6},{2,4},{4,2},{6,0},{8,14},{10,12},{12,10},{14,8},{16,22},{18,... | collective-permute-start | bytes 147464 | tf_op jit(solution)/shard_map/ppermute | solution.py:21
  6.9 4.3 %collective-permute-start.2 = (bf16[16,1536]{1,0:T(8,128)(2,1)}, bf16[16,1536]{1,0:T(8,128)(2,1)S(1)}, u32[]{:S(2)}, u32[]{:S(2)}) collective-permute-start(bf16[16,1536]{1,0:T(8,128)(2,1)} %shard_map.122.p0.refs_0_.refs_5_.current), channel_id=1, source_target_pairs={{0,4},{2,6},{4,0},{6,2},{8,12},{10,14},{12,8},{14,10},{16,20},{18,... | collective-permute-start | bytes 147464 | tf_op jit(solution)/shard_map/ppermute | solution.py:21
  7.4 4.3 %collective-permute-start.1 = (bf16[16,1536]{1,0:T(8,128)(2,1)}, bf16[16,1536]{1,0:T(8,128)(2,1)S(1)}, u32[]{:S(2)}, u32[]{:S(2)}) collective-permute-start(bf16[16,1536]{1,0:T(8,128)(2,1)} %shard_map.122.p0.refs_0_.refs_5_.current), channel_id=1, source_target_pairs={{0,2},{2,0},{4,6},{6,4},{8,10},{10,8},{12,14},{14,12},{16,18},{18,... | collective-permute-start | bytes 147464 | tf_op jit(solution)/shard_map/ppermute | solution.py:21
  9.2 2.5 %copy-start.2 = (bf16[16,1536]{1,0:T(8,128)(2,1)}, bf16[16,1536]{1,0:T(8,128)(2,1)S(1)}, u32[]{:S(2)}) copy-start(bf16[16,1536]{1,0:T(8,128)(2,1)S(1)} %collective-permute-done.3.p3.refs_3_.refs_8_) | copy-start | bytes 147460
  14.6 6.3 %collective-permute-start.6 = (bf16[32,1024]{1,0:T(8,128)(2,1)}, bf16[32,1024]{1,0:T(8,128)(2,1)S(1)}, u32[]{:S(2)}, u32[]{:S(2)}) collective-permute-start(bf16[32,1024]{1,0:T(8,128)(2,1)} %get-tuple-element.10.z0), channel_id=1, source_target_pairs={{0,24},{2,26},{4,28},{6,30},{8,16},{10,18},{12,20},{14,22},{16,8},... | collective-permute-start | bytes 196616 | tf_op jit(solution)/shard_map/ppermute | solution.py:21
  18.2 5.5 %collective-permute-start.5 = (bf16[32,1024]{1,0:T(8,128)(2,1)}, bf16[32,1024]{1,0:T(8,128)(2,1)S(1)}, u32[]{:S(2)}, u32[]{:S(2)}) collective-permute-start(bf16[32,1024]{1,0:T(8,128)(2,1)} %get-tuple-element.10.z0), channel_id=1, source_target_pairs={{0,16},{2,18},{4,20},{6,22},{8,24},{10,26},{12,28},{14,30},{16,0},... | collective-permute-start | bytes 196616 | tf_op jit(solution)/shard_map/ppermute | solution.py:21
  18.2 5.5 %collective-permute-start.4 = (bf16[32,1024]{1,0:T(8,128)(2,1)}, bf16[32,1024]{1,0:T(8,128)(2,1)S(1)}, u32[]{:S(2)}, u32[]{:S(2)}) collective-permute-start(bf16[32,1024]{1,0:T(8,128)(2,1)} %get-tuple-element.10.z0), channel_id=1, source_target_pairs={{0,8},{2,10},{4,12},{6,14},{8,0},{10,2},{12,4},{14,6},{16,24},{18,... | collective-permute-start | bytes 196616 | tf_op jit(solution)/shard_map/ppermute | solution.py:21
  21.0 2.8 %copy-start.5 = (bf16[32,1024]{1,0:T(8,128)(2,1)}, bf16[32,1024]{1,0:T(8,128)(2,1)S(1)}, u32[]{:S(2)}) copy-start(bf16[32,1024]{1,0:T(8,128)(2,1)S(1)} %collective-permute-done.6.z3) | copy-start | bytes 196612
  23.7 0.6 copy-start.6
  24.4 0.6 copy-start.7
  26.7 14.1 %collective-permute-start.7 = (bf16[256,256]{1,0:T(8,128)(2,1)}, bf16[256,256]{1,0:T(8,128)(2,1)S(1)}, u32[]{:S(2)}, u32[]{:S(2)}) collective-permute-start(bf16[256,256]{1,0:T(8,128)(2,1)} %shard_map.124.table_mine), channel_id=1, source_target_pairs={{0,1},{1,0},{2,3},{3,2},{4,5},{5,4},{6,7},{7,6},{8,9},{9,8},{10,11... | collective-permute-start | bytes 393224 | tf_op jit(solution)/shard_map/ppermute | solution.py:471
  27.5 0.7 collective-permute-start.8
  39.1 1.7 %collective-permute-start.9 = (f32[16,480]{1,0:T(8,128)}, f32[16,480]{1,0:T(8,128)S(1)}, u32[]{:S(2)}, u32[]{:S(2)}) collective-permute-start(f32[16,480]{1,0:T(8,128)} %get-tuple-element.13), channel_id=1, source_target_pairs={{0,1},{1,0},{2,3},{3,2},{4,5},{5,4},{6,7},{7,6},{8,9},{9,8},{10,11... | collective-permute-start | bytes 92168 | tf_op jit(solution)/shard_map/ppermute | solution.py:471
  39.6 1.2 %collective-permute-start = (s32[8,16]{1,0:T(8,128)S(1)}, s32[8,16]{1,0:T(8,128)S(1)}, u32[]{:S(2)}, u32[]{:S(2)}) collective-permute-start(s32[8,16]{1,0:T(8,128)S(1)} %copy-done.19), channel_id=1, source_target_pairs={{0,1},{1,0},{2,3},{3,2},{4,5},{5,4},{6,7},{7,6},{8,9},{9,8},{10,11... | collective-permute-start | bytes 1544 | tf_op jit(solution)/shard_map/ppermute | solution.py:471
  40.8 0.6 copy-start
  44.0 15.1 %collective-permute-start.13 = (bf16[16,480]{1,0:T(8,128)(2,1)}, bf16[16,480]{1,0:T(8,128)(2,1)S(1)}, u32[]{:S(2)}, u32[]{:S(2)}) collective-permute-start(bf16[16,480]{1,0:T(8,128)(2,1)} %shard_map.126.refs_0_.p0.current), channel_id=1, source_target_pairs={{6,8},{8,6},{14,16},{16,14},{22,24},{24,22},{7,9},{9,7},{15,17},{1... | collective-permute-start | bytes 46088 | tf_op jit(solution)/shard_map/ppermute | solution.py:51
  44.6 14.4 %collective-permute-start.12 = (bf16[16,480]{1,0:T(8,128)(2,1)}, bf16[16,480]{1,0:T(8,128)(2,1)S(1)}, u32[]{:S(2)}, u32[]{:S(2)}) collective-permute-start(bf16[16,480]{1,0:T(8,128)(2,1)} %shard_map.126.refs_0_.p0.current), channel_id=1, source_target_pairs={{0,6},{2,4},{4,2},{6,0},{8,14},{10,12},{12,10},{14,8},{16,22},{18,... | collective-permute-start | bytes 46088 | tf_op jit(solution)/shard_map/ppermute | solution.py:21
  55.1 4.0 %collective-permute-start.11 = (bf16[16,480]{1,0:T(8,128)(2,1)}, bf16[16,480]{1,0:T(8,128)(2,1)S(1)}, u32[]{:S(2)}, u32[]{:S(2)}) collective-permute-start(bf16[16,480]{1,0:T(8,128)(2,1)} %shard_map.126.refs_0_.p0.current), channel_id=1, source_target_pairs={{0,4},{2,6},{4,0},{6,2},{8,12},{10,14},{12,8},{14,10},{16,20},{18,... | collective-permute-start | bytes 46088 | tf_op jit(solution)/shard_map/ppermute | solution.py:21
  55.1 3.9 %collective-permute-start.10 = (bf16[16,480]{1,0:T(8,128)(2,1)}, bf16[16,480]{1,0:T(8,128)(2,1)S(1)}, u32[]{:S(2)}, u32[]{:S(2)}) collective-permute-start(bf16[16,480]{1,0:T(8,128)(2,1)} %shard_map.126.refs_0_.p0.current), channel_id=1, source_target_pairs={{0,2},{2,0},{4,6},{6,4},{8,10},{10,8},{12,14},{14,12},{16,18},{18,... | collective-permute-start | bytes 46088 | tf_op jit(solution)/shard_map/ppermute | solution.py:21
  59.1 7.1 %copy-start.13 = (bf16[16,480]{1,0:T(8,128)(2,1)}, bf16[16,480]{1,0:T(8,128)(2,1)S(1)}, u32[]{:S(2)}) copy-start(bf16[16,480]{1,0:T(8,128)(2,1)S(1)} %collective-permute-done.13.refs_4_) | copy-start | bytes 46084
  59.1 7.1 %collective-permute-start.14 = (bf16[80,480]{1,0:T(8,128)(2,1)S(1)}, bf16[80,480]{1,0:T(8,128)(2,1)S(1)}, u32[]{:S(2)}, u32[]{:S(2)}) collective-permute-start(bf16[80,480]{1,0:T(8,128)(2,1)S(1)} %constant_dynamic-update-slice_fusion), channel_id=1, source_target_pairs={{0,1},{1,0},{2,3},{3,2},{4,5},{5,4},{6,7},{7,6},{8,9},{9,8},{10,11... | collective-permute-start | bytes 230408 | tf_op jit(solution)/shard_map/ppermute | solution.py:471
  61.8 15.0 %collective-permute-start.17 = (bf16[32,512]{1,0:T(8,128)(2,1)}, bf16[32,512]{1,0:T(8,128)(2,1)S(1)}, u32[]{:S(2)}, u32[]{:S(2)}) collective-permute-start(bf16[32,512]{1,0:T(8,128)(2,1)} %shard_map.128.z0), channel_id=1, source_target_pairs={{0,24},{2,26},{4,28},{6,30},{8,16},{10,18},{12,20},{14,22},{16,8},... | collective-permute-start | bytes 98312 | tf_op jit(solution)/shard_map/ppermute | solution.py:21
  64.4 12.3 %collective-permute-start.16 = (bf16[32,512]{1,0:T(8,128)(2,1)}, bf16[32,512]{1,0:T(8,128)(2,1)S(1)}, u32[]{:S(2)}, u32[]{:S(2)}) collective-permute-start(bf16[32,512]{1,0:T(8,128)(2,1)} %shard_map.128.z0), channel_id=1, source_target_pairs={{0,16},{2,18},{4,20},{6,22},{8,24},{10,26},{12,28},{14,30},{16,0},... | collective-permute-start | bytes 98312 | tf_op jit(solution)/shard_map/ppermute | solution.py:21
  65.3 11.5 %collective-permute-start.15 = (bf16[32,512]{1,0:T(8,128)(2,1)}, bf16[32,512]{1,0:T(8,128)(2,1)S(1)}, u32[]{:S(2)}, u32[]{:S(2)}) collective-permute-start(bf16[32,512]{1,0:T(8,128)(2,1)} %shard_map.128.z0), channel_id=1, source_target_pairs={{0,8},{2,10},{4,12},{6,14},{8,0},{10,2},{12,4},{14,6},{16,24},{18,... | collective-permute-start | bytes 98312 | tf_op jit(solution)/shard_map/ppermute | solution.py:21
  66.2 0.6 copy-start.12
  76.7 1.4 %collective-permute-start.18 = (f32[16,480]{1,0:T(8,128)}, f32[16,480]{1,0:T(8,128)S(1)}, u32[]{:S(2)}, u32[]{:S(2)}) collective-permute-start(f32[16,480]{1,0:T(8,128)} %get-tuple-element.17), channel_id=1, source_target_pairs={{0,1},{1,0},{2,3},{3,2},{4,5},{5,4},{6,7},{7,6},{8,9},{9,8},{10,11... | collective-permute-start | bytes 92168 | tf_op jit(solution)/shard_map/ppermute | solution.py:471
  76.8 1.4 %copy-start.14 = (bf16[32,512]{1,0:T(8,128)(2,1)}, bf16[32,512]{1,0:T(8,128)(2,1)S(1)}, u32[]{:S(2)}) copy-start(bf16[32,512]{1,0:T(8,128)(2,1)S(1)} %collective-permute-done.17.z3) | copy-start | bytes 98308
  76.8 1.4 %copy-start.15 = (bf16[32,512]{1,0:T(8,128)(2,1)}, bf16[32,512]{1,0:T(8,128)(2,1)S(1)}, u32[]{:S(2)}) copy-start(bf16[32,512]{1,0:T(8,128)(2,1)S(1)} %collective-permute-done.16.z2) | copy-start | bytes 98308
  76.8 1.4 %copy-start.16 = (bf16[32,512]{1,0:T(8,128)(2,1)}, bf16[32,512]{1,0:T(8,128)(2,1)S(1)}, u32[]{:S(2)}) copy-start(bf16[32,512]{1,0:T(8,128)(2,1)S(1)} %collective-permute-done.15.z1) | copy-start | bytes 98308
  81.2 1.4 %collective-permute-start.19 = (bf16[16,480]{1,0:T(8,128)(2,1)}, bf16[16,480]{1,0:T(8,128)(2,1)S(1)}, u32[]{:S(2)}, u32[]{:S(2)}) collective-permute-start(bf16[16,480]{1,0:T(8,128)(2,1)} %shard_map.129.mine), channel_id=1, source_target_pairs={{0,1},{1,0},{2,3},{3,2},{4,5},{5,4},{6,7},{7,6},{8,9},{9,8},{10,11... | collective-permute-start | bytes 46088 | tf_op jit(solution)/shard_map/ppermute | solution.py:471
  (10 other events, 6.0 us)

commit v3 on v2

--- a/solution.py
+++ b/solution.py
@@ -222,7 +222,7 @@
 SM = pl.BlockSpec(memory_space=pltpu.SMEM)
 
 
-def call(kernel, outs, specs, args, scratch=(), flops=0, moved=0):
+def call(kernel, outs, specs, args, scratch=(), flops=0, moved=6 << 20, limit=4 << 20):
     return pl.pallas_call(
         kernel,
         out_shape=tuple(jax.ShapeDtypeStruct(shape, kind) for shape, kind in outs),
@@ -230,10 +230,17 @@
         out_specs=(VM,) * len(outs),
         scratch_shapes=list(scratch),
         cost_estimate=pl.CostEstimate(flops=flops, bytes_accessed=moved, transcendentals=0),
+        compiler_params=pltpu.CompilerParams(vmem_limit_bytes=limit),
     )(*args)
 
 
-def pack_kernel(place, box, vectors, angle, factors, out):
+def here():
+    near_pos = lax.axis_index("near")
+    return lax.axis_index("far"), near_pos % 4, near_pos // 4, near_pos
+
+
+def pack_kernel(box, vectors, angle, factors, out, edge):
+    place = here()
     spheres, newton, width = vectors.shape
     share = newton // 2
     waves = angle.shape[1]
@@ -254,6 +261,7 @@
     out[pl.ds(0, spheres), pl.ds(1024, waves)] = hi
     out[pl.ds(spheres, spheres), pl.ds(1024, waves)] = low
     out[:, pl.ds(1024 + waves, factors.shape[0])] = factors[...].T.astype(BF16)
+    edge[...] = out[:, pl.ds(0, 1024)]
 
 
 def sum_rows(member, waves):
@@ -271,7 +279,8 @@
     return jnp.concatenate([re * cosine - im * sine, re * sine + im * cosine], axis=1)
 
 
-def first_waves_kernel(boxes, place, p0, p1, p2, p3, agg, out, turn, member, table):
+def first_waves_kernel(boxes, p0, p1, p2, p3, agg, out, turn, member, table):
+    place = here()
     parts = (p0, p1, p2, p3)
     width = agg.shape[0]
     waves = agg.shape[1] // 2
@@ -301,14 +310,18 @@
         out[:, pl.ds(2 * waves + j * span, span)] = table[pl.ds(j * lines, lines), :].astype(BF16)
 
 
-def next_waves_kernel(p0, p1, p2, p3, agg, turn, member, out):
+def next_waves_kernel(p0, p1, p2, p3, p4, agg, turn, member, out, around):
     waves = agg.shape[1] // 2
+    rows = p0.shape[0]
+    for j, part in enumerate((p0, p1, p2, p3, p4)):
+        around[pl.ds(j * rows, rows), :] = part[...]
     flat = jnp.concatenate([p0[...], p1[...], p2[...], p3[...]], axis=0)
     product = jnp.dot(flat, agg[...], preferred_element_type=F32)
     out[...] = sum_rows(member[...], turned(product, turn[...], waves)).astype(BF16)
 
 
-def table_kernel(waves, place, z0, z1, z2, z3, out, held):
+def table_kernel(waves, z0, z1, z2, z3, out, held):
+    place = here()
     lines = z0.shape[0]
     span = held.shape[1]
     pieces = (z0.shape[1] - 2 * waves) // span
@@ -319,91 +332,101 @@
     out[...] = held[...].T.astype(BF16)
 
 
-def near_kernel(starts, emit, place, neighbours, live, *refs):
+def near_kernel(starts, emit, neighbours, live, *refs):
+    place = here()
     mine, theirs = refs[:5], refs[5 : 5 + (5 if starts[1] is not None else 1)]
     refs = refs[5 + len(theirs) :]
     blocks = refs[0]
     out_mine, out_theirs = refs[1], refs[2]
     image = refs[3] if emit else None
-    held = refs[-1]
-    n = pl.program_id(0)
+    held = refs[4]
+    if not emit:
+        source_blocks, blocks, arrived = blocks, refs[3], refs[5]
+        copies = [
+            pltpu.make_async_copy(source_blocks.at[n], blocks.at[n], arrived.at[n])
+            for n in range(blocks.shape[0])
+        ]
+        for copy in copies:
+            copy.start()
     spheres = out_mine.shape[0] // 2
     slots = blocks.shape[1]
     coeffs = blocks.shape[3]
-
-    @pl.when(n == 0)
-    def _():
-        for j in range(5):
-            for side in range(2):
-                for r in range(2):
-                    rows = pl.ds(r * spheres, spheres)
-                    if side == 0:
-                        value = mine[j][rows, pl.ds(0, 2 * coeffs)]
-                    elif starts[1] is not None:
-                        value = theirs[j][rows, pl.ds(starts[1], 2 * coeffs)]
-                    else:
-                        value = theirs[0][pl.ds((2 * j + r) * spheres, spheres), :]
-                    value = value.astype(F32)
-                    at = pl.ds(j * spheres, spheres)
-                    held[at, side * 2 + r, :] = value[:, :coeffs]
-                    held[at, 4 + side * 2 + r, :] = value[:, coeffs:]
-        if emit:
-            first = place[0] == 0
+    for j in range(5):
+        for side in range(2):
             for r in range(2):
-                own = mine[0][pl.ds(r * spheres, spheres), :].astype(F32)
-                other = theirs[0][pl.ds(r * spheres, spheres), :].astype(F32)
-                image[:, r, :] = jnp.where(first, own, other).astype(BF16)
-                image[:, 2 + r, :] = jnp.where(first, other, own).astype(BF16)
-
-    real = jnp.zeros((8, coeffs), F32)
-    imag = jnp.zeros((8, coeffs), F32)
-    for k in range(slots):
-        source = neighbours[n, k]
-        chip = source // spheres
-        near = jnp.where(chip // 4 == place[3] // 4, chip ^ place[3], 4)
-        value = held[near * spheres + source % spheres]
-        alive = place[0] * slots + k < live[n]
-        value = jnp.where(alive, value, 0.0).astype(BF16)
-        real += jnp.dot(value, blocks[0, k, 0], preferred_element_type=F32)
-        imag += jnp.dot(value, blocks[0, k, 1], preferred_element_type=F32)
-    near_re = real[:4] - imag[4:]
-    near_im = imag[:4] + real[4:]
-    for r in range(2):
-        row = pl.ds(r * spheres + n, 1)
-        out_mine[row, pl.ds(0, coeffs)] = near_re[r : r + 1]
-        out_mine[row, pl.ds(coeffs, coeffs)] = near_im[r : r + 1]
-        out_theirs[row, pl.ds(0, coeffs)] = near_re[2 + r : 3 + r]
-        out_theirs[row, pl.ds(coeffs, coeffs)] = near_im[2 + r : 3 + r]
-
-
-def near_call(starts, emit, place, neighbours, live, mine, theirs, blocks):
+                rows = pl.ds(r * spheres, spheres)
+                if side == 0:
+                    value = mine[j][rows, pl.ds(0, 2 * coeffs)]
+                elif starts[1] is not None:
+                    value = theirs[j][rows, pl.ds(starts[1], 2 * coeffs)]
+                else:
+                    value = theirs[0][pl.ds((2 * j + r) * spheres, spheres), :]
+                value = value.astype(F32)
+                at = pl.ds(j * spheres, spheres)
+                held[at, side * 2 + r, :] = value[:, :coeffs]
+                held[at, 4 + side * 2 + r, :] = value[:, coeffs:]
+    if emit:
+        first = place[0] == 0
+        for r in range(2):
+            own = mine[0][pl.ds(r * spheres, spheres), :].astype(F32)
+            other = theirs[0][pl.ds(r * spheres, spheres), :].astype(F32)
+            image[:, r, :] = jnp.where(first, own, other).astype(BF16)
+            image[:, 2 + r, :] = jnp.where(first, other, own).astype(BF16)
+
+    for n in range(spheres):
+        real = jnp.zeros((8, coeffs), F32)
+        imag = jnp.zeros((8, coeffs), F32)
+        if not emit:
+            copies[n].wait()
+        for k in range(slots):
+            source = neighbours[n, k]
+            chip = source // spheres
+            near = jnp.where(chip // 4 == place[3] // 4, chip ^ place[3], 4)
+            value = held[near * spheres + source % spheres]
+            alive = place[0] * slots + k < live[n]
+            value = jnp.where(alive, value, 0.0).astype(BF16)
+            real += jnp.dot(value, blocks[n, k, 0], preferred_element_type=F32)
+            imag += jnp.dot(value, blocks[n, k, 1], preferred_element_type=F32)
+        near_re = real[:4] - imag[4:]
+        near_im = imag[:4] + real[4:]
+        for r in range(2):
+            row = pl.ds(r * spheres + n, 1)
+            out_mine[row, pl.ds(0, coeffs)] = near_re[r : r + 1]
+            out_mine[row, pl.ds(coeffs, coeffs)] = near_im[r : r + 1]
+            out_theirs[row, pl.ds(0, coeffs)] = near_re[2 + r : 3 + r]
+            out_theirs[row, pl.ds(coeffs, coeffs)] = near_im[2 + r : 3 + r]
+
+
+def near_call(starts, emit, neighbours, live, mine, theirs, blocks):
     spheres, slots, _, coeffs, _ = blocks.shape
     rows = 2 * spheres
     outs = [jax.ShapeDtypeStruct((rows, 2 * coeffs), F32)] * 2
     if emit:
         outs.append(jax.ShapeDtypeStruct((spheres, 4, 2 * coeffs), BF16))
+    else:
+        outs.append(pltpu.VMEM(blocks.shape, BF16))
     full = [VM] * (len(mine) + len(theirs))
     return pl.pallas_call(
         functools.partial(near_kernel, starts, emit),
-        grid=(spheres,),
         out_shape=tuple(outs),
-        in_specs=[SM] * 3
-        + full
-        + [pl.BlockSpec((1, slots, 2, coeffs, coeffs), lambda n: (n, 0, 0, 0, 0))],
+        in_specs=[SM] * 2 + full + [VM if emit else pl.BlockSpec(memory_space=pl.ANY)],
         out_specs=(VM,) * len(outs),
-        scratch_shapes=[pltpu.VMEM((5 * spheres, 8, coeffs), F32)],
+        scratch_shapes=[pltpu.VMEM((5 * spheres, 8, coeffs), F32)]
+        + ([] if emit else [pltpu.SemaphoreType.DMA((spheres,))]),
         cost_estimate=pl.CostEstimate(
             flops=2 * 8 * 2 * coeffs * coeffs * spheres * slots,
             bytes_accessed=blocks.size * 2,
             transcendentals=0,
         ),
-    )(place, neighbours, live, *mine, *theirs, blocks)
+        compiler_params=pltpu.CompilerParams(vmem_limit_bytes=(4 if emit else 34) << 20),
+    )(neighbours, live, *mine, *theirs, blocks)
 
 
 def finish_kernel(
-    place, box, list_mine, list_theirs, z0, z1, z2, z3, table_mine, table_theirs, turn, dis,
+    box, list_mine, list_theirs, z0, z1, z2, z3, table_mine, table_theirs, turn, dis,
     near_mine, near_got, tmatrix, current, out, source, factor, field, local
 ):
+    place = here()
     own_boxes, listed = list_mine.shape
     boxes = 2 * own_boxes
     waves = source.shape[2]
@@ -447,7 +470,8 @@
     cosine = turn[pl.ds(0, 2 * spheres), pl.ds(0, waves)]
     sine = turn[pl.ds(0, 2 * spheres), pl.ds(waves, waves)]
     shifted = jnp.concatenate([re * cosine + im * sine, im * cosine - re * sine], axis=1)
-    total = jnp.dot(shifted.astype(BF16), dis[...], preferred_element_type=F32)
+    dims = (((1,), (1,)), ((), ()))
+    total = lax.dot_general(shifted.astype(BF16), dis[...], dims, preferred_element_type=F32)
     total += near_mine[...] + near_got[...]
     t_re = jnp.concatenate([tmatrix[:, 0], tmatrix[:, 0]], axis=0)
     t_im = jnp.concatenate([tmatrix[:, 1], tmatrix[:, 1]], axis=0)
@@ -457,9 +481,9 @@
     out[:, pl.ds(coeffs, coeffs)] = (start[:, coeffs:] - (t_re * f_im + t_im * f_re)).astype(BF16)
 
 
-def join_kernel(place, mine, theirs, out):
+def join_kernel(mine, theirs, out):
     spheres = out.shape[0]
-    first = place[0] == 0
+    first = lax.axis_index("far") == 0
     for r in range(2):
         own = mine[pl.ds(r * spheres, spheres), :].astype(F32)
         other = theirs[pl.ds(r * spheres, spheres), :].astype(F32)
@@ -481,22 +505,20 @@
     boxes = 2 * own_boxes
     waves = agg_matrix.shape[1] // 2
     rows = spheres * newton // 2
-    near_pos = lax.axis_index("near")
-    place = jnp.stack([lax.axis_index("far"), near_pos % 4, near_pos // 4, near_pos])
-    place = place.astype(jnp.int32)
     entries = own_boxes * listed * 2
-    message = call(
+    message, edge = call(
         pack_kernel,
-        [((rows, 1024 + waves + entries), BF16)],
-        [SM, SM, VM, VM, VM],
-        (place, sphere_box, vectors, agg_angle, far_factors.reshape(entries, -1)),
-    )[0]
+        [((rows, 1024 + waves + entries), BF16), ((rows, 1024), BF16)],
+        [SM, VM, VM, VM],
+        (sphere_box, vectors, agg_angle, far_factors.reshape(entries, -1)),
+    )
     list_theirs = swap_far(far_list)
-    current, edge = message, edge_rows(message[:, :1024])
+    current, edge = message, edge_rows(edge)
     table = None
     for step in range(2):
         if step == 0:
             parts = xor_gather(message, (1, 2, 3))
+            parts, edge, list_theirs = lax.optimization_barrier((parts, edge, list_theirs))
             block, turn, member, _ = call(
                 functools.partial(first_waves_kernel, boxes),
                 [
@@ -505,45 +527,46 @@
                     ((4 * rows, 2 * boxes), BF16),
                     ((waves // 4, entries), F32),
                 ],
-                [SM] + [VM] * 5,
-                (place, *parts, agg_matrix),
+                [VM] * 5,
+                (*parts, agg_matrix),
             )
         else:
             edge = edge_rows(current)
             parts = xor_gather(current, (1, 2, 3))
-            block = call(
+            block, around = call(
                 next_waves_kernel,
-                [((2 * boxes, 2 * waves), BF16)],
-                [VM] * 7,
-                (*parts, agg_matrix, turn, member),
-            )[0]
+                [((2 * boxes, 2 * waves), BF16), ((5 * rows, width), BF16)],
+                [VM] * 8,
+                (*parts, edge, agg_matrix, turn, member),
+            )
         pieces = xor_gather(block, (4, 8, 12))
         mine = (*parts, edge)
         if step == 0:
-            near_mine, near_theirs = near_call(
-                (0, 512), False, place, neighbours, live_counts, mine, mine, near_blocks
+            near_mine, near_theirs, held_blocks = near_call(
+                (0, 512), False, neighbours, live_counts, mine, mine, near_blocks
             )
         else:
-            theirs = swap_far(jnp.concatenate(mine, axis=0))
+            theirs = swap_far(around)
             near_mine, near_theirs, first_image = near_call(
-                (0, None), True, place, neighbours, live_counts, mine, (theirs,), near_blocks
+                (0, None), True, neighbours, live_counts, mine, (theirs,), held_blocks
             )
         near_got = swap_far(near_theirs)
         if step == 0:
+            pieces, near_mine = lax.optimization_barrier((pieces, near_mine))
             table = call(
                 functools.partial(table_kernel, waves),
                 [((entries, waves), BF16)],
-                [SM] + [VM] * 4,
-                (place, *pieces),
+                [VM] * 4,
+                (*pieces,),
                 [pltpu.VMEM((waves, entries), F32)],
             )[0]
             table = (table, swap_far(table))
         current = call(
             finish_kernel,
             [((rows, width), BF16)],
-            [SM] * 4 + [VM] * 12,
+            [SM] * 3 + [VM] * 12,
             (
-                place, sphere_box, far_list, list_theirs, *pieces, *table, turn, dis_matrix,
+                sphere_box, far_list, list_theirs, *pieces, *table, turn, dis_matrix.T,
                 near_mine, near_got, tmatrix, current
             ),
             [
@@ -556,8 +579,8 @@
     second_image = call(
         join_kernel,
         [((spheres, newton, width), BF16)],
-        [SM, VM, VM],
-        (place, current, swap_far(current)),
+        [VM, VM],
+        (current, swap_far(current)),
     )[0]
     return first_image, second_image
 

time: 85.2 us -> 56.8 us (0.67)
  Pallas kernels: 34.4 us -> 15.5 us
  waiting for transfers between devices: 14.2 us -> 9.43 us
  local copies, waits for them, and re-layouts: 8.06 us -> 5.4 us
  starting transfers between devices: 26.5 us -> 25.3 us
    pallas_call x2, Pallas kernels: 20.3 us -> 10.4 us  [near_call(): pl.pallas_call(functools.partial(near_kernel, starts, emit), out_shape=tu...]
    pallas_call x7, Pallas kernels: 14.1 us -> 5.17 us  [call(): pl.pallas_call(kernel, out_shape=tuple((jax.ShapeDtypeStruct(shape, kind)...]
    ppermute x12, waiting for transfers between devices: 11.5 us -> 5.02 us  [swap_near(): return lax.ppermute(block, 'near', [(i, i ^ mask) for i in range(count)])]
    unnamed x49 -> x24, local copies, waits for them, and re-layouts: 7.3 us -> 5.4 us
    ppermute x6, waiting for transfers between devices: 2.66 us -> 4.41 us  [swap_far(): return lax.ppermute(block, 'far', [(0, 1), (1, 0)])]
    ppermute x12, starting transfers between devices: 24.3 us -> 23.1 us  [swap_near(): return lax.ppermute(block, 'near', [(i, i ^ mask) for i in range(count)])]
  transfers between devices with their start and end apart: 20 -> 20, of which waited for: 9 -> 9; matrix products, arithmetic and copies ran while one was open for 3% -> 0% of each run, Pallas kernels for 26% -> 18%
where the time goes in v3:
time: 56.8 us; the launch traced here: 56.4 us
  starting transfers between devices  25.3 us (45%)
  Pallas kernels  15.5 us (27%)
  waiting for transfers between devices  9.43 us (17%)
  local copies, waits for them, and re-layouts  5.4 us (10%)
  between operations  0.78 us (1%)
    ppermute x12, starting transfers between devices, swap_near(): return lax.ppermute(block, 'near', [(i, i ^ mask) for i in range(count)])  23.1 us
    pallas_call x2, Pallas kernels, near_call(): pl.pallas_call(functools.partial(near_kernel, starts, emit), out_shape=tu...  10.4 us
    unnamed x24, local copies, waits for them, and re-layouts  5.4 us
    pallas_call x7, Pallas kernels, call(): pl.pallas_call(kernel, out_shape=tuple((jax.ShapeDtypeStruct(shape, kind)...  5.17 us
    ppermute x12, waiting for transfers between devices, swap_near(): return lax.ppermute(block, 'near', [(i, i ^ mask) for i in range(count)])  5.02 us
    ppermute x6, waiting for transfers between devices, swap_far(): return lax.ppermute(block, 'far', [(0, 1), (1, 0)])  4.41 us
    ppermute x2, starting transfers between devices, edge_rows(): lax.ppermute(block, 'near', pairs)  1.32 us
  transfers between devices with their start and end apart: 20, of which 9 were waited for; matrix products, arithmetic and copies ran while one was open for 0% of the time, Pallas kernels for 18%

profile of v3, /device:TPU:0, one launch (start us, length us, event | category | flops | bytes accessed | tf_op | source)
XLA Modules:
  0.0 56.4 jit_solution(12731002263540393250)
XLA Ops:
  0.7 0.9 %copy-done.3 = f32[8,16,2,16]{3,2,1,0:T(2,128)S(1)} copy-done((f32[8,16,2,16]{3,2,1,0:T(2,128)S(1)}, f32[8,16,2,16]{3,2,1,0:T(2,128)}, u32[]{:S(2)}) %copy-start.3) | copy-done | bytes 16408
  1.6 0.8 %copy-done.5 = bf16[8,4,480]{2,1,0:T(4,128)(2,1)S(1)} copy-done((bf16[8,4,480]{2,1,0:T(4,128)(2,1)S(1)}, bf16[8,4,480]{2,1,0:T(4,128)(2,1)}, u32[]{:S(2)}) %copy-start.5) | copy-done | bytes 30744
  2.3 0.7 %copy-done.8 = f32[8,256]{1,0:T(8,128)S(1)} copy-done((f32[8,256]{1,0:T(8,128)S(1)}, f32[8,256]{1,0:T(8,128)}, u32[]{:S(2)}) %copy-start.8) | copy-done | bytes 8216
  3.0 0.7 %copy-done.9 = s32[8]{0:T(128)S(1)} copy-done((s32[8]{0:T(128)S(1)}, s32[8]{0:T(128)}, u32[]{:S(2)}) %copy-start.9) | copy-done | bytes 56
  3.7 0.7 %shard_map.122 = (bf16[16,1536]{1,0:T(8,128)(2,1)S(1)}, bf16[16,1024]{1,0:T(8,128)(2,1)S(1)}) custom-call(s32[8]{0:T(128)S(1)} %copy-done.9, bf16[8,4,480]{2,1,0:T(4,128)(2,1)S(1)} %copy-done.5, f32[8,256]{1,0:T(8,128)S(1)} %copy-done.8, f32[256,16]{1,0:T(8,128)S(1)} %bitcast.4), custom_call_target="tpu_custom_call" | custom-call | bytes 6291456 | tf_op jit(solution)/shard_map/pallas_call | solution.py:226
  4.3 4.0 %collective-permute-start.2 = (bf16[16,1536]{1,0:T(8,128)(2,1)S(1)}, bf16[16,1536]{1,0:T(8,128)(2,1)S(1)}, u32[]{:S(2)}, u32[]{:S(2)}) collective-permute-start(bf16[16,1536]{1,0:T(8,128)(2,1)S(1)} %get-tuple-element.29.p0.refs_0_.refs_5_.current), channel_id=1, source_target_pairs={{0,6},{2,4},{4,2},{6,0},{8,14},{10,12},{12,10},{14,8},{16,22},{18,... | collective-permute-start | bytes 147464 | tf_op jit(solution)/shard_map/ppermute | solution.py:21
  8.3 0.5 collective-permute-start.1
  9.0 0.7 %collective-permute-start.3 = (bf16[16,1024]{1,0:T(8,128)(2,1)S(1)}, bf16[16,1024]{1,0:T(8,128)(2,1)S(1)}, u32[]{:S(2)}, u32[]{:S(2)}) collective-permute-start(bf16[16,1024]{1,0:T(8,128)(2,1)S(1)} %get-tuple-element.27), channel_id=1, source_target_pairs={{6,8},{8,6},{14,16},{16,14},{22,24},{24,22},{7,9},{9,7},{15,17},{1... | collective-permute-start | bytes 98312 | tf_op jit(solution)/shard_map/ppermute | solution.py:51
  9.7 1.4 %collective-permute-done.4.list_theirs = s32[8,16]{1,0:T(8,128)S(1)} collective-permute-done((s32[8,16]{1,0:T(8,128)}, s32[8,16]{1,0:T(8,128)S(1)}, u32[]{:S(2)}, u32[]{:S(2)}) %collective-permute-start.4) | collective-permute-done | bytes 544 | tf_op jit(solution)/shard_map/ppermute | solution.py:495
  11.1 1.3 %collective-permute-done.1.p2.refs_2_.refs_7_ = bf16[16,1536]{1,0:T(8,128)(2,1)S(1)} collective-permute-done((bf16[16,1536]{1,0:T(8,128)(2,1)S(1)}, bf16[16,1536]{1,0:T(8,128)(2,1)S(1)}, u32[]{:S(2)}, u32[]{:S(2)}) %collective-permute-start.1) | collective-permute-done | bytes 49184 | tf_op jit(solution)/shard_map/ppermute | solution.py:21
  12.4 0.5 collective-permute-done.p1.refs_1_.refs_6_
  12.9 1.0 %copy-done = bf16[480,512]{1,0:T(8,128)(2,1)S(1)} copy-done((bf16[480,512]{1,0:T(8,128)(2,1)S(1)}, bf16[480,512]{1,0:T(8,128)(2,1)}, u32[]{:S(2)}) %copy-start) | copy-done | bytes 491544
  13.9 0.9 %shard_map.123 = (bf16[32,1024]{1,0:T(8,128)(2,1)S(1)}, f32[64,512]{1,0:T(8,128)S(1)}, bf16[64,32]{1,0:T(8,128)(2,1)S(1)}, f32[64,256]{1,0:T(8,128)}) custom-call(bf16[16,1536]{1,0:T(8,128)(2,1)S(1)} %get-tuple-element.29.p0.refs_0_.refs_5_.current, bf16[16,1536]{1,0:T(8,128)(2,1)S(1)} %collective-permute-done.p1.refs_1_.refs_6_, ...), custom_call_target="tpu_custom_call" | custom-call | bytes 6291456 | tf_op jit(solution)/shard_map/pallas_call | solution.py:226
  14.9 7.7 %collective-permute-start.7 = (bf16[32,1024]{1,0:T(8,128)(2,1)S(1)}, bf16[32,1024]{1,0:T(8,128)(2,1)S(1)}, u32[]{:S(2)}, u32[]{:S(2)}) collective-permute-start(bf16[32,1024]{1,0:T(8,128)(2,1)S(1)} %get-tuple-element.36.z0), channel_id=1, source_target_pairs={{0,24},{2,26},{4,28},{6,30},{8,16},{10,18},{12,20},{14,22},{16,8},... | collective-permute-start | bytes 196616 | tf_op jit(solution)/shard_map/ppermute | solution.py:21
  22.5 0.6 collective-permute-start.5
  23.1 0.7 %copy-done.7 = s32[8,8]{1,0:T(8,128)S(1)} copy-done((s32[8,8]{1,0:T(8,128)S(1)}, s32[8,8]{1,0:T(8,128)}, u32[]{:S(2)}) %copy-start.7) | copy-done | bytes 280
  23.8 0.7 %copy-done.11 = s32[8]{0:T(128)S(1)} copy-done((s32[8]{0:T(128)S(1)}, s32[8]{0:T(128)}, u32[]{:S(2)}) %copy-start.11) | copy-done | bytes 56
  24.4 6.7 %shard_map.124 = (f32[16,480]{1,0:T(8,128)S(1)}, f32[16,480]{1,0:T(8,128)S(1)}, bf16[8,8,2,240,240]{4,3,2,1,0:T(8,128)(2,1)S(1)}) custom-call(s32[8,8]{1,0:T(8,128)S(1)} %copy-done.7, s32[8]{0:T(128)S(1)} %copy-done.11, bf16[16,1536]{1,0:T(8,128)(2,1)S(1)} %get-tuple-element.29.p0.refs_0_.refs_5_.current, ...), custom_call_target="tpu_custom_call" | custom-call | flops 117964800 | bytes 14745600 | tf_op jit(solution)/shard_map/pallas_call | solution.py:409
  31.9 0.9 %collective-permute-done.9.near_got = f32[16,480]{1,0:T(8,128)S(1)} collective-permute-done((f32[16,480]{1,0:T(8,128)S(1)}, f32[16,480]{1,0:T(8,128)S(1)}, u32[]{:S(2)}, u32[]{:S(2)}) %collective-permute-start.9) | collective-permute-done | bytes 30752 | tf_op jit(solution)/shard_map/ppermute | solution.py:495
  32.8 1.2 %shard_map.126.p0.refs_0_.current = bf16[16,480]{1,0:T(8,128)(2,1)S(1)} custom-call(s32[8]{0:T(128)S(1)} %copy-done.10, s32[8,16]{1,0:T(8,128)S(1)} %copy-done.6, s32[8,16]{1,0:T(8,128)S(1)} %collective-permute-done.4.list_theirs, bf16[32,1024]{1,0:T(8,128)(2,1)S(1)} %get-tuple-element.36.z0, bf16[32,1024]{1,0:T(8,128)(2,1)S(1)} %collective-permute-done.5.z1, ...), custom_call_target="tpu_custom_call" | custom-call | bytes 6291456 | tf_op jit(solution)/shard_map/pallas_call | solution.py:226
  34.1 0.7 %collective-permute-start.13 = (bf16[16,480]{1,0:T(8,128)(2,1)S(1)}, bf16[16,480]{1,0:T(8,128)(2,1)S(1)}, u32[]{:S(2)}, u32[]{:S(2)}) collective-permute-start(bf16[16,480]{1,0:T(8,128)(2,1)S(1)} %shard_map.126.p0.refs_0_.current), channel_id=1, source_target_pairs={{6,8},{8,6},{14,16},{16,14},{22,24},{24,22},{7,9},{9,7},{15,17},{1... | collective-permute-start | bytes 46088 | tf_op jit(solution)/shard_map/ppermute | solution.py:51
  34.8 5.1 %collective-permute-start.12 = (bf16[16,480]{1,0:T(8,128)(2,1)S(1)}, bf16[16,480]{1,0:T(8,128)(2,1)S(1)}, u32[]{:S(2)}, u32[]{:S(2)}) collective-permute-start(bf16[16,480]{1,0:T(8,128)(2,1)S(1)} %shard_map.126.p0.refs_0_.current), channel_id=1, source_target_pairs={{0,6},{2,4},{4,2},{6,0},{8,14},{10,12},{12,10},{14,8},{16,22},{18,... | collective-permute-start | bytes 46088 | tf_op jit(solution)/shard_map/ppermute | solution.py:21
  39.9 0.6 %collective-permute-start.10 = (bf16[16,480]{1,0:T(8,128)(2,1)S(1)}, bf16[16,480]{1,0:T(8,128)(2,1)S(1)}, u32[]{:S(2)}, u32[]{:S(2)}) collective-permute-start(bf16[16,480]{1,0:T(8,128)(2,1)S(1)} %shard_map.126.p0.refs_0_.current), channel_id=1, source_target_pairs={{0,2},{2,0},{4,6},{6,4},{8,10},{10,8},{12,14},{14,12},{16,18},{18,... | collective-permute-start | bytes 46088 | tf_op jit(solution)/shard_map/ppermute | solution.py:21
  40.5 1.1 %collective-permute-done.12.p3.refs_3_ = bf16[16,480]{1,0:T(8,128)(2,1)S(1)} collective-permute-done((bf16[16,480]{1,0:T(8,128)(2,1)S(1)}, bf16[16,480]{1,0:T(8,128)(2,1)S(1)}, u32[]{:S(2)}, u32[]{:S(2)}) %collective-permute-start.12) | collective-permute-done | bytes 15392 | tf_op jit(solution)/shard_map/ppermute | solution.py:21
  41.6 2.0 %collective-permute-done.11.p2.refs_2_ = bf16[16,480]{1,0:T(8,128)(2,1)S(1)} collective-permute-done((bf16[16,480]{1,0:T(8,128)(2,1)S(1)}, bf16[16,480]{1,0:T(8,128)(2,1)S(1)}, u32[]{:S(2)}, u32[]{:S(2)}) %collective-permute-start.11) | collective-permute-done | bytes 15392 | tf_op jit(solution)/shard_map/ppermute | solution.py:21
  44.0 3.0 %collective-permute-start.17 = (bf16[32,512]{1,0:T(8,128)(2,1)S(1)}, bf16[32,512]{1,0:T(8,128)(2,1)S(1)}, u32[]{:S(2)}, u32[]{:S(2)}) collective-permute-start(bf16[32,512]{1,0:T(8,128)(2,1)S(1)} %get-tuple-element.47.z0), channel_id=1, source_target_pairs={{0,24},{2,26},{4,28},{6,30},{8,16},{10,18},{12,20},{14,22},{16,8},... | collective-permute-start | bytes 98312 | tf_op jit(solution)/shard_map/ppermute | solution.py:21
  47.4 1.1 %collective-permute-start.15 = (bf16[32,512]{1,0:T(8,128)(2,1)S(1)}, bf16[32,512]{1,0:T(8,128)(2,1)S(1)}, u32[]{:S(2)}, u32[]{:S(2)}) collective-permute-start(bf16[32,512]{1,0:T(8,128)(2,1)S(1)} %get-tuple-element.47.z0), channel_id=1, source_target_pairs={{0,8},{2,10},{4,12},{6,14},{8,0},{10,2},{12,4},{14,6},{16,24},{18,... | collective-permute-start | bytes 98312 | tf_op jit(solution)/shard_map/ppermute | solution.py:21
  48.4 3.6 %shard_map.128 = (f32[16,480]{1,0:T(8,128)S(1)}, f32[16,480]{1,0:T(8,128)S(1)}, bf16[8,4,480]{2,1,0:T(4,128)(2,1)}) custom-call(s32[8,8]{1,0:T(8,128)S(1)} %copy-done.7, s32[8]{0:T(128)S(1)} %copy-done.11, bf16[16,480]{1,0:T(8,128)(2,1)S(1)} %shard_map.126.p0.refs_0_.current, bf16[16,480]{1,0:T(8,128)(2,1)S(1)} %collective-permute-done.10.p1.refs_1_, ...), custom_call_target="tpu_custom_call" | custom-call | flops 117964800 | bytes 14745600 | tf_op jit(solution)/shard_map/pallas_call | solution.py:409
  52.1 1.1 %collective-permute-done.18.near_got = f32[16,480]{1,0:T(8,128)S(1)} collective-permute-done((f32[16,480]{1,0:T(8,128)S(1)}, f32[16,480]{1,0:T(8,128)S(1)}, u32[]{:S(2)}, u32[]{:S(2)}) %collective-permute-start.18) | collective-permute-done | bytes 30752 | tf_op jit(solution)/shard_map/ppermute | solution.py:495
  53.3 1.2 %shard_map.129.mine = bf16[16,480]{1,0:T(8,128)(2,1)S(1)} custom-call(s32[8]{0:T(128)S(1)} %copy-done.10, s32[8,16]{1,0:T(8,128)S(1)} %copy-done.6, s32[8,16]{1,0:T(8,128)S(1)} %collective-permute-done.4.list_theirs, bf16[32,512]{1,0:T(8,128)(2,1)S(1)} %get-tuple-element.47.z0, bf16[32,512]{1,0:T(8,128)(2,1)S(1)} %collective-permute-done.15.z1, ...), custom_call_target="tpu_custom_call" | custom-call | bytes 6291456 | tf_op jit(solution)/shard_map/pallas_call | solution.py:226
  54.7 1.0 %collective-permute-done.19.theirs = bf16[16,480]{1,0:T(8,128)(2,1)S(1)} collective-permute-done((bf16[16,480]{1,0:T(8,128)(2,1)S(1)}, bf16[16,480]{1,0:T(8,128)(2,1)S(1)}, u32[]{:S(2)}, u32[]{:S(2)}) %collective-permute-start.19) | collective-permute-done | bytes 15392 | tf_op jit(solution)/shard_map/ppermute | solution.py:495
  55.8 0.7 %shard_map.130 = bf16[8,4,480]{2,1,0:T(4,128)(2,1)} custom-call(bf16[16,480]{1,0:T(8,128)(2,1)S(1)} %shard_map.129.mine, bf16[16,480]{1,0:T(8,128)(2,1)S(1)} %collective-permute-done.19.theirs), custom_call_target="tpu_custom_call" | custom-call | bytes 6291456 | tf_op jit(solution)/shard_map/pallas_call | solution.py:226
  (41 shorter events, 1.9 us)
Async XLA Ops:
  0.6 32.2 %copy-start.10 = (s32[8]{0:T(128)S(1)}, s32[8]{0:T(128)}, u32[]{:S(2)}) copy-start(s32[8]{0:T(128)} %box.5) | copy-start | bytes 100
  0.6 0.9 %copy-start.3 = (f32[8,16,2,16]{3,2,1,0:T(2,128)S(1)}, f32[8,16,2,16]{3,2,1,0:T(2,128)}, u32[]{:S(2)}) copy-start(f32[8,16,2,16]{3,2,1,0:T(2,128)} %param.20) | copy-start | bytes 49156
  1.6 0.8 %copy-start.5 = (bf16[8,4,480]{2,1,0:T(4,128)(2,1)S(1)}, bf16[8,4,480]{2,1,0:T(4,128)(2,1)}, u32[]{:S(2)}) copy-start(bf16[8,4,480]{2,1,0:T(4,128)(2,1)} %vectors.1) | copy-start | bytes 92164
  2.3 0.7 %copy-start.8 = (f32[8,256]{1,0:T(8,128)S(1)}, f32[8,256]{1,0:T(8,128)}, u32[]{:S(2)}) copy-start(f32[8,256]{1,0:T(8,128)} %angle.1) | copy-start | bytes 24580
  3.0 0.7 %copy-start.9 = (s32[8]{0:T(128)S(1)}, s32[8]{0:T(128)}, u32[]{:S(2)}) copy-start(s32[8]{0:T(128)} %box.5) | copy-start | bytes 100
  3.7 29.1 %copy-start.4 = (f32[8,2,240]{2,1,0:T(2,128)S(1)}, f32[8,2,240]{2,1,0:T(2,128)}, u32[]{:S(2)}) copy-start(f32[8,2,240]{2,1,0:T(2,128)} %tmatrix.3) | copy-start | bytes 46084
  3.7 29.1 %copy-start.6 = (s32[8,16]{1,0:T(8,128)S(1)}, s32[8,16]{1,0:T(8,128)}, u32[]{:S(2)}) copy-start(s32[8,16]{1,0:T(8,128)} %list_mine.3) | copy-start | bytes 1540
  4.3 6.7 %collective-permute-start.2 = (bf16[16,1536]{1,0:T(8,128)(2,1)S(1)}, bf16[16,1536]{1,0:T(8,128)(2,1)S(1)}, u32[]{:S(2)}, u32[]{:S(2)}) collective-permute-start(bf16[16,1536]{1,0:T(8,128)(2,1)S(1)} %get-tuple-element.29.p0.refs_0_.refs_5_.current), channel_id=1, source_target_pairs={{0,6},{2,4},{4,2},{6,0},{8,14},{10,12},{12,10},{14,8},{16,22},{18,... | collective-permute-start | bytes 147464 | tf_op jit(solution)/shard_map/ppermute | solution.py:21
  8.3 4.1 %collective-permute-start.1 = (bf16[16,1536]{1,0:T(8,128)(2,1)S(1)}, bf16[16,1536]{1,0:T(8,128)(2,1)S(1)}, u32[]{:S(2)}, u32[]{:S(2)}) collective-permute-start(bf16[16,1536]{1,0:T(8,128)(2,1)S(1)} %get-tuple-element.29.p0.refs_0_.refs_5_.current), channel_id=1, source_target_pairs={{0,4},{2,6},{4,0},{6,2},{8,12},{10,14},{12,8},{14,10},{16,20},{18,... | collective-permute-start | bytes 147464 | tf_op jit(solution)/shard_map/ppermute | solution.py:21
  8.8 4.1 %collective-permute-start = (bf16[16,1536]{1,0:T(8,128)(2,1)S(1)}, bf16[16,1536]{1,0:T(8,128)(2,1)S(1)}, u32[]{:S(2)}, u32[]{:S(2)}) collective-permute-start(bf16[16,1536]{1,0:T(8,128)(2,1)S(1)} %get-tuple-element.29.p0.refs_0_.refs_5_.current), channel_id=1, source_target_pairs={{0,2},{2,0},{4,6},{6,4},{8,10},{10,8},{12,14},{14,12},{16,18},{18,... | collective-permute-start | bytes 147464 | tf_op jit(solution)/shard_map/ppermute | solution.py:21
  9.0 2.1 %collective-permute-start.3 = (bf16[16,1024]{1,0:T(8,128)(2,1)S(1)}, bf16[16,1024]{1,0:T(8,128)(2,1)S(1)}, u32[]{:S(2)}, u32[]{:S(2)}) collective-permute-start(bf16[16,1024]{1,0:T(8,128)(2,1)S(1)} %get-tuple-element.27), channel_id=1, source_target_pairs={{6,8},{8,6},{14,16},{16,14},{22,24},{24,22},{7,9},{9,7},{15,17},{1... | collective-permute-start | bytes 98312 | tf_op jit(solution)/shard_map/ppermute | solution.py:51
  9.6 1.4 %collective-permute-start.4 = (s32[8,16]{1,0:T(8,128)}, s32[8,16]{1,0:T(8,128)S(1)}, u32[]{:S(2)}, u32[]{:S(2)}) collective-permute-start(s32[8,16]{1,0:T(8,128)} %list_mine.3), channel_id=1, source_target_pairs={{0,1},{1,0},{2,3},{3,2},{4,5},{5,4},{6,7},{7,6},{8,9},{9,8},{10,11... | collective-permute-start | bytes 1544 | tf_op jit(solution)/shard_map/ppermute | solution.py:495
  12.9 1.0 %copy-start = (bf16[480,512]{1,0:T(8,128)(2,1)S(1)}, bf16[480,512]{1,0:T(8,128)(2,1)}, u32[]{:S(2)}) copy-start(bf16[480,512]{1,0:T(8,128)(2,1)} %agg.3) | copy-start | bytes 1474564
  13.9 18.9 %copy-start.2 = (bf16[512,480]{0,1:T(8,128)(2,1)S(1)}, bf16[512,480]{0,1:T(8,128)(2,1)}, u32[]{:S(2)}) copy-start(bf16[512,480]{0,1:T(8,128)(2,1)} %param.21) | copy-start | bytes 1474564
  13.9 29.7 %copy-start.1 = (bf16[480,512]{1,0:T(8,128)(2,1)S(1)}, bf16[480,512]{1,0:T(8,128)(2,1)}, u32[]{:S(2)}) copy-start(bf16[480,512]{1,0:T(8,128)(2,1)} %agg.3) | copy-start | bytes 1474564
  14.9 16.3 %collective-permute-start.7 = (bf16[32,1024]{1,0:T(8,128)(2,1)S(1)}, bf16[32,1024]{1,0:T(8,128)(2,1)S(1)}, u32[]{:S(2)}, u32[]{:S(2)}) collective-permute-start(bf16[32,1024]{1,0:T(8,128)(2,1)S(1)} %get-tuple-element.36.z0), channel_id=1, source_target_pairs={{0,24},{2,26},{4,28},{6,30},{8,16},{10,18},{12,20},{14,22},{16,8},... | collective-permute-start | bytes 196616 | tf_op jit(solution)/shard_map/ppermute | solution.py:21
  22.5 8.7 %collective-permute-start.6 = (bf16[32,1024]{1,0:T(8,128)(2,1)S(1)}, bf16[32,1024]{1,0:T(8,128)(2,1)S(1)}, u32[]{:S(2)}, u32[]{:S(2)}) collective-permute-start(bf16[32,1024]{1,0:T(8,128)(2,1)S(1)} %get-tuple-element.36.z0), channel_id=1, source_target_pairs={{0,16},{2,18},{4,20},{6,22},{8,24},{10,26},{12,28},{14,30},{16,0},... | collective-permute-start | bytes 196616 | tf_op jit(solution)/shard_map/ppermute | solution.py:21
  22.5 8.7 %collective-permute-start.5 = (bf16[32,1024]{1,0:T(8,128)(2,1)S(1)}, bf16[32,1024]{1,0:T(8,128)(2,1)S(1)}, u32[]{:S(2)}, u32[]{:S(2)}) collective-permute-start(bf16[32,1024]{1,0:T(8,128)(2,1)S(1)} %get-tuple-element.36.z0), channel_id=1, source_target_pairs={{0,8},{2,10},{4,12},{6,14},{8,0},{10,2},{12,4},{14,6},{16,24},{18,... | collective-permute-start | bytes 196616 | tf_op jit(solution)/shard_map/ppermute | solution.py:21
  23.1 0.7 %copy-start.7 = (s32[8,8]{1,0:T(8,128)S(1)}, s32[8,8]{1,0:T(8,128)}, u32[]{:S(2)}) copy-start(s32[8,8]{1,0:T(8,128)} %neighbours.3) | copy-start | bytes 772
  23.8 0.7 %copy-start.11 = (s32[8]{0:T(128)S(1)}, s32[8]{0:T(128)}, u32[]{:S(2)}) copy-start(s32[8]{0:T(128)} %live.3) | copy-start | bytes 100
  31.3 1.5 %collective-permute-start.8 = (bf16[256,256]{1,0:T(8,128)(2,1)S(1)}, bf16[256,256]{1,0:T(8,128)(2,1)S(1)}, u32[]{:S(2)}, u32[]{:S(2)}) collective-permute-start(bf16[256,256]{1,0:T(8,128)(2,1)S(1)} %shard_map.125.table_mine), channel_id=1, source_target_pairs={{0,1},{1,0},{2,3},{3,2},{4,5},{5,4},{6,7},{7,6},{8,9},{9,8},{10,11... | collective-permute-start | bytes 393224 | tf_op jit(solution)/shard_map/ppermute | solution.py:495
  31.4 1.4 %collective-permute-start.9 = (f32[16,480]{1,0:T(8,128)S(1)}, f32[16,480]{1,0:T(8,128)S(1)}, u32[]{:S(2)}, u32[]{:S(2)}) collective-permute-start(f32[16,480]{1,0:T(8,128)S(1)} %get-tuple-element.42), channel_id=1, source_target_pairs={{0,1},{1,0},{2,3},{3,2},{4,5},{5,4},{6,7},{7,6},{8,9},{9,8},{10,11... | collective-permute-start | bytes 92168 | tf_op jit(solution)/shard_map/ppermute | solution.py:495
  34.1 6.5 %collective-permute-start.13 = (bf16[16,480]{1,0:T(8,128)(2,1)S(1)}, bf16[16,480]{1,0:T(8,128)(2,1)S(1)}, u32[]{:S(2)}, u32[]{:S(2)}) collective-permute-start(bf16[16,480]{1,0:T(8,128)(2,1)S(1)} %shard_map.126.p0.refs_0_.current), channel_id=1, source_target_pairs={{6,8},{8,6},{14,16},{16,14},{22,24},{24,22},{7,9},{9,7},{15,17},{1... | collective-permute-start | bytes 46088 | tf_op jit(solution)/shard_map/ppermute | solution.py:51
  34.8 6.9 %collective-permute-start.12 = (bf16[16,480]{1,0:T(8,128)(2,1)S(1)}, bf16[16,480]{1,0:T(8,128)(2,1)S(1)}, u32[]{:S(2)}, u32[]{:S(2)}) collective-permute-start(bf16[16,480]{1,0:T(8,128)(2,1)S(1)} %shard_map.126.p0.refs_0_.current), channel_id=1, source_target_pairs={{0,6},{2,4},{4,2},{6,0},{8,14},{10,12},{12,10},{14,8},{16,22},{18,... | collective-permute-start | bytes 46088 | tf_op jit(solution)/shard_map/ppermute | solution.py:21
  39.9 3.7 %collective-permute-start.11 = (bf16[16,480]{1,0:T(8,128)(2,1)S(1)}, bf16[16,480]{1,0:T(8,128)(2,1)S(1)}, u32[]{:S(2)}, u32[]{:S(2)}) collective-permute-start(bf16[16,480]{1,0:T(8,128)(2,1)S(1)} %shard_map.126.p0.refs_0_.current), channel_id=1, source_target_pairs={{0,4},{2,6},{4,0},{6,2},{8,12},{10,14},{12,8},{14,10},{16,20},{18,... | collective-permute-start | bytes 46088 | tf_op jit(solution)/shard_map/ppermute | solution.py:21
  39.9 3.7 %collective-permute-start.10 = (bf16[16,480]{1,0:T(8,128)(2,1)S(1)}, bf16[16,480]{1,0:T(8,128)(2,1)S(1)}, u32[]{:S(2)}, u32[]{:S(2)}) collective-permute-start(bf16[16,480]{1,0:T(8,128)(2,1)S(1)} %shard_map.126.p0.refs_0_.current), channel_id=1, source_target_pairs={{0,2},{2,0},{4,6},{6,4},{8,10},{10,8},{12,14},{14,12},{16,18},{18,... | collective-permute-start | bytes 46088 | tf_op jit(solution)/shard_map/ppermute | solution.py:21
  44.0 4.5 %collective-permute-start.14 = (bf16[80,480]{1,0:T(8,128)(2,1)S(1)}, bf16[80,480]{1,0:T(8,128)(2,1)S(1)}, u32[]{:S(2)}, u32[]{:S(2)}) collective-permute-start(bf16[80,480]{1,0:T(8,128)(2,1)S(1)} %get-tuple-element.44), channel_id=1, source_target_pairs={{0,1},{1,0},{2,3},{3,2},{4,5},{5,4},{6,7},{7,6},{8,9},{9,8},{10,11... | collective-permute-start | bytes 230408 | tf_op jit(solution)/shard_map/ppermute | solution.py:495
  44.0 8.1 %collective-permute-start.17 = (bf16[32,512]{1,0:T(8,128)(2,1)S(1)}, bf16[32,512]{1,0:T(8,128)(2,1)S(1)}, u32[]{:S(2)}, u32[]{:S(2)}) collective-permute-start(bf16[32,512]{1,0:T(8,128)(2,1)S(1)} %get-tuple-element.47.z0), channel_id=1, source_target_pairs={{0,24},{2,26},{4,28},{6,30},{8,16},{10,18},{12,20},{14,22},{16,8},... | collective-permute-start | bytes 98312 | tf_op jit(solution)/shard_map/ppermute | solution.py:21
  47.0 5.1 %collective-permute-start.16 = (bf16[32,512]{1,0:T(8,128)(2,1)S(1)}, bf16[32,512]{1,0:T(8,128)(2,1)S(1)}, u32[]{:S(2)}, u32[]{:S(2)}) collective-permute-start(bf16[32,512]{1,0:T(8,128)(2,1)S(1)} %get-tuple-element.47.z0), channel_id=1, source_target_pairs={{0,16},{2,18},{4,20},{6,22},{8,24},{10,26},{12,28},{14,30},{16,0},... | collective-permute-start | bytes 98312 | tf_op jit(solution)/shard_map/ppermute | solution.py:21
  47.4 4.8 %collective-permute-start.15 = (bf16[32,512]{1,0:T(8,128)(2,1)S(1)}, bf16[32,512]{1,0:T(8,128)(2,1)S(1)}, u32[]{:S(2)}, u32[]{:S(2)}) collective-permute-start(bf16[32,512]{1,0:T(8,128)(2,1)S(1)} %get-tuple-element.47.z0), channel_id=1, source_target_pairs={{0,8},{2,10},{4,12},{6,14},{8,0},{10,2},{12,4},{14,6},{16,24},{18,... | collective-permute-start | bytes 98312 | tf_op jit(solution)/shard_map/ppermute | solution.py:21
  52.1 1.2 %collective-permute-start.18 = (f32[16,480]{1,0:T(8,128)S(1)}, f32[16,480]{1,0:T(8,128)S(1)}, u32[]{:S(2)}, u32[]{:S(2)}) collective-permute-start(f32[16,480]{1,0:T(8,128)S(1)} %get-tuple-element.49), channel_id=1, source_target_pairs={{0,1},{1,0},{2,3},{3,2},{4,5},{5,4},{6,7},{7,6},{8,9},{9,8},{10,11... | collective-permute-start | bytes 92168 | tf_op jit(solution)/shard_map/ppermute | solution.py:495
  54.5 1.2 %collective-permute-start.19 = (bf16[16,480]{1,0:T(8,128)(2,1)S(1)}, bf16[16,480]{1,0:T(8,128)(2,1)S(1)}, u32[]{:S(2)}, u32[]{:S(2)}) collective-permute-start(bf16[16,480]{1,0:T(8,128)(2,1)S(1)} %shard_map.129.mine), channel_id=1, source_target_pairs={{0,1},{1,0},{2,3},{3,2},{4,5},{5,4},{6,7},{7,6},{8,9},{9,8},{10,11... | collective-permute-start | bytes 46088 | tf_op jit(solution)/shard_map/ppermute | solution.py:495

commit v4 on v3

--- a/solution.py
+++ b/solution.py
@@ -88,7 +88,6 @@
     coeffs = width // 2
     slots = neighbours.shape[1]
     far_count = lax.axis_size("far")
-    near_count = lax.axis_size("near")
     own_boxes, listed = far_list.shape
     boxes = own_boxes * far_count
     waves = agg_matrix.shape[1] // 2
@@ -105,7 +104,6 @@
     rounded = lax.reduce_precision(agg_angle, 8, 7)
     hi, low = rounded.astype(BF16), (agg_angle - rounded).astype(BF16)
     factors = far_factors.astype(BF16).reshape(-1, far_factors.shape[-1]).T
-    per_part = factors.size
     lists = over_far_lists(far_list)
     extra = jnp.concatenate(
         [
@@ -127,7 +125,6 @@
     state = {}
     images = []
     current = own_share(vectors)
-    whole = vectors
     for step in range(2):
         flat = current.reshape(rows, width)
         edge = edge_rows(current)
@@ -220,12 +217,14 @@
 
 VM = pl.BlockSpec(memory_space=pltpu.VMEM)
 SM = pl.BlockSpec(memory_space=pltpu.SMEM)
-
-
-def call(kernel, outs, specs, args, scratch=(), flops=0, moved=6 << 20, limit=4 << 20):
+HB = pl.BlockSpec(memory_space=pl.ANY)
+
+
+def call(kernel, outs, specs, args, scratch=(), flops=0, moved=6 << 20, limit=4 << 20, held=False):
+    make = pltpu.VMEM if held else jax.ShapeDtypeStruct
     return pl.pallas_call(
         kernel,
-        out_shape=tuple(jax.ShapeDtypeStruct(shape, kind) for shape, kind in outs),
+        out_shape=tuple(make(shape, kind) for shape, kind in outs),
         in_specs=list(specs),
         out_specs=(VM,) * len(outs),
         scratch_shapes=list(scratch),
@@ -239,7 +238,8 @@
     return lax.axis_index("far"), near_pos % 4, near_pos // 4, near_pos
 
 
-def pack_kernel(box, vectors, angle, factors, out, edge):
+def pack_kernel(box, vectors, angle, factors, *refs):
+    out, edge = refs[-2:]
     place = here()
     spheres, newton, width = vectors.shape
     share = newton // 2
@@ -409,7 +409,7 @@
     return pl.pallas_call(
         functools.partial(near_kernel, starts, emit),
         out_shape=tuple(outs),
-        in_specs=[SM] * 2 + full + [VM if emit else pl.BlockSpec(memory_space=pl.ANY)],
+        in_specs=[SM] * 2 + full + [VM if emit else HB],
         out_specs=(VM,) * len(outs),
         scratch_shapes=[pltpu.VMEM((5 * spheres, 8, coeffs), F32)]
         + ([] if emit else [pltpu.SemaphoreType.DMA((spheres,))]),
@@ -422,16 +422,15 @@
     )(neighbours, live, *mine, *theirs, blocks)
 
 
-def finish_kernel(
-    box, list_mine, list_theirs, z0, z1, z2, z3, table_mine, table_theirs, turn, dis,
-    near_mine, near_got, tmatrix, current, out, source, factor, field, local
+def far_kernel(
+    box, list_mine, list_theirs, z0, z1, z2, z3, table_mine, table_theirs, turn, dis, out,
+    source, factor, field, local
 ):
     place = here()
     own_boxes, listed = list_mine.shape
     boxes = 2 * own_boxes
     waves = source.shape[2]
-    spheres = tmatrix.shape[0]
-    coeffs = tmatrix.shape[2]
+    spheres = local.shape[1]
     first = place[0] == 0
     total = jnp.zeros((2 * boxes, 2 * waves), F32)
     for part in (z0, z1, z2, z3):
@@ -471,8 +470,12 @@
     sine = turn[pl.ds(0, 2 * spheres), pl.ds(waves, waves)]
     shifted = jnp.concatenate([re * cosine + im * sine, im * cosine - re * sine], axis=1)
     dims = (((1,), (1,)), ((), ()))
-    total = lax.dot_general(shifted.astype(BF16), dis[...], dims, preferred_element_type=F32)
-    total += near_mine[...] + near_got[...]
+    out[...] = lax.dot_general(shifted.astype(BF16), dis[...], dims, preferred_element_type=F32)
+
+
+def scatter_kernel(far, near_mine, near_got, tmatrix, current, out):
+    coeffs = tmatrix.shape[2]
+    total = far[...] + (near_mine[...] + near_got[...])
     t_re = jnp.concatenate([tmatrix[:, 0], tmatrix[:, 0]], axis=0)
     t_im = jnp.concatenate([tmatrix[:, 1], tmatrix[:, 1]], axis=0)
     f_re, f_im = total[:, :coeffs], total[:, coeffs:]
@@ -500,24 +503,27 @@
     far_list, far_factors, dis_matrix
 ):
     spheres, newton, width = vectors.shape
-    coeffs = width // 2
     own_boxes, listed = far_list.shape
     boxes = 2 * own_boxes
     waves = agg_matrix.shape[1] // 2
     rows = spheres * newton // 2
     entries = own_boxes * listed * 2
+    later = (near_blocks, agg_matrix, neighbours, live_counts)
     message, edge = call(
         pack_kernel,
         [((rows, 1024 + waves + entries), BF16), ((rows, 1024), BF16)],
-        [SM, VM, VM, VM],
-        (sphere_box, vectors, agg_angle, far_factors.reshape(entries, -1)),
+        [SM, VM, VM, VM] + [HB] * 4,
+        (sphere_box, vectors, agg_angle, far_factors.reshape(entries, -1), *later),
+        limit=60 << 20,
+        held=True,
     )
     list_theirs = swap_far(far_list)
-    current, edge = message, edge_rows(edge)
+    current = message
     table = None
     for step in range(2):
         if step == 0:
             parts = xor_gather(message, (1, 2, 3))
+            edge = edge_rows(edge)
             parts, edge, list_theirs = lax.optimization_barrier((parts, edge, list_theirs))
             block, turn, member, _ = call(
                 functools.partial(first_waves_kernel, boxes),
@@ -531,8 +537,10 @@
                 (*parts, agg_matrix),
             )
         else:
+            parts = [current]
+            for mask in (1, 2, 3):
+                parts.append(swap_near(current, mask))
             edge = edge_rows(current)
-            parts = xor_gather(current, (1, 2, 3))
             block, around = call(
                 next_waves_kernel,
                 [((2 * boxes, 2 * waves), BF16), ((5 * rows, width), BF16)],
@@ -561,13 +569,12 @@
                 [pltpu.VMEM((waves, entries), F32)],
             )[0]
             table = (table, swap_far(table))
-        current = call(
-            finish_kernel,
-            [((rows, width), BF16)],
-            [SM] * 3 + [VM] * 12,
+        far_field = call(
+            far_kernel,
+            [((rows, width), F32)],
+            [SM] * 3 + [VM] * 8,
             (
-                sphere_box, far_list, list_theirs, *pieces, *table, turn, dis_matrix.T,
-                near_mine, near_got, tmatrix, current
+                sphere_box, far_list, list_theirs, *pieces, *table, turn, dis_matrix.T
             ),
             [
                 pltpu.VMEM((boxes, 8, waves), F32),
@@ -575,6 +582,12 @@
                 pltpu.VMEM((boxes, 4, waves), F32),
                 pltpu.VMEM((4, spheres, waves), F32),
             ],
+        )[0]
+        current = call(
+            scatter_kernel,
+            [((rows, width), BF16)],
+            [VM] * 5,
+            (far_field, near_mine, near_got, tmatrix, current),
         )[0]
     second_image = call(
         join_kernel,

time: 56.8 us -> 50.6 us (0.89)
  local copies, waits for them, and re-layouts: 5.4 us -> 0.03 us
  waiting for transfers between devices: 9.43 us -> 8.11 us
    unnamed x24 -> x14, local copies, waits for them, and re-layouts: 5.4 us -> 0.03 us
    ppermute x6, waiting for transfers between devices: 4.41 us -> 2.88 us  [swap_far(): return lax.ppermute(block, 'far', [(0, 1), (1, 0)])]
    pallas_call x7 -> x9, Pallas kernels: 5.17 us -> 5.63 us  [call(): pl.pallas_call(kernel, out_shape=tuple((make(shape, kind) for shape, kind...]
  transfers between devices with their start and end apart: 20 -> 20, of which waited for: 9 -> 8; matrix products, arithmetic and copies ran while one was open for 0% -> 0% of each run, Pallas kernels for 18% -> 25%
where the time goes in v4:
time: 50.6 us; the launch traced here: 50.4 us
  starting transfers between devices  25.5 us (50%)
  Pallas kernels  16 us (32%)
  waiting for transfers between devices  8.11 us (16%)
  between operations  0.83 us (2%)
    ppermute x12, starting transfers between devices, swap_near(): return lax.ppermute(block, 'near', [(i, i ^ mask) for i in range(count)])  23.1 us
    pallas_call x2, Pallas kernels, near_call(): pl.pallas_call(functools.partial(near_kernel, starts, emit), out_shape=tu...  10.4 us
    pallas_call x9, Pallas kernels, call(): pl.pallas_call(kernel, out_shape=tuple((make(shape, kind) for shape, kind...  5.63 us
    ppermute x12, waiting for transfers between devices, swap_near(): return lax.ppermute(block, 'near', [(i, i ^ mask) for i in range(count)])  5.22 us
    ppermute x6, waiting for transfers between devices, swap_far(): return lax.ppermute(block, 'far', [(0, 1), (1, 0)])  2.88 us
    ppermute x2, starting transfers between devices, edge_rows(): lax.ppermute(block, 'near', pairs)  1.31 us
    ppermute x6, starting transfers between devices, swap_far(): return lax.ppermute(block, 'far', [(0, 1), (1, 0)])  1.09 us
  transfers between devices with their start and end apart: 20, of which 8 were waited for; matrix products, arithmetic and copies ran while one was open for 0% of the time, Pallas kernels for 25%

profile of v4, /device:TPU:0, one launch (start us, length us, event | category | flops | bytes accessed | tf_op | source)
XLA Modules:
  0.0 50.4 jit_solution(18277188242642741208)
XLA Ops:
  0.7 1.1 %shard_map.122 = (bf16[16,1536]{1,0:T(8,128)(2,1)S(1)}, bf16[16,1024]{1,0:T(8,128)(2,1)S(1)}) custom-call(s32[8]{0:T(128)} %box.5, bf16[8,4,480]{2,1,0:T(4,128)(2,1)} %vectors.1, f32[8,256]{1,0:T(8,128)} %angle.1, f32[256,16]{1,0:T(8,128)} %bitcast.4, bf16[8,8,2,240,240]{4,3,2,1,0:T(8,128)(2,1)} %refs_10_.1, bf16[480,512]{1,0:T(8,128)(2,1)} %agg.3, ...), custom_call_target="tpu_custom_call" | custom-call | bytes 6291456 | tf_op jit(solution)/shard_map/pallas_call | solution.py:225
  1.8 4.0 %collective-permute-start.2 = (bf16[16,1536]{1,0:T(8,128)(2,1)S(1)}, bf16[16,1536]{1,0:T(8,128)(2,1)S(1)}, u32[]{:S(2)}, u32[]{:S(2)}) collective-permute-start(bf16[16,1536]{1,0:T(8,128)(2,1)S(1)} %get-tuple-element.29.p0.refs_0_.refs_5_.current), channel_id=1, source_target_pairs={{0,6},{2,4},{4,2},{6,0},{8,14},{10,12},{12,10},{14,8},{16,22},{18,... | collective-permute-start | bytes 147464 | tf_op jit(solution)/shard_map/ppermute | solution.py:21
  5.8 0.5 %collective-permute-start.1 = (bf16[16,1536]{1,0:T(8,128)(2,1)S(1)}, bf16[16,1536]{1,0:T(8,128)(2,1)S(1)}, u32[]{:S(2)}, u32[]{:S(2)}) collective-permute-start(bf16[16,1536]{1,0:T(8,128)(2,1)S(1)} %get-tuple-element.29.p0.refs_0_.refs_5_.current), channel_id=1, source_target_pairs={{0,4},{2,6},{4,0},{6,2},{8,12},{10,14},{12,8},{14,10},{16,20},{18,... | collective-permute-start | bytes 147464 | tf_op jit(solution)/shard_map/ppermute | solution.py:21
  6.3 0.1 collective-permute-start
  6.5 0.7 %collective-permute-start.3 = (bf16[16,1024]{1,0:T(8,128)(2,1)S(1)}, bf16[16,1024]{1,0:T(8,128)(2,1)S(1)}, u32[]{:S(2)}, u32[]{:S(2)}) collective-permute-start(bf16[16,1024]{1,0:T(8,128)(2,1)S(1)} %get-tuple-element.27), channel_id=1, source_target_pairs={{6,8},{8,6},{14,16},{16,14},{22,24},{24,22},{7,9},{9,7},{15,17},{1... | collective-permute-start | bytes 98312 | tf_op jit(solution)/shard_map/ppermute | solution.py:51
  7.2 1.2 %collective-permute-done.4.list_theirs = s32[8,16]{1,0:T(8,128)S(1)} collective-permute-done((s32[8,16]{1,0:T(8,128)S(1)}, s32[8,16]{1,0:T(8,128)S(1)}, u32[]{:S(2)}, u32[]{:S(2)}) %collective-permute-start.4) | collective-permute-done | bytes 544 | tf_op jit(solution)/shard_map/ppermute | solution.py:498
  8.4 1.5 %collective-permute-done.1.p2.refs_2_.refs_7_ = bf16[16,1536]{1,0:T(8,128)(2,1)S(1)} collective-permute-done((bf16[16,1536]{1,0:T(8,128)(2,1)S(1)}, bf16[16,1536]{1,0:T(8,128)(2,1)S(1)}, u32[]{:S(2)}, u32[]{:S(2)}) %collective-permute-start.1) | collective-permute-done | bytes 49184 | tf_op jit(solution)/shard_map/ppermute | solution.py:21
  9.9 0.5 %collective-permute-done.p1.refs_1_.refs_6_ = bf16[16,1536]{1,0:T(8,128)(2,1)S(1)} collective-permute-done((bf16[16,1536]{1,0:T(8,128)(2,1)S(1)}, bf16[16,1536]{1,0:T(8,128)(2,1)S(1)}, u32[]{:S(2)}, u32[]{:S(2)}) %collective-permute-start) | collective-permute-done | bytes 49184 | tf_op jit(solution)/shard_map/ppermute | solution.py:21
  10.4 0.9 %shard_map.123 = (bf16[32,1024]{1,0:T(8,128)(2,1)S(1)}, f32[64,512]{1,0:T(8,128)S(1)}, bf16[64,32]{1,0:T(8,128)(2,1)S(1)}, f32[64,256]{1,0:T(8,128)}) custom-call(bf16[16,1536]{1,0:T(8,128)(2,1)S(1)} %get-tuple-element.29.p0.refs_0_.refs_5_.current, bf16[16,1536]{1,0:T(8,128)(2,1)S(1)} %collective-permute-done.p1.refs_1_.refs_6_, ...), custom_call_target="tpu_custom_call" | custom-call | bytes 6291456 | tf_op jit(solution)/shard_map/pallas_call | solution.py:225
  11.3 7.7 %collective-permute-start.7 = (bf16[32,1024]{1,0:T(8,128)(2,1)S(1)}, bf16[32,1024]{1,0:T(8,128)(2,1)S(1)}, u32[]{:S(2)}, u32[]{:S(2)}) collective-permute-start(bf16[32,1024]{1,0:T(8,128)(2,1)S(1)} %get-tuple-element.36.z0), channel_id=1, source_target_pairs={{0,24},{2,26},{4,28},{6,30},{8,16},{10,18},{12,20},{14,22},{16,8},... | collective-permute-start | bytes 196616 | tf_op jit(solution)/shard_map/ppermute | solution.py:21
  19.0 0.6 %collective-permute-start.5 = (bf16[32,1024]{1,0:T(8,128)(2,1)S(1)}, bf16[32,1024]{1,0:T(8,128)(2,1)S(1)}, u32[]{:S(2)}, u32[]{:S(2)}) collective-permute-start(bf16[32,1024]{1,0:T(8,128)(2,1)S(1)} %get-tuple-element.36.z0), channel_id=1, source_target_pairs={{0,8},{2,10},{4,12},{6,14},{8,0},{10,2},{12,4},{14,6},{16,24},{18,... | collective-permute-start | bytes 196616 | tf_op jit(solution)/shard_map/ppermute | solution.py:21
  19.6 6.7 %shard_map.124 = (f32[16,480]{1,0:T(8,128)S(1)}, f32[16,480]{1,0:T(8,128)S(1)}, bf16[8,8,2,240,240]{4,3,2,1,0:T(8,128)(2,1)S(1)}) custom-call(s32[8,8]{1,0:T(8,128)S(1)} %copy-done.3, s32[8]{0:T(128)S(1)} %copy-done.5, bf16[16,1536]{1,0:T(8,128)(2,1)S(1)} %get-tuple-element.29.p0.refs_0_.refs_5_.current, ...), custom_call_target="tpu_custom_call" | custom-call | flops 117964800 | bytes 14745600 | tf_op jit(solution)/shard_map/pallas_call | solution.py:409
  26.3 0.1 shard_map.125.table_mine
  26.6 0.5 collective-permute-start.9
  27.1 0.8 %collective-permute-done.8.table_theirs = bf16[256,256]{1,0:T(8,128)(2,1)S(1)} collective-permute-done((bf16[256,256]{1,0:T(8,128)(2,1)S(1)}, bf16[256,256]{1,0:T(8,128)(2,1)S(1)}, u32[]{:S(2)}, u32[]{:S(2)}) %collective-permute-start.8) | collective-permute-done | bytes 131104 | tf_op jit(solution)/shard_map/ppermute | solution.py:498
  27.9 1.1 %shard_map.126.far = f32[16,480]{1,0:T(8,128)S(1)} custom-call(s32[8]{0:T(128)S(1)} %copy-done.6, s32[8,16]{1,0:T(8,128)S(1)} %copy-done.4, s32[8,16]{1,0:T(8,128)S(1)} %collective-permute-done.4.list_theirs, bf16[32,1024]{1,0:T(8,128)(2,1)S(1)} %get-tuple-element.36.z0, bf16[32,1024]{1,0:T(8,128)(2,1)S(1)} %collective-permute-done.5.z1, ...), custom_call_target="tpu_custom_call" | custom-call | bytes 6291456 | tf_op jit(solution)/shard_map/pallas_call | solution.py:225
  29.0 0.2 shard_map.127.p0.refs_0_.current
  29.2 0.7 %collective-permute-start.13 = (bf16[16,480]{1,0:T(8,128)(2,1)S(1)}, bf16[16,480]{1,0:T(8,128)(2,1)S(1)}, u32[]{:S(2)}, u32[]{:S(2)}) collective-permute-start(bf16[16,480]{1,0:T(8,128)(2,1)S(1)} %shard_map.127.p0.refs_0_.current), channel_id=1, source_target_pairs={{6,8},{8,6},{14,16},{16,14},{22,24},{24,22},{7,9},{9,7},{15,17},{1... | collective-permute-start | bytes 46088 | tf_op jit(solution)/shard_map/ppermute | solution.py:51
  29.8 5.1 %collective-permute-start.12 = (bf16[16,480]{1,0:T(8,128)(2,1)S(1)}, bf16[16,480]{1,0:T(8,128)(2,1)S(1)}, u32[]{:S(2)}, u32[]{:S(2)}) collective-permute-start(bf16[16,480]{1,0:T(8,128)(2,1)S(1)} %shard_map.127.p0.refs_0_.current), channel_id=1, source_target_pairs={{0,6},{2,4},{4,2},{6,0},{8,14},{10,12},{12,10},{14,8},{16,22},{18,... | collective-permute-start | bytes 46088 | tf_op jit(solution)/shard_map/ppermute | solution.py:21
  35.0 0.6 %collective-permute-start.10 = (bf16[16,480]{1,0:T(8,128)(2,1)S(1)}, bf16[16,480]{1,0:T(8,128)(2,1)S(1)}, u32[]{:S(2)}, u32[]{:S(2)}) collective-permute-start(bf16[16,480]{1,0:T(8,128)(2,1)S(1)} %shard_map.127.p0.refs_0_.current), channel_id=1, source_target_pairs={{0,2},{2,0},{4,6},{6,4},{8,10},{10,8},{12,14},{14,12},{16,18},{18,... | collective-permute-start | bytes 46088 | tf_op jit(solution)/shard_map/ppermute | solution.py:21
  35.6 1.1 %collective-permute-done.12.p3.refs_3_ = bf16[16,480]{1,0:T(8,128)(2,1)S(1)} collective-permute-done((bf16[16,480]{1,0:T(8,128)(2,1)S(1)}, bf16[16,480]{1,0:T(8,128)(2,1)S(1)}, u32[]{:S(2)}, u32[]{:S(2)}) %collective-permute-start.12) | collective-permute-done | bytes 15392 | tf_op jit(solution)/shard_map/ppermute | solution.py:21
  36.7 2.0 %collective-permute-done.11.p2.refs_2_ = bf16[16,480]{1,0:T(8,128)(2,1)S(1)} collective-permute-done((bf16[16,480]{1,0:T(8,128)(2,1)S(1)}, bf16[16,480]{1,0:T(8,128)(2,1)S(1)}, u32[]{:S(2)}, u32[]{:S(2)}) %collective-permute-start.11) | collective-permute-done | bytes 15392 | tf_op jit(solution)/shard_map/ppermute | solution.py:21
  38.7 0.3 shard_map.128
  39.1 3.1 %collective-permute-start.17 = (bf16[32,512]{1,0:T(8,128)(2,1)S(1)}, bf16[32,512]{1,0:T(8,128)(2,1)S(1)}, u32[]{:S(2)}, u32[]{:S(2)}) collective-permute-start(bf16[32,512]{1,0:T(8,128)(2,1)S(1)} %get-tuple-element.47.z0), channel_id=1, source_target_pairs={{0,24},{2,26},{4,28},{6,30},{8,16},{10,18},{12,20},{14,22},{16,8},... | collective-permute-start | bytes 98312 | tf_op jit(solution)/shard_map/ppermute | solution.py:21
  42.2 0.3 collective-permute-start.16
  42.5 1.0 %collective-permute-start.15 = (bf16[32,512]{1,0:T(8,128)(2,1)S(1)}, bf16[32,512]{1,0:T(8,128)(2,1)S(1)}, u32[]{:S(2)}, u32[]{:S(2)}) collective-permute-start(bf16[32,512]{1,0:T(8,128)(2,1)S(1)} %get-tuple-element.47.z0), channel_id=1, source_target_pairs={{0,8},{2,10},{4,12},{6,14},{8,0},{10,2},{12,4},{14,6},{16,24},{18,... | collective-permute-start | bytes 98312 | tf_op jit(solution)/shard_map/ppermute | solution.py:21
  43.5 3.6 %shard_map.129 = (f32[16,480]{1,0:T(8,128)S(1)}, f32[16,480]{1,0:T(8,128)S(1)}, bf16[8,4,480]{2,1,0:T(4,128)(2,1)}) custom-call(s32[8,8]{1,0:T(8,128)S(1)} %copy-done.3, s32[8]{0:T(128)S(1)} %copy-done.5, bf16[16,480]{1,0:T(8,128)(2,1)S(1)} %shard_map.127.p0.refs_0_.current, bf16[16,480]{1,0:T(8,128)(2,1)S(1)} %collective-permute-done.10.p1.refs_1_, ...), custom_call_target="tpu_custom_call" | custom-call | flops 117964800 | bytes 14745600 | tf_op jit(solution)/shard_map/pallas_call | solution.py:409
  47.2 1.1 %shard_map.130.far = f32[16,480]{1,0:T(8,128)S(1)} custom-call(s32[8]{0:T(128)S(1)} %copy-done.6, s32[8,16]{1,0:T(8,128)S(1)} %copy-done.4, s32[8,16]{1,0:T(8,128)S(1)} %collective-permute-done.4.list_theirs, bf16[32,512]{1,0:T(8,128)(2,1)S(1)} %get-tuple-element.47.z0, bf16[32,512]{1,0:T(8,128)(2,1)S(1)} %collective-permute-done.15.z1, ...), custom_call_target="tpu_custom_call" | custom-call | bytes 6291456 | tf_op jit(solution)/shard_map/pallas_call | solution.py:225
  48.4 0.1 shard_map.131.mine
  48.5 0.4 collective-permute-start.19
  49.0 0.8 %collective-permute-done.19.theirs = bf16[16,480]{1,0:T(8,128)(2,1)S(1)} collective-permute-done((bf16[16,480]{1,0:T(8,128)(2,1)S(1)}, bf16[16,480]{1,0:T(8,128)(2,1)S(1)}, u32[]{:S(2)}, u32[]{:S(2)}) %collective-permute-start.19) | collective-permute-done | bytes 15392 | tf_op jit(solution)/shard_map/ppermute | solution.py:498
  49.8 0.7 %shard_map.132 = bf16[8,4,480]{2,1,0:T(4,128)(2,1)} custom-call(bf16[16,480]{1,0:T(8,128)(2,1)S(1)} %shard_map.131.mine, bf16[16,480]{1,0:T(8,128)(2,1)S(1)} %collective-permute-done.19.theirs), custom_call_target="tpu_custom_call" | custom-call | bytes 6291456 | tf_op jit(solution)/shard_map/pallas_call | solution.py:225
  (33 shorter events, 0.3 us)
Async XLA Ops:
  0.6 9.8 %copy-start = (bf16[480,512]{1,0:T(8,128)(2,1)S(1)}, bf16[480,512]{1,0:T(8,128)(2,1)}, u32[]{:S(2)}) copy-start(bf16[480,512]{1,0:T(8,128)(2,1)} %agg.3) | copy-start | bytes 1474564
  0.6 18.9 %copy-start.5 = (s32[8]{0:T(128)S(1)}, s32[8]{0:T(128)}, u32[]{:S(2)}) copy-start(s32[8]{0:T(128)} %live.3) | copy-start | bytes 100
  0.7 18.9 %copy-start.3 = (s32[8,8]{1,0:T(8,128)S(1)}, s32[8,8]{1,0:T(8,128)}, u32[]{:S(2)}) copy-start(s32[8,8]{1,0:T(8,128)} %neighbours.3) | copy-start | bytes 772
  0.7 6.5 %copy-start.4 = (s32[8,16]{1,0:T(8,128)S(1)}, s32[8,16]{1,0:T(8,128)}, u32[]{:S(2)}) copy-start(s32[8,16]{1,0:T(8,128)} %list_mine.3) | copy-start | bytes 1540
  0.7 27.2 %copy-start.1 = (bf16[512,480]{0,1:T(8,128)(2,1)S(1)}, bf16[512,480]{0,1:T(8,128)(2,1)}, u32[]{:S(2)}) copy-start(bf16[512,480]{0,1:T(8,128)(2,1)} %param.21) | copy-start | bytes 1474564
  0.7 27.2 %copy-start.6 = (s32[8]{0:T(128)S(1)}, s32[8]{0:T(128)}, u32[]{:S(2)}) copy-start(s32[8]{0:T(128)} %box.5) | copy-start | bytes 100
  0.7 28.3 %copy-start.2 = (f32[8,2,240]{2,1,0:T(2,128)S(1)}, f32[8,2,240]{2,1,0:T(2,128)}, u32[]{:S(2)}) copy-start(f32[8,2,240]{2,1,0:T(2,128)} %tmatrix.3) | copy-start | bytes 46084
  1.8 6.5 %collective-permute-start.2 = (bf16[16,1536]{1,0:T(8,128)(2,1)S(1)}, bf16[16,1536]{1,0:T(8,128)(2,1)S(1)}, u32[]{:S(2)}, u32[]{:S(2)}) collective-permute-start(bf16[16,1536]{1,0:T(8,128)(2,1)S(1)} %get-tuple-element.29.p0.refs_0_.refs_5_.current), channel_id=1, source_target_pairs={{0,6},{2,4},{4,2},{6,0},{8,14},{10,12},{12,10},{14,8},{16,22},{18,... | collective-permute-start | bytes 147464 | tf_op jit(solution)/shard_map/ppermute | solution.py:21
  5.8 4.1 %collective-permute-start.1 = (bf16[16,1536]{1,0:T(8,128)(2,1)S(1)}, bf16[16,1536]{1,0:T(8,128)(2,1)S(1)}, u32[]{:S(2)}, u32[]{:S(2)}) collective-permute-start(bf16[16,1536]{1,0:T(8,128)(2,1)S(1)} %get-tuple-element.29.p0.refs_0_.refs_5_.current), channel_id=1, source_target_pairs={{0,4},{2,6},{4,0},{6,2},{8,12},{10,14},{12,8},{14,10},{16,20},{18,... | collective-permute-start | bytes 147464 | tf_op jit(solution)/shard_map/ppermute | solution.py:21
  6.3 4.1 %collective-permute-start = (bf16[16,1536]{1,0:T(8,128)(2,1)S(1)}, bf16[16,1536]{1,0:T(8,128)(2,1)S(1)}, u32[]{:S(2)}, u32[]{:S(2)}) collective-permute-start(bf16[16,1536]{1,0:T(8,128)(2,1)S(1)} %get-tuple-element.29.p0.refs_0_.refs_5_.current), channel_id=1, source_target_pairs={{0,2},{2,0},{4,6},{6,4},{8,10},{10,8},{12,14},{14,12},{16,18},{18,... | collective-permute-start | bytes 147464 | tf_op jit(solution)/shard_map/ppermute | solution.py:21
  6.5 1.9 %collective-permute-start.3 = (bf16[16,1024]{1,0:T(8,128)(2,1)S(1)}, bf16[16,1024]{1,0:T(8,128)(2,1)S(1)}, u32[]{:S(2)}, u32[]{:S(2)}) collective-permute-start(bf16[16,1024]{1,0:T(8,128)(2,1)S(1)} %get-tuple-element.27), channel_id=1, source_target_pairs={{6,8},{8,6},{14,16},{16,14},{22,24},{24,22},{7,9},{9,7},{15,17},{1... | collective-permute-start | bytes 98312 | tf_op jit(solution)/shard_map/ppermute | solution.py:51
  7.1 1.2 %collective-permute-start.4 = (s32[8,16]{1,0:T(8,128)S(1)}, s32[8,16]{1,0:T(8,128)S(1)}, u32[]{:S(2)}, u32[]{:S(2)}) collective-permute-start(s32[8,16]{1,0:T(8,128)S(1)} %copy-done.4), channel_id=1, source_target_pairs={{0,1},{1,0},{2,3},{3,2},{4,5},{5,4},{6,7},{7,6},{8,9},{9,8},{10,11... | collective-permute-start | bytes 1544 | tf_op jit(solution)/shard_map/ppermute | solution.py:498
  11.3 15.0 %collective-permute-start.7 = (bf16[32,1024]{1,0:T(8,128)(2,1)S(1)}, bf16[32,1024]{1,0:T(8,128)(2,1)S(1)}, u32[]{:S(2)}, u32[]{:S(2)}) collective-permute-start(bf16[32,1024]{1,0:T(8,128)(2,1)S(1)} %get-tuple-element.36.z0), channel_id=1, source_target_pairs={{0,24},{2,26},{4,28},{6,30},{8,16},{10,18},{12,20},{14,22},{16,8},... | collective-permute-start | bytes 196616 | tf_op jit(solution)/shard_map/ppermute | solution.py:21
  19.0 7.3 %collective-permute-start.6 = (bf16[32,1024]{1,0:T(8,128)(2,1)S(1)}, bf16[32,1024]{1,0:T(8,128)(2,1)S(1)}, u32[]{:S(2)}, u32[]{:S(2)}) collective-permute-start(bf16[32,1024]{1,0:T(8,128)(2,1)S(1)} %get-tuple-element.36.z0), channel_id=1, source_target_pairs={{0,16},{2,18},{4,20},{6,22},{8,24},{10,26},{12,28},{14,30},{16,0},... | collective-permute-start | bytes 196616 | tf_op jit(solution)/shard_map/ppermute | solution.py:21
  19.0 7.3 %collective-permute-start.5 = (bf16[32,1024]{1,0:T(8,128)(2,1)S(1)}, bf16[32,1024]{1,0:T(8,128)(2,1)S(1)}, u32[]{:S(2)}, u32[]{:S(2)}) collective-permute-start(bf16[32,1024]{1,0:T(8,128)(2,1)S(1)} %get-tuple-element.36.z0), channel_id=1, source_target_pairs={{0,8},{2,10},{4,12},{6,14},{8,0},{10,2},{12,4},{14,6},{16,24},{18,... | collective-permute-start | bytes 196616 | tf_op jit(solution)/shard_map/ppermute | solution.py:21
  26.5 1.4 %collective-permute-start.8 = (bf16[256,256]{1,0:T(8,128)(2,1)S(1)}, bf16[256,256]{1,0:T(8,128)(2,1)S(1)}, u32[]{:S(2)}, u32[]{:S(2)}) collective-permute-start(bf16[256,256]{1,0:T(8,128)(2,1)S(1)} %shard_map.125.table_mine), channel_id=1, source_target_pairs={{0,1},{1,0},{2,3},{3,2},{4,5},{5,4},{6,7},{7,6},{8,9},{9,8},{10,11... | collective-permute-start | bytes 393224 | tf_op jit(solution)/shard_map/ppermute | solution.py:498
  26.6 2.4 %collective-permute-start.9 = (f32[16,480]{1,0:T(8,128)S(1)}, f32[16,480]{1,0:T(8,128)S(1)}, u32[]{:S(2)}, u32[]{:S(2)}) collective-permute-start(f32[16,480]{1,0:T(8,128)S(1)} %get-tuple-element.42), channel_id=1, source_target_pairs={{0,1},{1,0},{2,3},{3,2},{4,5},{5,4},{6,7},{7,6},{8,9},{9,8},{10,11... | collective-permute-start | bytes 92168 | tf_op jit(solution)/shard_map/ppermute | solution.py:498
  29.2 6.5 %collective-permute-start.13 = (bf16[16,480]{1,0:T(8,128)(2,1)S(1)}, bf16[16,480]{1,0:T(8,128)(2,1)S(1)}, u32[]{:S(2)}, u32[]{:S(2)}) collective-permute-start(bf16[16,480]{1,0:T(8,128)(2,1)S(1)} %shard_map.127.p0.refs_0_.current), channel_id=1, source_target_pairs={{6,8},{8,6},{14,16},{16,14},{22,24},{24,22},{7,9},{9,7},{15,17},{1... | collective-permute-start | bytes 46088 | tf_op jit(solution)/shard_map/ppermute | solution.py:51
  29.8 6.9 %collective-permute-start.12 = (bf16[16,480]{1,0:T(8,128)(2,1)S(1)}, bf16[16,480]{1,0:T(8,128)(2,1)S(1)}, u32[]{:S(2)}, u32[]{:S(2)}) collective-permute-start(bf16[16,480]{1,0:T(8,128)(2,1)S(1)} %shard_map.127.p0.refs_0_.current), channel_id=1, source_target_pairs={{0,6},{2,4},{4,2},{6,0},{8,14},{10,12},{12,10},{14,8},{16,22},{18,... | collective-permute-start | bytes 46088 | tf_op jit(solution)/shard_map/ppermute | solution.py:21
  35.0 3.7 %collective-permute-start.11 = (bf16[16,480]{1,0:T(8,128)(2,1)S(1)}, bf16[16,480]{1,0:T(8,128)(2,1)S(1)}, u32[]{:S(2)}, u32[]{:S(2)}) collective-permute-start(bf16[16,480]{1,0:T(8,128)(2,1)S(1)} %shard_map.127.p0.refs_0_.current), channel_id=1, source_target_pairs={{0,4},{2,6},{4,0},{6,2},{8,12},{10,14},{12,8},{14,10},{16,20},{18,... | collective-permute-start | bytes 46088 | tf_op jit(solution)/shard_map/ppermute | solution.py:21
  35.0 3.7 %collective-permute-start.10 = (bf16[16,480]{1,0:T(8,128)(2,1)S(1)}, bf16[16,480]{1,0:T(8,128)(2,1)S(1)}, u32[]{:S(2)}, u32[]{:S(2)}) collective-permute-start(bf16[16,480]{1,0:T(8,128)(2,1)S(1)} %shard_map.127.p0.refs_0_.current), channel_id=1, source_target_pairs={{0,2},{2,0},{4,6},{6,4},{8,10},{10,8},{12,14},{14,12},{16,18},{18,... | collective-permute-start | bytes 46088 | tf_op jit(solution)/shard_map/ppermute | solution.py:21
  39.0 4.5 %collective-permute-start.14 = (bf16[80,480]{1,0:T(8,128)(2,1)S(1)}, bf16[80,480]{1,0:T(8,128)(2,1)S(1)}, u32[]{:S(2)}, u32[]{:S(2)}) collective-permute-start(bf16[80,480]{1,0:T(8,128)(2,1)S(1)} %get-tuple-element.44), channel_id=1, source_target_pairs={{0,1},{1,0},{2,3},{3,2},{4,5},{5,4},{6,7},{7,6},{8,9},{9,8},{10,11... | collective-permute-start | bytes 230408 | tf_op jit(solution)/shard_map/ppermute | solution.py:498
  39.1 8.1 %collective-permute-start.17 = (bf16[32,512]{1,0:T(8,128)(2,1)S(1)}, bf16[32,512]{1,0:T(8,128)(2,1)S(1)}, u32[]{:S(2)}, u32[]{:S(2)}) collective-permute-start(bf16[32,512]{1,0:T(8,128)(2,1)S(1)} %get-tuple-element.47.z0), channel_id=1, source_target_pairs={{0,24},{2,26},{4,28},{6,30},{8,16},{10,18},{12,20},{14,22},{16,8},... | collective-permute-start | bytes 98312 | tf_op jit(solution)/shard_map/ppermute | solution.py:21
  42.2 5.0 %collective-permute-start.16 = (bf16[32,512]{1,0:T(8,128)(2,1)S(1)}, bf16[32,512]{1,0:T(8,128)(2,1)S(1)}, u32[]{:S(2)}, u32[]{:S(2)}) collective-permute-start(bf16[32,512]{1,0:T(8,128)(2,1)S(1)} %get-tuple-element.47.z0), channel_id=1, source_target_pairs={{0,16},{2,18},{4,20},{6,22},{8,24},{10,26},{12,28},{14,30},{16,0},... | collective-permute-start | bytes 98312 | tf_op jit(solution)/shard_map/ppermute | solution.py:21
  42.5 4.7 %collective-permute-start.15 = (bf16[32,512]{1,0:T(8,128)(2,1)S(1)}, bf16[32,512]{1,0:T(8,128)(2,1)S(1)}, u32[]{:S(2)}, u32[]{:S(2)}) collective-permute-start(bf16[32,512]{1,0:T(8,128)(2,1)S(1)} %get-tuple-element.47.z0), channel_id=1, source_target_pairs={{0,8},{2,10},{4,12},{6,14},{8,0},{10,2},{12,4},{14,6},{16,24},{18,... | collective-permute-start | bytes 98312 | tf_op jit(solution)/shard_map/ppermute | solution.py:21
  47.1 1.2 %collective-permute-start.18 = (f32[16,480]{1,0:T(8,128)S(1)}, f32[16,480]{1,0:T(8,128)S(1)}, u32[]{:S(2)}, u32[]{:S(2)}) collective-permute-start(f32[16,480]{1,0:T(8,128)S(1)} %get-tuple-element.49), channel_id=1, source_target_pairs={{0,1},{1,0},{2,3},{3,2},{4,5},{5,4},{6,7},{7,6},{8,9},{9,8},{10,11... | collective-permute-start | bytes 92168 | tf_op jit(solution)/shard_map/ppermute | solution.py:498
  48.5 1.3 %collective-permute-start.19 = (bf16[16,480]{1,0:T(8,128)(2,1)S(1)}, bf16[16,480]{1,0:T(8,128)(2,1)S(1)}, u32[]{:S(2)}, u32[]{:S(2)}) collective-permute-start(bf16[16,480]{1,0:T(8,128)(2,1)S(1)} %shard_map.131.mine), channel_id=1, source_target_pairs={{0,1},{1,0},{2,3},{3,2},{4,5},{5,4},{6,7},{7,6},{8,9},{9,8},{10,11... | collective-permute-start | bytes 46088 | tf_op jit(solution)/shard_map/ppermute | solution.py:498

commit v5 on v4

--- a/solution.py
+++ b/solution.py
@@ -49,6 +49,13 @@
         pairs.append((low - 1, low))
         pairs.append((low, low - 1))
     return lax.ppermute(block, "near", pairs) if pairs else jnp.zeros_like(block)
+
+
+def edge_from_plane(diagonal):
+    count = lax.axis_size("near")
+    up = [(i, i + RADIX) for i in range(0, count - RADIX, RADIX)]
+    down = [(i + RADIX, i) for i in range(RADIX - 1, count - RADIX, RADIX)]
+    return lax.ppermute(diagonal, "near", up + down)
 
 
 def over_far(block):
@@ -239,7 +246,7 @@
 
 
 def pack_kernel(box, vectors, angle, factors, *refs):
-    out, edge = refs[-2:]
+    out = refs[-1]
     place = here()
     spheres, newton, width = vectors.shape
     share = newton // 2
@@ -261,7 +268,6 @@
     out[pl.ds(0, spheres), pl.ds(1024, waves)] = hi
     out[pl.ds(spheres, spheres), pl.ds(1024, waves)] = low
     out[:, pl.ds(1024 + waves, factors.shape[0])] = factors[...].T.astype(BF16)
-    edge[...] = out[:, pl.ds(0, 1024)]
 
 
 def sum_rows(member, waves):
@@ -310,10 +316,10 @@
         out[:, pl.ds(2 * waves + j * span, span)] = table[pl.ds(j * lines, lines), :].astype(BF16)
 
 
-def next_waves_kernel(p0, p1, p2, p3, p4, agg, turn, member, out, around):
+def next_waves_kernel(p0, p1, p2, p3, agg, turn, member, out, around):
     waves = agg.shape[1] // 2
     rows = p0.shape[0]
-    for j, part in enumerate((p0, p1, p2, p3, p4)):
+    for j, part in enumerate((p0, p1, p2, p3)):
         around[pl.ds(j * rows, rows), :] = part[...]
     flat = jnp.concatenate([p0[...], p1[...], p2[...], p3[...]], axis=0)
     product = jnp.dot(flat, agg[...], preferred_element_type=F32)
@@ -334,7 +340,7 @@
 
 def near_kernel(starts, emit, neighbours, live, *refs):
     place = here()
-    mine, theirs = refs[:5], refs[5 : 5 + (5 if starts[1] is not None else 1)]
+    mine, theirs = refs[:5], refs[5 : 5 + (5 if starts[1] is not None else 2)]
     refs = refs[5 + len(theirs) :]
     blocks = refs[0]
     out_mine, out_theirs = refs[1], refs[2]
@@ -360,7 +366,7 @@
                 elif starts[1] is not None:
                     value = theirs[j][rows, pl.ds(starts[1], 2 * coeffs)]
                 else:
-                    value = theirs[0][pl.ds((2 * j + r) * spheres, spheres), :]
+                    value = theirs[j // 4][pl.ds((2 * (j % 4) + r) * spheres, spheres), :]
                 value = value.astype(F32)
                 at = pl.ds(j * spheres, spheres)
                 held[at, side * 2 + r, :] = value[:, :coeffs]
@@ -509,22 +515,21 @@
     rows = spheres * newton // 2
     entries = own_boxes * listed * 2
     later = (near_blocks, agg_matrix, neighbours, live_counts)
-    message, edge = call(
+    message = call(
         pack_kernel,
-        [((rows, 1024 + waves + entries), BF16), ((rows, 1024), BF16)],
+        [((rows, 1024 + waves + entries), BF16)],
         [SM, VM, VM, VM] + [HB] * 4,
         (sphere_box, vectors, agg_angle, far_factors.reshape(entries, -1), *later),
         limit=60 << 20,
         held=True,
-    )
+    )[0]
     list_theirs = swap_far(far_list)
     current = message
     table = None
     for step in range(2):
         if step == 0:
             parts = xor_gather(message, (1, 2, 3))
-            edge = edge_rows(edge)
-            parts, edge, list_theirs = lax.optimization_barrier((parts, edge, list_theirs))
+            parts, list_theirs = lax.optimization_barrier((parts, list_theirs))
             block, turn, member, _ = call(
                 functools.partial(first_waves_kernel, boxes),
                 [
@@ -537,26 +542,27 @@
                 (*parts, agg_matrix),
             )
         else:
-            parts = [current]
-            for mask in (1, 2, 3):
-                parts.append(swap_near(current, mask))
-            edge = edge_rows(current)
+            parts = xor_gather(current, (1, 2, 3))
             block, around = call(
                 next_waves_kernel,
-                [((2 * boxes, 2 * waves), BF16), ((5 * rows, width), BF16)],
-                [VM] * 8,
-                (*parts, edge, agg_matrix, turn, member),
+                [((2 * boxes, 2 * waves), BF16), ((4 * rows, width), BF16)],
+                [VM] * 7,
+                (*parts, agg_matrix, turn, member),
             )
-        pieces = xor_gather(block, (4, 8, 12))
+        edge = edge_from_plane(parts[3])
+        pieces = [block]
+        for mask in (4, 8, 12):
+            pieces.append(swap_near(block, mask))
         mine = (*parts, edge)
         if step == 0:
             near_mine, near_theirs, held_blocks = near_call(
                 (0, 512), False, neighbours, live_counts, mine, mine, near_blocks
             )
         else:
-            theirs = swap_far(around)
+            around = swap_far(around)
+            theirs = (around, swap_far(edge))
             near_mine, near_theirs, first_image = near_call(
-                (0, None), True, neighbours, live_counts, mine, (theirs,), held_blocks
+                (0, None), True, neighbours, live_counts, mine, theirs, held_blocks
             )
         near_got = swap_far(near_theirs)
         if step == 0:

time: 50.6 us -> 54.2 us (1.071)
  waiting for transfers between devices: 8.11 us -> 12.8 us
  starting transfers between devices: 25.5 us -> 24.4 us
    ppermute x12, starting transfers between devices: 23.1 us -> 17.6 us  [swap_near(): return lax.ppermute(block, 'near', [(i, i ^ mask) for i in range(count)])]
    ppermute x2, starting transfers between devices: 1.31 us -> 6.19 us  [edge_from_plane(): return lax.ppermute(diagonal, 'near', up + down)]
    ppermute x2, waiting for transfers between devices: 0.01 us -> 3.16 us  [edge_from_plane(): return lax.ppermute(diagonal, 'near', up + down)]
    ppermute x12, waiting for transfers between devices: 5.22 us -> 6.42 us  [swap_near(): return lax.ppermute(block, 'near', [(i, i ^ mask) for i in range(count)])]
    ppermute x6 -> x7, starting transfers between devices: 1.09 us -> 0.6 us  [swap_far(): return lax.ppermute(block, 'far', [(0, 1), (1, 0)])]
    ppermute x6 -> x7, waiting for transfers between devices: 2.88 us -> 3.18 us  [swap_far(): return lax.ppermute(block, 'far', [(0, 1), (1, 0)])]
  transfers between devices with their start and end apart: 20 -> 21, of which waited for: 8 -> 11; matrix products, arithmetic and copies ran while one was open for 0% -> 0% of each run, Pallas kernels for 25% -> 23%
where the time goes in v5:
time: 54.2 us; the launch traced here: 54 us
  starting transfers between devices  24.4 us (45%)
  Pallas kernels  16 us (30%)
  waiting for transfers between devices  12.8 us (24%)
  between operations  0.83 us (2%)
    ppermute x12, starting transfers between devices, swap_near(): return lax.ppermute(block, 'near', [(i, i ^ mask) for i in range(count)])  17.6 us
    pallas_call x2, Pallas kernels, near_call(): pl.pallas_call(functools.partial(near_kernel, starts, emit), out_shape=tu...  10.4 us
    ppermute x12, waiting for transfers between devices, swap_near(): return lax.ppermute(block, 'near', [(i, i ^ mask) for i in range(count)])  6.42 us
    ppermute x2, starting transfers between devices, edge_from_plane(): return lax.ppermute(diagonal, 'near', up + down)  6.19 us
    pallas_call x9, Pallas kernels, call(): pl.pallas_call(kernel, out_shape=tuple((make(shape, kind) for shape, kind...  5.64 us
    ppermute x7, waiting for transfers between devices, swap_far(): return lax.ppermute(block, 'far', [(0, 1), (1, 0)])  3.18 us
    ppermute x2, waiting for transfers between devices, edge_from_plane(): return lax.ppermute(diagonal, 'near', up + down)  3.16 us
  transfers between devices with their start and end apart: 21, of which 11 were waited for; matrix products, arithmetic and copies ran while one was open for 0% of the time, Pallas kernels for 23%

profile of v5, /device:TPU:0, one launch (start us, length us, event | category | flops | bytes accessed | tf_op | source)
XLA Modules:
  0.0 54.0 jit_solution(1954674293977040195)
XLA Ops:
  0.7 1.1 %shard_map.122.p0.refs_0_.refs_5_.current = bf16[16,1536]{1,0:T(8,128)(2,1)S(1)} custom-call(s32[8]{0:T(128)} %box.5, bf16[8,4,480]{2,1,0:T(4,128)(2,1)} %vectors.1, f32[8,256]{1,0:T(8,128)} %angle.1, f32[256,16]{1,0:T(8,128)} %bitcast.4, bf16[8,8,2,240,240]{4,3,2,1,0:T(8,128)(2,1)} %refs_10_.1, bf16[480,512]{1,0:T(8,128)(2,1)} %agg.3, s32[8,8]{1,0:T(8,128)} %neighbours.3, ...), custom_call_target="tpu_custom_call" | custom-call | bytes 6291456 | tf_op jit(solution)/shard_map/pallas_call | solution.py:232
  1.8 4.0 %collective-permute-start.2 = (bf16[16,1536]{1,0:T(8,128)(2,1)S(1)}, bf16[16,1536]{1,0:T(8,128)(2,1)S(1)}, u32[]{:S(2)}, u32[]{:S(2)}) collective-permute-start(bf16[16,1536]{1,0:T(8,128)(2,1)S(1)} %shard_map.122.p0.refs_0_.refs_5_.current), channel_id=1, source_target_pairs={{0,6},{2,4},{4,2},{6,0},{8,14},{10,12},{12,10},{14,8},{16,22},{18,... | collective-permute-start | bytes 147464 | tf_op jit(solution)/shard_map/ppermute | solution.py:21
  5.8 0.5 collective-permute-start.1
  6.5 1.2 %collective-permute-done.3.list_theirs = s32[8,16]{1,0:T(8,128)S(1)} collective-permute-done((s32[8,16]{1,0:T(8,128)S(1)}, s32[8,16]{1,0:T(8,128)S(1)}, u32[]{:S(2)}, u32[]{:S(2)}) %collective-permute-start.3) | collective-permute-done | bytes 544 | tf_op jit(solution)/shard_map/ppermute | solution.py:504
  7.6 0.3 collective-permute-done.2.p3.refs_3_.refs_8_
  7.9 2.0 %collective-permute-done.1.p2.refs_2_.refs_7_ = bf16[16,1536]{1,0:T(8,128)(2,1)S(1)} collective-permute-done((bf16[16,1536]{1,0:T(8,128)(2,1)S(1)}, bf16[16,1536]{1,0:T(8,128)(2,1)S(1)}, u32[]{:S(2)}, u32[]{:S(2)}) %collective-permute-start.1) | collective-permute-done | bytes 49184 | tf_op jit(solution)/shard_map/ppermute | solution.py:21
  9.9 0.5 collective-permute-done.p1.refs_1_.refs_6_
  10.4 0.9 %shard_map.123 = (bf16[32,1024]{1,0:T(8,128)(2,1)S(1)}, f32[64,512]{1,0:T(8,128)S(1)}, bf16[64,32]{1,0:T(8,128)(2,1)S(1)}, f32[64,256]{1,0:T(8,128)}) custom-call(bf16[16,1536]{1,0:T(8,128)(2,1)S(1)} %shard_map.122.p0.refs_0_.refs_5_.current, bf16[16,1536]{1,0:T(8,128)(2,1)S(1)} %collective-permute-done.p1.refs_1_.refs_6_, ...), custom_call_target="tpu_custom_call" | custom-call | bytes 6291456 | tf_op jit(solution)/shard_map/pallas_call | solution.py:232
  11.3 3.6 %collective-permute-start.6 = (bf16[32,1024]{1,0:T(8,128)(2,1)S(1)}, bf16[32,1024]{1,0:T(8,128)(2,1)S(1)}, u32[]{:S(2)}, u32[]{:S(2)}) collective-permute-start(bf16[32,1024]{1,0:T(8,128)(2,1)S(1)} %get-tuple-element.30.z0), channel_id=1, source_target_pairs={{0,24},{2,26},{4,28},{6,30},{8,16},{10,18},{12,20},{14,22},{16,8},... | collective-permute-start | bytes 196616 | tf_op jit(solution)/shard_map/ppermute | solution.py:21
  14.9 0.8 %collective-permute-start.4 = (bf16[32,1024]{1,0:T(8,128)(2,1)S(1)}, bf16[32,1024]{1,0:T(8,128)(2,1)S(1)}, u32[]{:S(2)}, u32[]{:S(2)}) collective-permute-start(bf16[32,1024]{1,0:T(8,128)(2,1)S(1)} %get-tuple-element.30.z0), channel_id=1, source_target_pairs={{0,8},{2,10},{4,12},{6,14},{8,0},{10,2},{12,4},{14,6},{16,24},{18,... | collective-permute-start | bytes 196616 | tf_op jit(solution)/shard_map/ppermute | solution.py:21
  15.7 3.1 %collective-permute-start.7 = (bf16[16,1536]{1,0:T(8,128)(2,1)S(1)}, bf16[16,1536]{1,0:T(8,128)(2,1)S(1)}, u32[]{:S(2)}, u32[]{:S(2)}) collective-permute-start(bf16[16,1536]{1,0:T(8,128)(2,1)S(1)} %collective-permute-done.2.p3.refs_3_.refs_8_), channel_id=1, source_target_pairs={{0,8},{8,16},{16,24},{14,6},{22,14},{30,22},{1,9},{9,17},{17,25},{... | collective-permute-start | bytes 147464 | tf_op jit(solution)/shard_map/ppermute | solution.py:58
  18.9 1.7 %collective-permute-done.7.refs_4_.refs_9_ = bf16[16,1536]{1,0:T(8,128)(2,1)S(1)} collective-permute-done((bf16[16,1536]{1,0:T(8,128)(2,1)S(1)}, bf16[16,1536]{1,0:T(8,128)(2,1)S(1)}, u32[]{:S(2)}, u32[]{:S(2)}) %collective-permute-start.7) | collective-permute-done | bytes 49184 | tf_op jit(solution)/shard_map/ppermute | solution.py:58
  20.6 6.7 %shard_map.124 = (f32[16,480]{1,0:T(8,128)S(1)}, f32[16,480]{1,0:T(8,128)S(1)}, bf16[8,8,2,240,240]{4,3,2,1,0:T(8,128)(2,1)S(1)}) custom-call(s32[8,8]{1,0:T(8,128)S(1)} %copy-done.3, s32[8]{0:T(128)S(1)} %copy-done.5, bf16[16,1536]{1,0:T(8,128)(2,1)S(1)} %shard_map.122.p0.refs_0_.refs_5_.current, ...), custom_call_target="tpu_custom_call" | custom-call | flops 117964800 | bytes 14745600 | tf_op jit(solution)/shard_map/pallas_call | solution.py:415
  27.6 0.5 collective-permute-start.9
  28.1 0.8 %collective-permute-done.8.table_theirs = bf16[256,256]{1,0:T(8,128)(2,1)S(1)} collective-permute-done((bf16[256,256]{1,0:T(8,128)(2,1)S(1)}, bf16[256,256]{1,0:T(8,128)(2,1)S(1)}, u32[]{:S(2)}, u32[]{:S(2)}) %collective-permute-start.8) | collective-permute-done | bytes 131104 | tf_op jit(solution)/shard_map/ppermute | solution.py:504
  28.9 1.1 %shard_map.126.far = f32[16,480]{1,0:T(8,128)S(1)} custom-call(s32[8]{0:T(128)S(1)} %copy-done.6, s32[8,16]{1,0:T(8,128)S(1)} %copy-done.4, s32[8,16]{1,0:T(8,128)S(1)} %collective-permute-done.3.list_theirs, bf16[32,1024]{1,0:T(8,128)(2,1)S(1)} %get-tuple-element.30.z0, bf16[32,1024]{1,0:T(8,128)(2,1)S(1)} %collective-permute-done.4.z1, ...), custom_call_target="tpu_custom_call" | custom-call | bytes 6291456 | tf_op jit(solution)/shard_map/pallas_call | solution.py:232
  30.0 0.2 shard_map.127.p0.refs_0_.current
  30.2 2.8 %collective-permute-start.12 = (bf16[16,480]{1,0:T(8,128)(2,1)S(1)}, bf16[16,480]{1,0:T(8,128)(2,1)S(1)}, u32[]{:S(2)}, u32[]{:S(2)}) collective-permute-start(bf16[16,480]{1,0:T(8,128)(2,1)S(1)} %shard_map.127.p0.refs_0_.current), channel_id=1, source_target_pairs={{0,6},{2,4},{4,2},{6,0},{8,14},{10,12},{12,10},{14,8},{16,22},{18,... | collective-permute-start | bytes 46088 | tf_op jit(solution)/shard_map/ppermute | solution.py:21
  33.0 0.7 %collective-permute-start.10 = (bf16[16,480]{1,0:T(8,128)(2,1)S(1)}, bf16[16,480]{1,0:T(8,128)(2,1)S(1)}, u32[]{:S(2)}, u32[]{:S(2)}) collective-permute-start(bf16[16,480]{1,0:T(8,128)(2,1)S(1)} %shard_map.127.p0.refs_0_.current), channel_id=1, source_target_pairs={{0,2},{2,0},{4,6},{6,4},{8,10},{10,8},{12,14},{14,12},{16,18},{18,... | collective-permute-start | bytes 46088 | tf_op jit(solution)/shard_map/ppermute | solution.py:21
  33.7 1.1 %collective-permute-done.12.p3.refs_3_ = bf16[16,480]{1,0:T(8,128)(2,1)S(1)} collective-permute-done((bf16[16,480]{1,0:T(8,128)(2,1)S(1)}, bf16[16,480]{1,0:T(8,128)(2,1)S(1)}, u32[]{:S(2)}, u32[]{:S(2)}) %collective-permute-start.12) | collective-permute-done | bytes 15392 | tf_op jit(solution)/shard_map/ppermute | solution.py:21
  34.9 1.9 %collective-permute-done.11.p2.refs_2_ = bf16[16,480]{1,0:T(8,128)(2,1)S(1)} collective-permute-done((bf16[16,480]{1,0:T(8,128)(2,1)S(1)}, bf16[16,480]{1,0:T(8,128)(2,1)S(1)}, u32[]{:S(2)}, u32[]{:S(2)}) %collective-permute-start.11) | collective-permute-done | bytes 15392 | tf_op jit(solution)/shard_map/ppermute | solution.py:21
  36.7 0.3 shard_map.128
  37.1 3.1 %collective-permute-start.13 = (bf16[16,480]{1,0:T(8,128)(2,1)S(1)}, bf16[16,480]{1,0:T(8,128)(2,1)S(1)}, u32[]{:S(2)}, u32[]{:S(2)}) collective-permute-start(bf16[16,480]{1,0:T(8,128)(2,1)S(1)} %collective-permute-done.12.p3.refs_3_), channel_id=1, source_target_pairs={{0,8},{8,16},{16,24},{14,6},{22,14},{30,22},{1,9},{9,17},{17,25},{... | collective-permute-start | bytes 46088 | tf_op jit(solution)/shard_map/ppermute | solution.py:58
  40.1 1.4 %collective-permute-done.13.refs_4_ = bf16[16,480]{1,0:T(8,128)(2,1)S(1)} collective-permute-done((bf16[16,480]{1,0:T(8,128)(2,1)S(1)}, bf16[16,480]{1,0:T(8,128)(2,1)S(1)}, u32[]{:S(2)}, u32[]{:S(2)}) %collective-permute-start.13) | collective-permute-done | bytes 15392 | tf_op jit(solution)/shard_map/ppermute | solution.py:58
  41.6 4.5 %collective-permute-start.18 = (bf16[32,512]{1,0:T(8,128)(2,1)S(1)}, bf16[32,512]{1,0:T(8,128)(2,1)S(1)}, u32[]{:S(2)}, u32[]{:S(2)}) collective-permute-start(bf16[32,512]{1,0:T(8,128)(2,1)S(1)} %get-tuple-element.41.z0), channel_id=1, source_target_pairs={{0,24},{2,26},{4,28},{6,30},{8,16},{10,18},{12,20},{14,22},{16,8},... | collective-permute-start | bytes 98312 | tf_op jit(solution)/shard_map/ppermute | solution.py:21
  46.1 0.6 %collective-permute-start.16 = (bf16[32,512]{1,0:T(8,128)(2,1)S(1)}, bf16[32,512]{1,0:T(8,128)(2,1)S(1)}, u32[]{:S(2)}, u32[]{:S(2)}) collective-permute-start(bf16[32,512]{1,0:T(8,128)(2,1)S(1)} %get-tuple-element.41.z0), channel_id=1, source_target_pairs={{0,8},{2,10},{4,12},{6,14},{8,0},{10,2},{12,4},{14,6},{16,24},{18,... | collective-permute-start | bytes 98312 | tf_op jit(solution)/shard_map/ppermute | solution.py:21
  46.7 3.6 %shard_map.129 = (f32[16,480]{1,0:T(8,128)S(1)}, f32[16,480]{1,0:T(8,128)S(1)}, bf16[8,4,480]{2,1,0:T(4,128)(2,1)}) custom-call(s32[8,8]{1,0:T(8,128)S(1)} %copy-done.3, s32[8]{0:T(128)S(1)} %copy-done.5, bf16[16,480]{1,0:T(8,128)(2,1)S(1)} %shard_map.127.p0.refs_0_.current, bf16[16,480]{1,0:T(8,128)(2,1)S(1)} %collective-permute-done.10.p1.refs_1_, ...), custom_call_target="tpu_custom_call" | custom-call | flops 117964800 | bytes 14745600 | tf_op jit(solution)/shard_map/pallas_call | solution.py:415
  50.3 0.6 %collective-permute-done.17.z2 = bf16[32,512]{1,0:T(8,128)(2,1)S(1)} collective-permute-done((bf16[32,512]{1,0:T(8,128)(2,1)S(1)}, bf16[32,512]{1,0:T(8,128)(2,1)S(1)}, u32[]{:S(2)}, u32[]{:S(2)}) %collective-permute-start.17) | collective-permute-done | bytes 32800 | tf_op jit(solution)/shard_map/ppermute | solution.py:21
  50.9 1.1 %shard_map.130.far = f32[16,480]{1,0:T(8,128)S(1)} custom-call(s32[8]{0:T(128)S(1)} %copy-done.6, s32[8,16]{1,0:T(8,128)S(1)} %copy-done.4, s32[8,16]{1,0:T(8,128)S(1)} %collective-permute-done.3.list_theirs, bf16[32,512]{1,0:T(8,128)(2,1)S(1)} %get-tuple-element.41.z0, bf16[32,512]{1,0:T(8,128)(2,1)S(1)} %collective-permute-done.16.z1, ...), custom_call_target="tpu_custom_call" | custom-call | bytes 6291456 | tf_op jit(solution)/shard_map/pallas_call | solution.py:232
  52.0 0.2 shard_map.131.mine
  52.2 1.2 %collective-permute-done.20.theirs = bf16[16,480]{1,0:T(8,128)(2,1)S(1)} collective-permute-done((bf16[16,480]{1,0:T(8,128)(2,1)S(1)}, bf16[16,480]{1,0:T(8,128)(2,1)S(1)}, u32[]{:S(2)}, u32[]{:S(2)}) %collective-permute-start.20) | collective-permute-done | bytes 15392 | tf_op jit(solution)/shard_map/ppermute | solution.py:504
  53.4 0.7 %shard_map.132 = bf16[8,4,480]{2,1,0:T(4,128)(2,1)} custom-call(bf16[16,480]{1,0:T(8,128)(2,1)S(1)} %shard_map.131.mine, bf16[16,480]{1,0:T(8,128)(2,1)S(1)} %collective-permute-done.20.theirs), custom_call_target="tpu_custom_call" | custom-call | bytes 6291456 | tf_op jit(solution)/shard_map/pallas_call | solution.py:232
  (35 shorter events, 0.4 us)
Async XLA Ops:
  0.6 9.8 %copy-start = (bf16[480,512]{1,0:T(8,128)(2,1)S(1)}, bf16[480,512]{1,0:T(8,128)(2,1)}, u32[]{:S(2)}) copy-start(bf16[480,512]{1,0:T(8,128)(2,1)} %agg.3) | copy-start | bytes 1474564
  0.6 20.0 %copy-start.5 = (s32[8]{0:T(128)S(1)}, s32[8]{0:T(128)}, u32[]{:S(2)}) copy-start(s32[8]{0:T(128)} %live.3) | copy-start | bytes 100
  0.7 20.0 %copy-start.3 = (s32[8,8]{1,0:T(8,128)S(1)}, s32[8,8]{1,0:T(8,128)}, u32[]{:S(2)}) copy-start(s32[8,8]{1,0:T(8,128)} %neighbours.3) | copy-start | bytes 772
  0.7 5.8 %copy-start.4 = (s32[8,16]{1,0:T(8,128)S(1)}, s32[8,16]{1,0:T(8,128)}, u32[]{:S(2)}) copy-start(s32[8,16]{1,0:T(8,128)} %list_mine.3) | copy-start | bytes 1540
  0.7 28.3 %copy-start.1 = (bf16[512,480]{0,1:T(8,128)(2,1)S(1)}, bf16[512,480]{0,1:T(8,128)(2,1)}, u32[]{:S(2)}) copy-start(bf16[512,480]{0,1:T(8,128)(2,1)} %param.21) | copy-start | bytes 1474564
  0.7 28.3 %copy-start.6 = (s32[8]{0:T(128)S(1)}, s32[8]{0:T(128)}, u32[]{:S(2)}) copy-start(s32[8]{0:T(128)} %box.5) | copy-start | bytes 100
  0.7 29.3 %copy-start.2 = (f32[8,2,240]{2,1,0:T(2,128)S(1)}, f32[8,2,240]{2,1,0:T(2,128)}, u32[]{:S(2)}) copy-start(f32[8,2,240]{2,1,0:T(2,128)} %tmatrix.3) | copy-start | bytes 46084
  1.8 6.1 %collective-permute-start.2 = (bf16[16,1536]{1,0:T(8,128)(2,1)S(1)}, bf16[16,1536]{1,0:T(8,128)(2,1)S(1)}, u32[]{:S(2)}, u32[]{:S(2)}) collective-permute-start(bf16[16,1536]{1,0:T(8,128)(2,1)S(1)} %shard_map.122.p0.refs_0_.refs_5_.current), channel_id=1, source_target_pairs={{0,6},{2,4},{4,2},{6,0},{8,14},{10,12},{12,10},{14,8},{16,22},{18,... | collective-permute-start | bytes 147464 | tf_op jit(solution)/shard_map/ppermute | solution.py:21
  5.8 4.1 %collective-permute-start.1 = (bf16[16,1536]{1,0:T(8,128)(2,1)S(1)}, bf16[16,1536]{1,0:T(8,128)(2,1)S(1)}, u32[]{:S(2)}, u32[]{:S(2)}) collective-permute-start(bf16[16,1536]{1,0:T(8,128)(2,1)S(1)} %shard_map.122.p0.refs_0_.refs_5_.current), channel_id=1, source_target_pairs={{0,4},{2,6},{4,0},{6,2},{8,12},{10,14},{12,8},{14,10},{16,20},{18,... | collective-permute-start | bytes 147464 | tf_op jit(solution)/shard_map/ppermute | solution.py:21
  6.3 4.1 %collective-permute-start = (bf16[16,1536]{1,0:T(8,128)(2,1)S(1)}, bf16[16,1536]{1,0:T(8,128)(2,1)S(1)}, u32[]{:S(2)}, u32[]{:S(2)}) collective-permute-start(bf16[16,1536]{1,0:T(8,128)(2,1)S(1)} %shard_map.122.p0.refs_0_.refs_5_.current), channel_id=1, source_target_pairs={{0,2},{2,0},{4,6},{6,4},{8,10},{10,8},{12,14},{14,12},{16,18},{18,... | collective-permute-start | bytes 147464 | tf_op jit(solution)/shard_map/ppermute | solution.py:21
  6.5 1.2 %collective-permute-start.3 = (s32[8,16]{1,0:T(8,128)S(1)}, s32[8,16]{1,0:T(8,128)S(1)}, u32[]{:S(2)}, u32[]{:S(2)}) collective-permute-start(s32[8,16]{1,0:T(8,128)S(1)} %copy-done.4), channel_id=1, source_target_pairs={{0,1},{1,0},{2,3},{3,2},{4,5},{5,4},{6,7},{7,6},{8,9},{9,8},{10,11... | collective-permute-start | bytes 1544 | tf_op jit(solution)/shard_map/ppermute | solution.py:504
  11.3 16.0 %collective-permute-start.6 = (bf16[32,1024]{1,0:T(8,128)(2,1)S(1)}, bf16[32,1024]{1,0:T(8,128)(2,1)S(1)}, u32[]{:S(2)}, u32[]{:S(2)}) collective-permute-start(bf16[32,1024]{1,0:T(8,128)(2,1)S(1)} %get-tuple-element.30.z0), channel_id=1, source_target_pairs={{0,24},{2,26},{4,28},{6,30},{8,16},{10,18},{12,20},{14,22},{16,8},... | collective-permute-start | bytes 196616 | tf_op jit(solution)/shard_map/ppermute | solution.py:21
  14.9 12.4 %collective-permute-start.5 = (bf16[32,1024]{1,0:T(8,128)(2,1)S(1)}, bf16[32,1024]{1,0:T(8,128)(2,1)S(1)}, u32[]{:S(2)}, u32[]{:S(2)}) collective-permute-start(bf16[32,1024]{1,0:T(8,128)(2,1)S(1)} %get-tuple-element.30.z0), channel_id=1, source_target_pairs={{0,16},{2,18},{4,20},{6,22},{8,24},{10,26},{12,28},{14,30},{16,0},... | collective-permute-start | bytes 196616 | tf_op jit(solution)/shard_map/ppermute | solution.py:21
  14.9 12.4 %collective-permute-start.4 = (bf16[32,1024]{1,0:T(8,128)(2,1)S(1)}, bf16[32,1024]{1,0:T(8,128)(2,1)S(1)}, u32[]{:S(2)}, u32[]{:S(2)}) collective-permute-start(bf16[32,1024]{1,0:T(8,128)(2,1)S(1)} %get-tuple-element.30.z0), channel_id=1, source_target_pairs={{0,8},{2,10},{4,12},{6,14},{8,0},{10,2},{12,4},{14,6},{16,24},{18,... | collective-permute-start | bytes 196616 | tf_op jit(solution)/shard_map/ppermute | solution.py:21
  15.7 4.9 %collective-permute-start.7 = (bf16[16,1536]{1,0:T(8,128)(2,1)S(1)}, bf16[16,1536]{1,0:T(8,128)(2,1)S(1)}, u32[]{:S(2)}, u32[]{:S(2)}) collective-permute-start(bf16[16,1536]{1,0:T(8,128)(2,1)S(1)} %collective-permute-done.2.p3.refs_3_.refs_8_), channel_id=1, source_target_pairs={{0,8},{8,16},{16,24},{14,6},{22,14},{30,22},{1,9},{9,17},{17,25},{... | collective-permute-start | bytes 147464 | tf_op jit(solution)/shard_map/ppermute | solution.py:58
  27.5 1.4 %collective-permute-start.8 = (bf16[256,256]{1,0:T(8,128)(2,1)S(1)}, bf16[256,256]{1,0:T(8,128)(2,1)S(1)}, u32[]{:S(2)}, u32[]{:S(2)}) collective-permute-start(bf16[256,256]{1,0:T(8,128)(2,1)S(1)} %shard_map.125.table_mine), channel_id=1, source_target_pairs={{0,1},{1,0},{2,3},{3,2},{4,5},{5,4},{6,7},{7,6},{8,9},{9,8},{10,11... | collective-permute-start | bytes 393224 | tf_op jit(solution)/shard_map/ppermute | solution.py:504
  27.6 2.4 %collective-permute-start.9 = (f32[16,480]{1,0:T(8,128)S(1)}, f32[16,480]{1,0:T(8,128)S(1)}, u32[]{:S(2)}, u32[]{:S(2)}) collective-permute-start(f32[16,480]{1,0:T(8,128)S(1)} %get-tuple-element.36), channel_id=1, source_target_pairs={{0,1},{1,0},{2,3},{3,2},{4,5},{5,4},{6,7},{7,6},{8,9},{9,8},{10,11... | collective-permute-start | bytes 92168 | tf_op jit(solution)/shard_map/ppermute | solution.py:504
  30.2 4.7 %collective-permute-start.12 = (bf16[16,480]{1,0:T(8,128)(2,1)S(1)}, bf16[16,480]{1,0:T(8,128)(2,1)S(1)}, u32[]{:S(2)}, u32[]{:S(2)}) collective-permute-start(bf16[16,480]{1,0:T(8,128)(2,1)S(1)} %shard_map.127.p0.refs_0_.current), channel_id=1, source_target_pairs={{0,6},{2,4},{4,2},{6,0},{8,14},{10,12},{12,10},{14,8},{16,22},{18,... | collective-permute-start | bytes 46088 | tf_op jit(solution)/shard_map/ppermute | solution.py:21
  33.0 3.7 %collective-permute-start.11 = (bf16[16,480]{1,0:T(8,128)(2,1)S(1)}, bf16[16,480]{1,0:T(8,128)(2,1)S(1)}, u32[]{:S(2)}, u32[]{:S(2)}) collective-permute-start(bf16[16,480]{1,0:T(8,128)(2,1)S(1)} %shard_map.127.p0.refs_0_.current), channel_id=1, source_target_pairs={{0,4},{2,6},{4,0},{6,2},{8,12},{10,14},{12,8},{14,10},{16,20},{18,... | collective-permute-start | bytes 46088 | tf_op jit(solution)/shard_map/ppermute | solution.py:21
  33.0 3.7 %collective-permute-start.10 = (bf16[16,480]{1,0:T(8,128)(2,1)S(1)}, bf16[16,480]{1,0:T(8,128)(2,1)S(1)}, u32[]{:S(2)}, u32[]{:S(2)}) collective-permute-start(bf16[16,480]{1,0:T(8,128)(2,1)S(1)} %shard_map.127.p0.refs_0_.current), channel_id=1, source_target_pairs={{0,2},{2,0},{4,6},{6,4},{8,10},{10,8},{12,14},{14,12},{16,18},{18,... | collective-permute-start | bytes 46088 | tf_op jit(solution)/shard_map/ppermute | solution.py:21
  37.1 9.6 %collective-permute-start.14 = (bf16[64,480]{1,0:T(8,128)(2,1)S(1)}, bf16[64,480]{1,0:T(8,128)(2,1)S(1)}, u32[]{:S(2)}, u32[]{:S(2)}) collective-permute-start(bf16[64,480]{1,0:T(8,128)(2,1)S(1)} %get-tuple-element.38), channel_id=1, source_target_pairs={{0,1},{1,0},{2,3},{3,2},{4,5},{5,4},{6,7},{7,6},{8,9},{9,8},{10,11... | collective-permute-start | bytes 184328 | tf_op jit(solution)/shard_map/ppermute | solution.py:504
  37.1 4.5 %collective-permute-start.13 = (bf16[16,480]{1,0:T(8,128)(2,1)S(1)}, bf16[16,480]{1,0:T(8,128)(2,1)S(1)}, u32[]{:S(2)}, u32[]{:S(2)}) collective-permute-start(bf16[16,480]{1,0:T(8,128)(2,1)S(1)} %collective-permute-done.12.p3.refs_3_), channel_id=1, source_target_pairs={{0,8},{8,16},{16,24},{14,6},{22,14},{30,22},{1,9},{9,17},{17,25},{... | collective-permute-start | bytes 46088 | tf_op jit(solution)/shard_map/ppermute | solution.py:58
  41.6 5.1 %collective-permute-start.15 = (bf16[16,480]{1,0:T(8,128)(2,1)S(1)}, bf16[16,480]{1,0:T(8,128)(2,1)S(1)}, u32[]{:S(2)}, u32[]{:S(2)}) collective-permute-start(bf16[16,480]{1,0:T(8,128)(2,1)S(1)} %collective-permute-done.13.refs_4_), channel_id=1, source_target_pairs={{0,1},{1,0},{2,3},{3,2},{4,5},{5,4},{6,7},{7,6},{8,9},{9,8},{10,11... | collective-permute-start | bytes 46088 | tf_op jit(solution)/shard_map/ppermute | solution.py:504
  41.6 8.7 %collective-permute-start.18 = (bf16[32,512]{1,0:T(8,128)(2,1)S(1)}, bf16[32,512]{1,0:T(8,128)(2,1)S(1)}, u32[]{:S(2)}, u32[]{:S(2)}) collective-permute-start(bf16[32,512]{1,0:T(8,128)(2,1)S(1)} %get-tuple-element.41.z0), channel_id=1, source_target_pairs={{0,24},{2,26},{4,28},{6,30},{8,16},{10,18},{12,20},{14,22},{16,8},... | collective-permute-start | bytes 98312 | tf_op jit(solution)/shard_map/ppermute | solution.py:21
  46.1 4.8 %collective-permute-start.17 = (bf16[32,512]{1,0:T(8,128)(2,1)S(1)}, bf16[32,512]{1,0:T(8,128)(2,1)S(1)}, u32[]{:S(2)}, u32[]{:S(2)}) collective-permute-start(bf16[32,512]{1,0:T(8,128)(2,1)S(1)} %get-tuple-element.41.z0), channel_id=1, source_target_pairs={{0,16},{2,18},{4,20},{6,22},{8,24},{10,26},{12,28},{14,30},{16,0},... | collective-permute-start | bytes 98312 | tf_op jit(solution)/shard_map/ppermute | solution.py:21
  46.1 4.8 %collective-permute-start.16 = (bf16[32,512]{1,0:T(8,128)(2,1)S(1)}, bf16[32,512]{1,0:T(8,128)(2,1)S(1)}, u32[]{:S(2)}, u32[]{:S(2)}) collective-permute-start(bf16[32,512]{1,0:T(8,128)(2,1)S(1)} %get-tuple-element.41.z0), channel_id=1, source_target_pairs={{0,8},{2,10},{4,12},{6,14},{8,0},{10,2},{12,4},{14,6},{16,24},{18,... | collective-permute-start | bytes 98312 | tf_op jit(solution)/shard_map/ppermute | solution.py:21
  50.3 1.7 %collective-permute-start.19 = (f32[16,480]{1,0:T(8,128)S(1)}, f32[16,480]{1,0:T(8,128)S(1)}, u32[]{:S(2)}, u32[]{:S(2)}) collective-permute-start(f32[16,480]{1,0:T(8,128)S(1)} %get-tuple-element.43), channel_id=1, source_target_pairs={{0,1},{1,0},{2,3},{3,2},{4,5},{5,4},{6,7},{7,6},{8,9},{9,8},{10,11... | collective-permute-start | bytes 92168 | tf_op jit(solution)/shard_map/ppermute | solution.py:504
  52.2 1.2 %collective-permute-start.20 = (bf16[16,480]{1,0:T(8,128)(2,1)S(1)}, bf16[16,480]{1,0:T(8,128)(2,1)S(1)}, u32[]{:S(2)}, u32[]{:S(2)}) collective-permute-start(bf16[16,480]{1,0:T(8,128)(2,1)S(1)} %shard_map.131.mine), channel_id=1, source_target_pairs={{0,1},{1,0},{2,3},{3,2},{4,5},{5,4},{6,7},{7,6},{8,9},{9,8},{10,11... | collective-permute-start | bytes 46088 | tf_op jit(solution)/shard_map/ppermute | solution.py:504

commit v6 on v5

--- a/solution.py
+++ b/solution.py
@@ -51,11 +51,25 @@
     return lax.ppermute(block, "near", pairs) if pairs else jnp.zeros_like(block)
 
 
-def edge_from_plane(diagonal):
+def edge_pairs():
     count = lax.axis_size("near")
     up = [(i, i + RADIX) for i in range(0, count - RADIX, RADIX)]
     down = [(i + RADIX, i) for i in range(RADIX - 1, count - RADIX, RADIX)]
-    return lax.ppermute(diagonal, "near", up + down)
+    return up + down
+
+
+def edge_from_plane(diagonal):
+    return lax.ppermute(diagonal, "near", edge_pairs())
+
+
+def edge_of_second_core(diagonal):
+    pairs = [(2 * source + 1, 2 * target + 1) for source, target in edge_pairs()]
+    return lax.ppermute(diagonal, ("near", "far"), pairs)
+
+
+def edge_to_first_core(edge):
+    ends = sorted(target for _, target in edge_pairs())
+    return lax.ppermute(edge, ("near", "far"), [(2 * i + 1, 2 * i) for i in ends])
 
 
 def over_far(block):
@@ -340,7 +354,7 @@
 
 def near_kernel(starts, emit, neighbours, live, *refs):
     place = here()
-    mine, theirs = refs[:5], refs[5 : 5 + (5 if starts[1] is not None else 2)]
+    mine, theirs = refs[:5], refs[5 : 5 + (1 if starts[1] is not None else 2)]
     refs = refs[5 + len(theirs) :]
     blocks = refs[0]
     out_mine, out_theirs = refs[1], refs[2]
@@ -361,10 +375,13 @@
         for side in range(2):
             for r in range(2):
                 rows = pl.ds(r * spheres, spheres)
-                if side == 0:
+                if starts[1] is not None:
+                    value = mine[j][rows, pl.ds(starts[side], 2 * coeffs)]
+                    if j == 4:
+                        other = theirs[0][rows, pl.ds(starts[1 - side], 2 * coeffs)]
+                        value = jnp.where(place[0] == 0, other, value)
+                elif side == 0:
                     value = mine[j][rows, pl.ds(0, 2 * coeffs)]
-                elif starts[1] is not None:
-                    value = theirs[j][rows, pl.ds(starts[1], 2 * coeffs)]
                 else:
                     value = theirs[j // 4][pl.ds((2 * (j % 4) + r) * spheres, spheres), :]
                 value = value.astype(F32)
@@ -549,14 +566,15 @@
                 [VM] * 7,
                 (*parts, agg_matrix, turn, member),
             )
-        edge = edge_from_plane(parts[3])
+        edge = edge_from_plane(parts[3]) if step else edge_of_second_core(parts[3])
         pieces = [block]
         for mask in (4, 8, 12):
             pieces.append(swap_near(block, mask))
         mine = (*parts, edge)
         if step == 0:
+            passed = edge_to_first_core(edge)
             near_mine, near_theirs, held_blocks = near_call(
-                (0, 512), False, neighbours, live_counts, mine, mine, near_blocks
+                (0, 512), False, neighbours, live_counts, mine, (passed,), near_blocks
             )
         else:
             around = swap_far(around)

time: 54.2 us -> 52 us (0.959)
  waiting for transfers between devices: 12.8 us -> 11.1 us
  starting transfers between devices: 24.4 us -> 23.8 us
    ppermute x2 -> x3, starting transfers between devices: 6.19 us -> 4.36 us  [the longest x1 3.06 us: edge_from_plane(): return lax.ppermute(diagonal, 'near', edge_pairs())]
    ppermute x2 -> x3, waiting for transfers between devices: 3.16 us -> 1.43 us  [the longest x1 1.43 us: edge_from_plane(): return lax.ppermute(diagonal, 'near', edge_pairs())]
    ppermute x12, starting transfers between devices: 17.6 us -> 18.9 us  [swap_near(): return lax.ppermute(block, 'near', [(i, i ^ mask) for i in range(count)])]
  transfers between devices with their start and end apart: 21 -> 22, of which waited for: 11 -> 10; matrix products, arithmetic and copies ran while one was open for 0% -> 0% of each run, Pallas kernels for 23% -> 26%
where the time goes in v6:
time: 52 us; the launch traced here: 51.9 us
  starting transfers between devices  23.8 us (46%)
  Pallas kernels  16 us (31%)
  waiting for transfers between devices  11.1 us (21%)
  between operations  0.87 us (2%)
    ppermute x12, starting transfers between devices, swap_near(): return lax.ppermute(block, 'near', [(i, i ^ mask) for i in range(count)])  18.9 us
    pallas_call x2, Pallas kernels, near_call(): pl.pallas_call(functools.partial(near_kernel, starts, emit), out_shape=tu...  10.3 us
    ppermute x12, waiting for transfers between devices, swap_near(): return lax.ppermute(block, 'near', [(i, i ^ mask) for i in range(count)])  6.5 us
    pallas_call x9, Pallas kernels, call(): pl.pallas_call(kernel, out_shape=tuple((make(shape, kind) for shape, kind...  5.66 us
    ppermute x7, waiting for transfers between devices, swap_far(): return lax.ppermute(block, 'far', [(0, 1), (1, 0)])  3.18 us
    ppermute x1, starting transfers between devices, edge_from_plane(): return lax.ppermute(diagonal, 'near', edge_pairs())  3.06 us
    ppermute x1, waiting for transfers between devices, edge_from_plane(): return lax.ppermute(diagonal, 'near', edge_pairs())  1.43 us
  transfers between devices with their start and end apart: 22, of which 10 were waited for; matrix products, arithmetic and copies ran while one was open for 0% of the time, Pallas kernels for 26%

profile of v6, /device:TPU:0, one launch (start us, length us, event | category | flops | bytes accessed | tf_op | source)
XLA Modules:
  0.0 51.9 jit_solution(4048515670419465266)
XLA Ops:
  0.7 1.1 %shard_map.122.p0.refs_0_.current = bf16[16,1536]{1,0:T(8,128)(2,1)S(1)} custom-call(s32[8]{0:T(128)} %box.5, bf16[8,4,480]{2,1,0:T(4,128)(2,1)} %vectors.1, f32[8,256]{1,0:T(8,128)} %angle.1, f32[256,16]{1,0:T(8,128)} %bitcast.4, bf16[8,8,2,240,240]{4,3,2,1,0:T(8,128)(2,1)} %refs_6_.1, bf16[480,512]{1,0:T(8,128)(2,1)} %agg.3, s32[8,8]{1,0:T(8,128)} %neighbours.3, ...), custom_call_target="tpu_custom_call" | custom-call | bytes 6291456 | tf_op jit(solution)/shard_map/pallas_call | solution.py:246
  1.8 4.0 %collective-permute-start.2 = (bf16[16,1536]{1,0:T(8,128)(2,1)S(1)}, bf16[16,1536]{1,0:T(8,128)(2,1)S(1)}, u32[]{:S(2)}, u32[]{:S(2)}) collective-permute-start(bf16[16,1536]{1,0:T(8,128)(2,1)S(1)} %shard_map.122.p0.refs_0_.current), channel_id=1, source_target_pairs={{0,6},{2,4},{4,2},{6,0},{8,14},{10,12},{12,10},{14,8},{16,22},{18,... | collective-permute-start | bytes 147464 | tf_op jit(solution)/shard_map/ppermute | solution.py:21
  5.8 0.5 collective-permute-start.1
  6.5 1.2 %collective-permute-done.3.list_theirs = s32[8,16]{1,0:T(8,128)S(1)} collective-permute-done((s32[8,16]{1,0:T(8,128)S(1)}, s32[8,16]{1,0:T(8,128)S(1)}, u32[]{:S(2)}, u32[]{:S(2)}) %collective-permute-start.3) | collective-permute-done | bytes 544 | tf_op jit(solution)/shard_map/ppermute | solution.py:521
  7.6 0.3 collective-permute-done.2.p3.refs_3_
  7.9 2.0 %collective-permute-done.1.p2.refs_2_ = bf16[16,1536]{1,0:T(8,128)(2,1)S(1)} collective-permute-done((bf16[16,1536]{1,0:T(8,128)(2,1)S(1)}, bf16[16,1536]{1,0:T(8,128)(2,1)S(1)}, u32[]{:S(2)}, u32[]{:S(2)}) %collective-permute-start.1) | collective-permute-done | bytes 49184 | tf_op jit(solution)/shard_map/ppermute | solution.py:21
  9.9 0.5 collective-permute-done.p1.refs_1_
  10.4 0.7 %collective-permute-start.7 = (bf16[16,1536]{1,0:T(8,128)(2,1)S(1)}, bf16[16,1536]{1,0:T(8,128)(2,1)S(1)}, u32[]{:S(2)}, u32[]{:S(2)}) collective-permute-start(bf16[16,1536]{1,0:T(8,128)(2,1)S(1)} %collective-permute-done.2.p3.refs_3_), channel_id=1, source_target_pairs={{1,9},{9,17},{17,25},{15,7},{23,15},{31,23}} | collective-permute-start | bytes 147464 | tf_op jit(solution)/shard_map/ppermute | solution.py:67
  11.1 0.9 %shard_map.123 = (bf16[32,1024]{1,0:T(8,128)(2,1)S(1)}, f32[64,512]{1,0:T(8,128)S(1)}, bf16[64,32]{1,0:T(8,128)(2,1)S(1)}, f32[64,256]{1,0:T(8,128)}) custom-call(bf16[16,1536]{1,0:T(8,128)(2,1)S(1)} %shard_map.122.p0.refs_0_.current, bf16[16,1536]{1,0:T(8,128)(2,1)S(1)} %collective-permute-done.p1.refs_1_, ...), custom_call_target="tpu_custom_call" | custom-call | bytes 6291456 | tf_op jit(solution)/shard_map/pallas_call | solution.py:246
  12.0 3.6 %collective-permute-start.6 = (bf16[32,1024]{1,0:T(8,128)(2,1)S(1)}, bf16[32,1024]{1,0:T(8,128)(2,1)S(1)}, u32[]{:S(2)}, u32[]{:S(2)}) collective-permute-start(bf16[32,1024]{1,0:T(8,128)(2,1)S(1)} %get-tuple-element.30.z0), channel_id=1, source_target_pairs={{0,24},{2,26},{4,28},{6,30},{8,16},{10,18},{12,20},{14,22},{16,8},... | collective-permute-start | bytes 196616 | tf_op jit(solution)/shard_map/ppermute | solution.py:21
  15.6 0.8 %collective-permute-start.4 = (bf16[32,1024]{1,0:T(8,128)(2,1)S(1)}, bf16[32,1024]{1,0:T(8,128)(2,1)S(1)}, u32[]{:S(2)}, u32[]{:S(2)}) collective-permute-start(bf16[32,1024]{1,0:T(8,128)(2,1)S(1)} %get-tuple-element.30.z0), channel_id=1, source_target_pairs={{0,8},{2,10},{4,12},{6,14},{8,0},{10,2},{12,4},{14,6},{16,24},{18,... | collective-permute-start | bytes 196616 | tf_op jit(solution)/shard_map/ppermute | solution.py:21
  16.4 0.7 %collective-permute-start.8 = (bf16[16,1536]{1,0:T(8,128)(2,1)S(1)}, bf16[16,1536]{1,0:T(8,128)(2,1)S(1)}, u32[]{:S(2)}, u32[]{:S(2)}) collective-permute-start(bf16[16,1536]{1,0:T(8,128)(2,1)S(1)} %collective-permute-done.7.refs_4_), channel_id=1, source_target_pairs={{7,6},{9,8},{15,14},{17,16},{23,22},{25,24}} | collective-permute-start | bytes 147464 | tf_op jit(solution)/shard_map/ppermute | solution.py:72
  17.1 6.7 %shard_map.124 = (f32[16,480]{1,0:T(8,128)S(1)}, f32[16,480]{1,0:T(8,128)S(1)}, bf16[8,8,2,240,240]{4,3,2,1,0:T(8,128)(2,1)S(1)}) custom-call(s32[8,8]{1,0:T(8,128)S(1)} %copy-done.3, s32[8]{0:T(128)S(1)} %copy-done.5, bf16[16,1536]{1,0:T(8,128)(2,1)S(1)} %shard_map.122.p0.refs_0_.current, bf16[16,1536]{1,0:T(8,128)(2,1)S(1)} %collective-permute-done.p1.refs_1_, ...), custom_call_target="tpu_custom_call" | custom-call | flops 117964800 | bytes 14745600 | tf_op jit(solution)/shard_map/pallas_call | solution.py:432
  24.1 0.5 collective-permute-start.10
  24.6 0.8 %collective-permute-done.9.table_theirs = bf16[256,256]{1,0:T(8,128)(2,1)S(1)} collective-permute-done((bf16[256,256]{1,0:T(8,128)(2,1)S(1)}, bf16[256,256]{1,0:T(8,128)(2,1)S(1)}, u32[]{:S(2)}, u32[]{:S(2)}) %collective-permute-start.9) | collective-permute-done | bytes 131104 | tf_op jit(solution)/shard_map/ppermute | solution.py:521
  25.4 1.1 %shard_map.126.far = f32[16,480]{1,0:T(8,128)S(1)} custom-call(s32[8]{0:T(128)S(1)} %copy-done.6, s32[8,16]{1,0:T(8,128)S(1)} %copy-done.4, s32[8,16]{1,0:T(8,128)S(1)} %collective-permute-done.3.list_theirs, bf16[32,1024]{1,0:T(8,128)(2,1)S(1)} %get-tuple-element.30.z0, bf16[32,1024]{1,0:T(8,128)(2,1)S(1)} %collective-permute-done.4.z1, ...), custom_call_target="tpu_custom_call" | custom-call | bytes 6291456 | tf_op jit(solution)/shard_map/pallas_call | solution.py:246
  26.5 0.2 shard_map.127.p0.refs_0_.current
  26.7 4.1 %collective-permute-start.13 = (bf16[16,480]{1,0:T(8,128)(2,1)S(1)}, bf16[16,480]{1,0:T(8,128)(2,1)S(1)}, u32[]{:S(2)}, u32[]{:S(2)}) collective-permute-start(bf16[16,480]{1,0:T(8,128)(2,1)S(1)} %shard_map.127.p0.refs_0_.current), channel_id=1, source_target_pairs={{0,6},{2,4},{4,2},{6,0},{8,14},{10,12},{12,10},{14,8},{16,22},{18,... | collective-permute-start | bytes 46088 | tf_op jit(solution)/shard_map/ppermute | solution.py:21
  30.8 0.6 %collective-permute-start.11 = (bf16[16,480]{1,0:T(8,128)(2,1)S(1)}, bf16[16,480]{1,0:T(8,128)(2,1)S(1)}, u32[]{:S(2)}, u32[]{:S(2)}) collective-permute-start(bf16[16,480]{1,0:T(8,128)(2,1)S(1)} %shard_map.127.p0.refs_0_.current), channel_id=1, source_target_pairs={{0,2},{2,0},{4,6},{6,4},{8,10},{10,8},{12,14},{14,12},{16,18},{18,... | collective-permute-start | bytes 46088 | tf_op jit(solution)/shard_map/ppermute | solution.py:21
  31.4 1.1 %collective-permute-done.13.p3.refs_3_ = bf16[16,480]{1,0:T(8,128)(2,1)S(1)} collective-permute-done((bf16[16,480]{1,0:T(8,128)(2,1)S(1)}, bf16[16,480]{1,0:T(8,128)(2,1)S(1)}, u32[]{:S(2)}, u32[]{:S(2)}) %collective-permute-start.13) | collective-permute-done | bytes 15392 | tf_op jit(solution)/shard_map/ppermute | solution.py:21
  32.5 2.0 %collective-permute-done.12.p2.refs_2_ = bf16[16,480]{1,0:T(8,128)(2,1)S(1)} collective-permute-done((bf16[16,480]{1,0:T(8,128)(2,1)S(1)}, bf16[16,480]{1,0:T(8,128)(2,1)S(1)}, u32[]{:S(2)}, u32[]{:S(2)}) %collective-permute-start.12) | collective-permute-done | bytes 15392 | tf_op jit(solution)/shard_map/ppermute | solution.py:21
  34.5 0.3 shard_map.128
  34.9 3.1 %collective-permute-start.14 = (bf16[16,480]{1,0:T(8,128)(2,1)S(1)}, bf16[16,480]{1,0:T(8,128)(2,1)S(1)}, u32[]{:S(2)}, u32[]{:S(2)}) collective-permute-start(bf16[16,480]{1,0:T(8,128)(2,1)S(1)} %collective-permute-done.13.p3.refs_3_), channel_id=1, source_target_pairs={{0,8},{8,16},{16,24},{14,6},{22,14},{30,22},{1,9},{9,17},{17,25},{... | collective-permute-start | bytes 46088 | tf_op jit(solution)/shard_map/ppermute | solution.py:62
  38.0 1.4 %collective-permute-done.14.refs_4_ = bf16[16,480]{1,0:T(8,128)(2,1)S(1)} collective-permute-done((bf16[16,480]{1,0:T(8,128)(2,1)S(1)}, bf16[16,480]{1,0:T(8,128)(2,1)S(1)}, u32[]{:S(2)}, u32[]{:S(2)}) %collective-permute-start.14) | collective-permute-done | bytes 15392 | tf_op jit(solution)/shard_map/ppermute | solution.py:62
  39.4 4.5 %collective-permute-start.19 = (bf16[32,512]{1,0:T(8,128)(2,1)S(1)}, bf16[32,512]{1,0:T(8,128)(2,1)S(1)}, u32[]{:S(2)}, u32[]{:S(2)}) collective-permute-start(bf16[32,512]{1,0:T(8,128)(2,1)S(1)} %get-tuple-element.41.z0), channel_id=1, source_target_pairs={{0,24},{2,26},{4,28},{6,30},{8,16},{10,18},{12,20},{14,22},{16,8},... | collective-permute-start | bytes 98312 | tf_op jit(solution)/shard_map/ppermute | solution.py:21
  43.9 0.6 %collective-permute-start.17 = (bf16[32,512]{1,0:T(8,128)(2,1)S(1)}, bf16[32,512]{1,0:T(8,128)(2,1)S(1)}, u32[]{:S(2)}, u32[]{:S(2)}) collective-permute-start(bf16[32,512]{1,0:T(8,128)(2,1)S(1)} %get-tuple-element.41.z0), channel_id=1, source_target_pairs={{0,8},{2,10},{4,12},{6,14},{8,0},{10,2},{12,4},{14,6},{16,24},{18,... | collective-permute-start | bytes 98312 | tf_op jit(solution)/shard_map/ppermute | solution.py:21
  44.5 3.6 %shard_map.129 = (f32[16,480]{1,0:T(8,128)S(1)}, f32[16,480]{1,0:T(8,128)S(1)}, bf16[8,4,480]{2,1,0:T(4,128)(2,1)}) custom-call(s32[8,8]{1,0:T(8,128)S(1)} %copy-done.3, s32[8]{0:T(128)S(1)} %copy-done.5, bf16[16,480]{1,0:T(8,128)(2,1)S(1)} %shard_map.127.p0.refs_0_.current, bf16[16,480]{1,0:T(8,128)(2,1)S(1)} %collective-permute-done.11.p1.refs_1_, ...), custom_call_target="tpu_custom_call" | custom-call | flops 117964800 | bytes 14745600 | tf_op jit(solution)/shard_map/pallas_call | solution.py:432
  48.1 0.6 %collective-permute-done.18.z2 = bf16[32,512]{1,0:T(8,128)(2,1)S(1)} collective-permute-done((bf16[32,512]{1,0:T(8,128)(2,1)S(1)}, bf16[32,512]{1,0:T(8,128)(2,1)S(1)}, u32[]{:S(2)}, u32[]{:S(2)}) %collective-permute-start.18) | collective-permute-done | bytes 32800 | tf_op jit(solution)/shard_map/ppermute | solution.py:21
  48.7 1.1 %shard_map.130.far = f32[16,480]{1,0:T(8,128)S(1)} custom-call(s32[8]{0:T(128)S(1)} %copy-done.6, s32[8,16]{1,0:T(8,128)S(1)} %copy-done.4, s32[8,16]{1,0:T(8,128)S(1)} %collective-permute-done.3.list_theirs, bf16[32,512]{1,0:T(8,128)(2,1)S(1)} %get-tuple-element.41.z0, bf16[32,512]{1,0:T(8,128)(2,1)S(1)} %collective-permute-done.17.z1, ...), custom_call_target="tpu_custom_call" | custom-call | bytes 6291456 | tf_op jit(solution)/shard_map/pallas_call | solution.py:246
  49.8 0.2 shard_map.131.mine
  50.0 1.2 %collective-permute-done.21.theirs = bf16[16,480]{1,0:T(8,128)(2,1)S(1)} collective-permute-done((bf16[16,480]{1,0:T(8,128)(2,1)S(1)}, bf16[16,480]{1,0:T(8,128)(2,1)S(1)}, u32[]{:S(2)}, u32[]{:S(2)}) %collective-permute-start.21) | collective-permute-done | bytes 15392 | tf_op jit(solution)/shard_map/ppermute | solution.py:521
  51.2 0.7 %shard_map.132 = bf16[8,4,480]{2,1,0:T(4,128)(2,1)} custom-call(bf16[16,480]{1,0:T(8,128)(2,1)S(1)} %shard_map.131.mine, bf16[16,480]{1,0:T(8,128)(2,1)S(1)} %collective-permute-done.21.theirs), custom_call_target="tpu_custom_call" | custom-call | bytes 6291456 | tf_op jit(solution)/shard_map/pallas_call | solution.py:246
  (37 shorter events, 0.5 us)
Async XLA Ops:
  0.6 10.5 %copy-start = (bf16[480,512]{1,0:T(8,128)(2,1)S(1)}, bf16[480,512]{1,0:T(8,128)(2,1)}, u32[]{:S(2)}) copy-start(bf16[480,512]{1,0:T(8,128)(2,1)} %agg.3) | copy-start | bytes 1474564
  0.6 16.4 %copy-start.5 = (s32[8]{0:T(128)S(1)}, s32[8]{0:T(128)}, u32[]{:S(2)}) copy-start(s32[8]{0:T(128)} %live.3) | copy-start | bytes 100
  0.7 16.4 %copy-start.3 = (s32[8,8]{1,0:T(8,128)S(1)}, s32[8,8]{1,0:T(8,128)}, u32[]{:S(2)}) copy-start(s32[8,8]{1,0:T(8,128)} %neighbours.3) | copy-start | bytes 772
  0.7 5.8 %copy-start.4 = (s32[8,16]{1,0:T(8,128)S(1)}, s32[8,16]{1,0:T(8,128)}, u32[]{:S(2)}) copy-start(s32[8,16]{1,0:T(8,128)} %list_mine.3) | copy-start | bytes 1540
  0.7 24.7 %copy-start.1 = (bf16[512,480]{0,1:T(8,128)(2,1)S(1)}, bf16[512,480]{0,1:T(8,128)(2,1)}, u32[]{:S(2)}) copy-start(bf16[512,480]{0,1:T(8,128)(2,1)} %param.21) | copy-start | bytes 1474564
  0.7 24.7 %copy-start.6 = (s32[8]{0:T(128)S(1)}, s32[8]{0:T(128)}, u32[]{:S(2)}) copy-start(s32[8]{0:T(128)} %box.5) | copy-start | bytes 100
  0.7 25.8 %copy-start.2 = (f32[8,2,240]{2,1,0:T(2,128)S(1)}, f32[8,2,240]{2,1,0:T(2,128)}, u32[]{:S(2)}) copy-start(f32[8,2,240]{2,1,0:T(2,128)} %tmatrix.3) | copy-start | bytes 46084
  1.8 6.1 %collective-permute-start.2 = (bf16[16,1536]{1,0:T(8,128)(2,1)S(1)}, bf16[16,1536]{1,0:T(8,128)(2,1)S(1)}, u32[]{:S(2)}, u32[]{:S(2)}) collective-permute-start(bf16[16,1536]{1,0:T(8,128)(2,1)S(1)} %shard_map.122.p0.refs_0_.current), channel_id=1, source_target_pairs={{0,6},{2,4},{4,2},{6,0},{8,14},{10,12},{12,10},{14,8},{16,22},{18,... | collective-permute-start | bytes 147464 | tf_op jit(solution)/shard_map/ppermute | solution.py:21
  5.8 4.1 %collective-permute-start.1 = (bf16[16,1536]{1,0:T(8,128)(2,1)S(1)}, bf16[16,1536]{1,0:T(8,128)(2,1)S(1)}, u32[]{:S(2)}, u32[]{:S(2)}) collective-permute-start(bf16[16,1536]{1,0:T(8,128)(2,1)S(1)} %shard_map.122.p0.refs_0_.current), channel_id=1, source_target_pairs={{0,4},{2,6},{4,0},{6,2},{8,12},{10,14},{12,8},{14,10},{16,20},{18,... | collective-permute-start | bytes 147464 | tf_op jit(solution)/shard_map/ppermute | solution.py:21
  6.3 4.1 %collective-permute-start = (bf16[16,1536]{1,0:T(8,128)(2,1)S(1)}, bf16[16,1536]{1,0:T(8,128)(2,1)S(1)}, u32[]{:S(2)}, u32[]{:S(2)}) collective-permute-start(bf16[16,1536]{1,0:T(8,128)(2,1)S(1)} %shard_map.122.p0.refs_0_.current), channel_id=1, source_target_pairs={{0,2},{2,0},{4,6},{6,4},{8,10},{10,8},{12,14},{14,12},{16,18},{18,... | collective-permute-start | bytes 147464 | tf_op jit(solution)/shard_map/ppermute | solution.py:21
  6.5 1.2 %collective-permute-start.3 = (s32[8,16]{1,0:T(8,128)S(1)}, s32[8,16]{1,0:T(8,128)S(1)}, u32[]{:S(2)}, u32[]{:S(2)}) collective-permute-start(s32[8,16]{1,0:T(8,128)S(1)} %copy-done.4), channel_id=1, source_target_pairs={{0,1},{1,0},{2,3},{3,2},{4,5},{5,4},{6,7},{7,6},{8,9},{9,8},{10,11... | collective-permute-start | bytes 1544 | tf_op jit(solution)/shard_map/ppermute | solution.py:521
  10.4 6.0 %collective-permute-start.7 = (bf16[16,1536]{1,0:T(8,128)(2,1)S(1)}, bf16[16,1536]{1,0:T(8,128)(2,1)S(1)}, u32[]{:S(2)}, u32[]{:S(2)}) collective-permute-start(bf16[16,1536]{1,0:T(8,128)(2,1)S(1)} %collective-permute-done.2.p3.refs_3_), channel_id=1, source_target_pairs={{1,9},{9,17},{17,25},{15,7},{23,15},{31,23}} | collective-permute-start | bytes 147464 | tf_op jit(solution)/shard_map/ppermute | solution.py:67
  12.0 11.8 %collective-permute-start.6 = (bf16[32,1024]{1,0:T(8,128)(2,1)S(1)}, bf16[32,1024]{1,0:T(8,128)(2,1)S(1)}, u32[]{:S(2)}, u32[]{:S(2)}) collective-permute-start(bf16[32,1024]{1,0:T(8,128)(2,1)S(1)} %get-tuple-element.30.z0), channel_id=1, source_target_pairs={{0,24},{2,26},{4,28},{6,30},{8,16},{10,18},{12,20},{14,22},{16,8},... | collective-permute-start | bytes 196616 | tf_op jit(solution)/shard_map/ppermute | solution.py:21
  15.6 8.2 %collective-permute-start.5 = (bf16[32,1024]{1,0:T(8,128)(2,1)S(1)}, bf16[32,1024]{1,0:T(8,128)(2,1)S(1)}, u32[]{:S(2)}, u32[]{:S(2)}) collective-permute-start(bf16[32,1024]{1,0:T(8,128)(2,1)S(1)} %get-tuple-element.30.z0), channel_id=1, source_target_pairs={{0,16},{2,18},{4,20},{6,22},{8,24},{10,26},{12,28},{14,30},{16,0},... | collective-permute-start | bytes 196616 | tf_op jit(solution)/shard_map/ppermute | solution.py:21
  15.6 8.2 %collective-permute-start.4 = (bf16[32,1024]{1,0:T(8,128)(2,1)S(1)}, bf16[32,1024]{1,0:T(8,128)(2,1)S(1)}, u32[]{:S(2)}, u32[]{:S(2)}) collective-permute-start(bf16[32,1024]{1,0:T(8,128)(2,1)S(1)} %get-tuple-element.30.z0), channel_id=1, source_target_pairs={{0,8},{2,10},{4,12},{6,14},{8,0},{10,2},{12,4},{14,6},{16,24},{18,... | collective-permute-start | bytes 196616 | tf_op jit(solution)/shard_map/ppermute | solution.py:21
  16.4 0.7 %collective-permute-start.8 = (bf16[16,1536]{1,0:T(8,128)(2,1)S(1)}, bf16[16,1536]{1,0:T(8,128)(2,1)S(1)}, u32[]{:S(2)}, u32[]{:S(2)}) collective-permute-start(bf16[16,1536]{1,0:T(8,128)(2,1)S(1)} %collective-permute-done.7.refs_4_), channel_id=1, source_target_pairs={{7,6},{9,8},{15,14},{17,16},{23,22},{25,24}} | collective-permute-start | bytes 147464 | tf_op jit(solution)/shard_map/ppermute | solution.py:72
  24.0 1.4 %collective-permute-start.9 = (bf16[256,256]{1,0:T(8,128)(2,1)S(1)}, bf16[256,256]{1,0:T(8,128)(2,1)S(1)}, u32[]{:S(2)}, u32[]{:S(2)}) collective-permute-start(bf16[256,256]{1,0:T(8,128)(2,1)S(1)} %shard_map.125.table_mine), channel_id=1, source_target_pairs={{0,1},{1,0},{2,3},{3,2},{4,5},{5,4},{6,7},{7,6},{8,9},{9,8},{10,11... | collective-permute-start | bytes 393224 | tf_op jit(solution)/shard_map/ppermute | solution.py:521
  24.1 2.4 %collective-permute-start.10 = (f32[16,480]{1,0:T(8,128)S(1)}, f32[16,480]{1,0:T(8,128)S(1)}, u32[]{:S(2)}, u32[]{:S(2)}) collective-permute-start(f32[16,480]{1,0:T(8,128)S(1)} %get-tuple-element.36), channel_id=1, source_target_pairs={{0,1},{1,0},{2,3},{3,2},{4,5},{5,4},{6,7},{7,6},{8,9},{9,8},{10,11... | collective-permute-start | bytes 92168 | tf_op jit(solution)/shard_map/ppermute | solution.py:521
  26.7 5.8 %collective-permute-start.13 = (bf16[16,480]{1,0:T(8,128)(2,1)S(1)}, bf16[16,480]{1,0:T(8,128)(2,1)S(1)}, u32[]{:S(2)}, u32[]{:S(2)}) collective-permute-start(bf16[16,480]{1,0:T(8,128)(2,1)S(1)} %shard_map.127.p0.refs_0_.current), channel_id=1, source_target_pairs={{0,6},{2,4},{4,2},{6,0},{8,14},{10,12},{12,10},{14,8},{16,22},{18,... | collective-permute-start | bytes 46088 | tf_op jit(solution)/shard_map/ppermute | solution.py:21
  30.8 3.7 %collective-permute-start.12 = (bf16[16,480]{1,0:T(8,128)(2,1)S(1)}, bf16[16,480]{1,0:T(8,128)(2,1)S(1)}, u32[]{:S(2)}, u32[]{:S(2)}) collective-permute-start(bf16[16,480]{1,0:T(8,128)(2,1)S(1)} %shard_map.127.p0.refs_0_.current), channel_id=1, source_target_pairs={{0,4},{2,6},{4,0},{6,2},{8,12},{10,14},{12,8},{14,10},{16,20},{18,... | collective-permute-start | bytes 46088 | tf_op jit(solution)/shard_map/ppermute | solution.py:21
  30.8 3.7 %collective-permute-start.11 = (bf16[16,480]{1,0:T(8,128)(2,1)S(1)}, bf16[16,480]{1,0:T(8,128)(2,1)S(1)}, u32[]{:S(2)}, u32[]{:S(2)}) collective-permute-start(bf16[16,480]{1,0:T(8,128)(2,1)S(1)} %shard_map.127.p0.refs_0_.current), channel_id=1, source_target_pairs={{0,2},{2,0},{4,6},{6,4},{8,10},{10,8},{12,14},{14,12},{16,18},{18,... | collective-permute-start | bytes 46088 | tf_op jit(solution)/shard_map/ppermute | solution.py:21
  34.9 9.6 %collective-permute-start.15 = (bf16[64,480]{1,0:T(8,128)(2,1)S(1)}, bf16[64,480]{1,0:T(8,128)(2,1)S(1)}, u32[]{:S(2)}, u32[]{:S(2)}) collective-permute-start(bf16[64,480]{1,0:T(8,128)(2,1)S(1)} %get-tuple-element.38), channel_id=1, source_target_pairs={{0,1},{1,0},{2,3},{3,2},{4,5},{5,4},{6,7},{7,6},{8,9},{9,8},{10,11... | collective-permute-start | bytes 184328 | tf_op jit(solution)/shard_map/ppermute | solution.py:521
  34.9 4.5 %collective-permute-start.14 = (bf16[16,480]{1,0:T(8,128)(2,1)S(1)}, bf16[16,480]{1,0:T(8,128)(2,1)S(1)}, u32[]{:S(2)}, u32[]{:S(2)}) collective-permute-start(bf16[16,480]{1,0:T(8,128)(2,1)S(1)} %collective-permute-done.13.p3.refs_3_), channel_id=1, source_target_pairs={{0,8},{8,16},{16,24},{14,6},{22,14},{30,22},{1,9},{9,17},{17,25},{... | collective-permute-start | bytes 46088 | tf_op jit(solution)/shard_map/ppermute | solution.py:62
  39.4 5.1 %collective-permute-start.16 = (bf16[16,480]{1,0:T(8,128)(2,1)S(1)}, bf16[16,480]{1,0:T(8,128)(2,1)S(1)}, u32[]{:S(2)}, u32[]{:S(2)}) collective-permute-start(bf16[16,480]{1,0:T(8,128)(2,1)S(1)} %collective-permute-done.14.refs_4_), channel_id=1, source_target_pairs={{0,1},{1,0},{2,3},{3,2},{4,5},{5,4},{6,7},{7,6},{8,9},{9,8},{10,11... | collective-permute-start | bytes 46088 | tf_op jit(solution)/shard_map/ppermute | solution.py:521
  39.4 8.7 %collective-permute-start.19 = (bf16[32,512]{1,0:T(8,128)(2,1)S(1)}, bf16[32,512]{1,0:T(8,128)(2,1)S(1)}, u32[]{:S(2)}, u32[]{:S(2)}) collective-permute-start(bf16[32,512]{1,0:T(8,128)(2,1)S(1)} %get-tuple-element.41.z0), channel_id=1, source_target_pairs={{0,24},{2,26},{4,28},{6,30},{8,16},{10,18},{12,20},{14,22},{16,8},... | collective-permute-start | bytes 98312 | tf_op jit(solution)/shard_map/ppermute | solution.py:21
  43.9 4.8 %collective-permute-start.18 = (bf16[32,512]{1,0:T(8,128)(2,1)S(1)}, bf16[32,512]{1,0:T(8,128)(2,1)S(1)}, u32[]{:S(2)}, u32[]{:S(2)}) collective-permute-start(bf16[32,512]{1,0:T(8,128)(2,1)S(1)} %get-tuple-element.41.z0), channel_id=1, source_target_pairs={{0,16},{2,18},{4,20},{6,22},{8,24},{10,26},{12,28},{14,30},{16,0},... | collective-permute-start | bytes 98312 | tf_op jit(solution)/shard_map/ppermute | solution.py:21
  43.9 4.8 %collective-permute-start.17 = (bf16[32,512]{1,0:T(8,128)(2,1)S(1)}, bf16[32,512]{1,0:T(8,128)(2,1)S(1)}, u32[]{:S(2)}, u32[]{:S(2)}) collective-permute-start(bf16[32,512]{1,0:T(8,128)(2,1)S(1)} %get-tuple-element.41.z0), channel_id=1, source_target_pairs={{0,8},{2,10},{4,12},{6,14},{8,0},{10,2},{12,4},{14,6},{16,24},{18,... | collective-permute-start | bytes 98312 | tf_op jit(solution)/shard_map/ppermute | solution.py:21
  48.1 1.7 %collective-permute-start.20 = (f32[16,480]{1,0:T(8,128)S(1)}, f32[16,480]{1,0:T(8,128)S(1)}, u32[]{:S(2)}, u32[]{:S(2)}) collective-permute-start(f32[16,480]{1,0:T(8,128)S(1)} %get-tuple-element.43), channel_id=1, source_target_pairs={{0,1},{1,0},{2,3},{3,2},{4,5},{5,4},{6,7},{7,6},{8,9},{9,8},{10,11... | collective-permute-start | bytes 92168 | tf_op jit(solution)/shard_map/ppermute | solution.py:521
  50.0 1.2 %collective-permute-start.21 = (bf16[16,480]{1,0:T(8,128)(2,1)S(1)}, bf16[16,480]{1,0:T(8,128)(2,1)S(1)}, u32[]{:S(2)}, u32[]{:S(2)}) collective-permute-start(bf16[16,480]{1,0:T(8,128)(2,1)S(1)} %shard_map.131.mine), channel_id=1, source_target_pairs={{0,1},{1,0},{2,3},{3,2},{4,5},{5,4},{6,7},{7,6},{8,9},{9,8},{10,11... | collective-permute-start | bytes 46088 | tf_op jit(solution)/shard_map/ppermute | solution.py:521

commit v7 on v5

--- a/solution.py
+++ b/solution.py
@@ -246,7 +246,9 @@
 
 
 def pack_kernel(box, vectors, angle, factors, *refs):
-    out = refs[-1]
+    out, first_block, arrived = refs[-3:]
+    copy = pltpu.make_async_copy(refs[0].at[pl.ds(0, 1)], first_block, arrived)
+    copy.start()
     place = here()
     spheres, newton, width = vectors.shape
     share = newton // 2
@@ -268,6 +270,7 @@
     out[pl.ds(0, spheres), pl.ds(1024, waves)] = hi
     out[pl.ds(spheres, spheres), pl.ds(1024, waves)] = low
     out[:, pl.ds(1024 + waves, factors.shape[0])] = factors[...].T.astype(BF16)
+    copy.wait()
 
 
 def sum_rows(member, waves):
@@ -342,14 +345,14 @@
     place = here()
     mine, theirs = refs[:5], refs[5 : 5 + (5 if starts[1] is not None else 2)]
     refs = refs[5 + len(theirs) :]
-    blocks = refs[0]
-    out_mine, out_theirs = refs[1], refs[2]
-    image = refs[3] if emit else None
-    held = refs[4]
+    first_block, blocks = refs[:2]
+    out_mine, out_theirs = refs[2], refs[3]
+    image = refs[4] if emit else None
+    held = refs[5]
     if not emit:
-        source_blocks, blocks, arrived = blocks, refs[3], refs[5]
+        source_blocks, blocks, arrived = blocks, refs[4], refs[6]
         copies = [
-            pltpu.make_async_copy(source_blocks.at[n], blocks.at[n], arrived.at[n])
+            pltpu.make_async_copy(source_blocks.at[n + 1], blocks.at[n], arrived.at[n])
             for n in range(blocks.shape[0])
         ]
         for copy in copies:
@@ -382,8 +385,9 @@
     for n in range(spheres):
         real = jnp.zeros((8, coeffs), F32)
         imag = jnp.zeros((8, coeffs), F32)
-        if not emit:
-            copies[n].wait()
+        block = blocks.at[n - 1] if n else first_block.at[0]
+        if n and not emit:
+            copies[n - 1].wait()
         for k in range(slots):
             source = neighbours[n, k]
             chip = source // spheres
@@ -391,8 +395,8 @@
             value = held[near * spheres + source % spheres]
             alive = place[0] * slots + k < live[n]
             value = jnp.where(alive, value, 0.0).astype(BF16)
-            real += jnp.dot(value, blocks[n, k, 0], preferred_element_type=F32)
-            imag += jnp.dot(value, blocks[n, k, 1], preferred_element_type=F32)
+            real += jnp.dot(value, block[k, 0], preferred_element_type=F32)
+            imag += jnp.dot(value, block[k, 1], preferred_element_type=F32)
         near_re = real[:4] - imag[4:]
         near_im = imag[:4] + real[4:]
         for r in range(2):
@@ -403,29 +407,30 @@
             out_theirs[row, pl.ds(coeffs, coeffs)] = near_im[2 + r : 3 + r]
 
 
-def near_call(starts, emit, neighbours, live, mine, theirs, blocks):
-    spheres, slots, _, coeffs, _ = blocks.shape
+def near_call(starts, emit, neighbours, live, mine, theirs, first_block, blocks):
+    slots, _, coeffs, _ = blocks.shape[1:]
+    spheres = live.shape[0]
     rows = 2 * spheres
     outs = [jax.ShapeDtypeStruct((rows, 2 * coeffs), F32)] * 2
     if emit:
         outs.append(jax.ShapeDtypeStruct((spheres, 4, 2 * coeffs), BF16))
     else:
-        outs.append(pltpu.VMEM(blocks.shape, BF16))
+        outs.append(pltpu.VMEM((spheres - 1,) + blocks.shape[1:], BF16))
     full = [VM] * (len(mine) + len(theirs))
     return pl.pallas_call(
         functools.partial(near_kernel, starts, emit),
         out_shape=tuple(outs),
-        in_specs=[SM] * 2 + full + [VM if emit else HB],
+        in_specs=[SM] * 2 + full + [VM, VM if emit else HB],
         out_specs=(VM,) * len(outs),
         scratch_shapes=[pltpu.VMEM((5 * spheres, 8, coeffs), F32)]
-        + ([] if emit else [pltpu.SemaphoreType.DMA((spheres,))]),
+        + ([] if emit else [pltpu.SemaphoreType.DMA((spheres - 1,))]),
         cost_estimate=pl.CostEstimate(
             flops=2 * 8 * 2 * coeffs * coeffs * spheres * slots,
             bytes_accessed=blocks.size * 2,
             transcendentals=0,
         ),
         compiler_params=pltpu.CompilerParams(vmem_limit_bytes=(4 if emit else 34) << 20),
-    )(neighbours, live, *mine, *theirs, blocks)
+    )(neighbours, live, *mine, *theirs, first_block, blocks)
 
 
 def far_kernel(
@@ -515,14 +520,15 @@
     rows = spheres * newton // 2
     entries = own_boxes * listed * 2
     later = (near_blocks, agg_matrix, neighbours, live_counts)
-    message = call(
+    message, first_block = call(
         pack_kernel,
-        [((rows, 1024 + waves + entries), BF16)],
+        [((rows, 1024 + waves + entries), BF16), ((1,) + near_blocks.shape[1:], BF16)],
         [SM, VM, VM, VM] + [HB] * 4,
         (sphere_box, vectors, agg_angle, far_factors.reshape(entries, -1), *later),
-        limit=60 << 20,
+        [pltpu.SemaphoreType.DMA],
+        limit=56 << 20,
         held=True,
-    )[0]
+    )
     list_theirs = swap_far(far_list)
     current = message
     table = None
@@ -556,13 +562,13 @@
         mine = (*parts, edge)
         if step == 0:
             near_mine, near_theirs, held_blocks = near_call(
-                (0, 512), False, neighbours, live_counts, mine, mine, near_blocks
+                (0, 512), False, neighbours, live_counts, mine, mine, first_block, near_blocks
             )
         else:
             around = swap_far(around)
             theirs = (around, swap_far(edge))
             near_mine, near_theirs, first_image = near_call(
-                (0, None), True, neighbours, live_counts, mine, theirs, held_blocks
+                (0, None), True, neighbours, live_counts, mine, theirs, first_block, held_blocks
             )
         near_got = swap_far(near_theirs)
         if step == 0:

time: 54.2 us -> 55.5 us (1.024)
  Pallas kernels: 16 us -> 17.2 us
    pallas_call x9, Pallas kernels: 5.64 us -> 7.1 us  [call(): pl.pallas_call(kernel, out_shape=tuple((make(shape, kind) for shape, kind...]
  transfers between devices with their start and end apart: 21 -> 21, of which waited for: 11 -> 11; matrix products, arithmetic and copies ran while one was open for 0% -> 0% of each run, Pallas kernels for 23% -> 22%
where the time goes in v7:
time: 55.5 us; the launch traced here: 55.3 us
  starting transfers between devices  24.4 us (44%)
  Pallas kernels  17.2 us (31%)
  waiting for transfers between devices  12.8 us (23%)
  between operations  0.83 us (1%)
    ppermute x12, starting transfers between devices, swap_near(): return lax.ppermute(block, 'near', [(i, i ^ mask) for i in range(count)])  17.6 us
    pallas_call x2, Pallas kernels, near_call(): pl.pallas_call(functools.partial(near_kernel, starts, emit), out_shape=tu...  10.1 us
    pallas_call x9, Pallas kernels, call(): pl.pallas_call(kernel, out_shape=tuple((make(shape, kind) for shape, kind...  7.1 us
    ppermute x12, waiting for transfers between devices, swap_near(): return lax.ppermute(block, 'near', [(i, i ^ mask) for i in range(count)])  6.42 us
    ppermute x2, starting transfers between devices, edge_from_plane(): return lax.ppermute(diagonal, 'near', up + down)  6.2 us
    ppermute x7, waiting for transfers between devices, swap_far(): return lax.ppermute(block, 'far', [(0, 1), (1, 0)])  3.18 us
    ppermute x2, waiting for transfers between devices, edge_from_plane(): return lax.ppermute(diagonal, 'near', up + down)  3.16 us
  transfers between devices with their start and end apart: 21, of which 11 were waited for; matrix products, arithmetic and copies ran while one was open for 0% of the time, Pallas kernels for 22%

profile of v7, /device:TPU:0, one launch (start us, length us, event | category | flops | bytes accessed | tf_op | source)
XLA Modules:
  0.0 55.3 jit_solution(13410876333258403445)
XLA Ops:
  0.7 2.6 %shard_map.122 = (bf16[16,1536]{1,0:T(8,128)(2,1)S(1)}, bf16[1,8,2,240,240]{4,3,2,1,0:T(8,128)(2,1)S(1)}) custom-call(s32[8]{0:T(128)} %box.5, bf16[8,4,480]{2,1,0:T(4,128)(2,1)} %vectors.1, f32[8,256]{1,0:T(8,128)} %angle.1, f32[256,16]{1,0:T(8,128)} %bitcast.4, bf16[8,8,2,240,240]{4,3,2,1,0:T(8,128)(2,1)} %refs_11_.1, bf16[480,512]{1,0:T(8,128)(2,1)} %agg.3, ...), custom_call_target="tpu_custom_call" | custom-call | bytes 6291456 | tf_op jit(solution)/shard_map/pallas_call | solution.py:232
  3.3 4.0 %collective-permute-start.2 = (bf16[16,1536]{1,0:T(8,128)(2,1)S(1)}, bf16[16,1536]{1,0:T(8,128)(2,1)S(1)}, u32[]{:S(2)}, u32[]{:S(2)}) collective-permute-start(bf16[16,1536]{1,0:T(8,128)(2,1)S(1)} %get-tuple-element.27.p0.refs_0_.refs_5_.current), channel_id=1, source_target_pairs={{0,6},{2,4},{4,2},{6,0},{8,14},{10,12},{12,10},{14,8},{16,22},{18,... | collective-permute-start | bytes 147464 | tf_op jit(solution)/shard_map/ppermute | solution.py:21
  7.3 0.5 collective-permute-start.1
  7.9 1.2 %collective-permute-done.3.list_theirs = s32[8,16]{1,0:T(8,128)S(1)} collective-permute-done((s32[8,16]{1,0:T(8,128)S(1)}, s32[8,16]{1,0:T(8,128)S(1)}, u32[]{:S(2)}, u32[]{:S(2)}) %collective-permute-start.3) | collective-permute-done | bytes 544 | tf_op jit(solution)/shard_map/ppermute | solution.py:509
  9.1 0.3 collective-permute-done.2.p3.refs_3_.refs_8_
  9.3 2.0 %collective-permute-done.1.p2.refs_2_.refs_7_ = bf16[16,1536]{1,0:T(8,128)(2,1)S(1)} collective-permute-done((bf16[16,1536]{1,0:T(8,128)(2,1)S(1)}, bf16[16,1536]{1,0:T(8,128)(2,1)S(1)}, u32[]{:S(2)}, u32[]{:S(2)}) %collective-permute-start.1) | collective-permute-done | bytes 49184 | tf_op jit(solution)/shard_map/ppermute | solution.py:21
  11.4 0.5 collective-permute-done.p1.refs_1_.refs_6_
  11.9 0.9 %shard_map.123 = (bf16[32,1024]{1,0:T(8,128)(2,1)S(1)}, f32[64,512]{1,0:T(8,128)S(1)}, bf16[64,32]{1,0:T(8,128)(2,1)S(1)}, f32[64,256]{1,0:T(8,128)}) custom-call(bf16[16,1536]{1,0:T(8,128)(2,1)S(1)} %get-tuple-element.27.p0.refs_0_.refs_5_.current, bf16[16,1536]{1,0:T(8,128)(2,1)S(1)} %collective-permute-done.p1.refs_1_.refs_6_, ...), custom_call_target="tpu_custom_call" | custom-call | bytes 6291456 | tf_op jit(solution)/shard_map/pallas_call | solution.py:232
  12.8 3.6 %collective-permute-start.6 = (bf16[32,1024]{1,0:T(8,128)(2,1)S(1)}, bf16[32,1024]{1,0:T(8,128)(2,1)S(1)}, u32[]{:S(2)}, u32[]{:S(2)}) collective-permute-start(bf16[32,1024]{1,0:T(8,128)(2,1)S(1)} %get-tuple-element.34.z0), channel_id=1, source_target_pairs={{0,24},{2,26},{4,28},{6,30},{8,16},{10,18},{12,20},{14,22},{16,8},... | collective-permute-start | bytes 196616 | tf_op jit(solution)/shard_map/ppermute | solution.py:21
  16.4 0.8 %collective-permute-start.4 = (bf16[32,1024]{1,0:T(8,128)(2,1)S(1)}, bf16[32,1024]{1,0:T(8,128)(2,1)S(1)}, u32[]{:S(2)}, u32[]{:S(2)}) collective-permute-start(bf16[32,1024]{1,0:T(8,128)(2,1)S(1)} %get-tuple-element.34.z0), channel_id=1, source_target_pairs={{0,8},{2,10},{4,12},{6,14},{8,0},{10,2},{12,4},{14,6},{16,24},{18,... | collective-permute-start | bytes 196616 | tf_op jit(solution)/shard_map/ppermute | solution.py:21
  17.2 3.1 %collective-permute-start.7 = (bf16[16,1536]{1,0:T(8,128)(2,1)S(1)}, bf16[16,1536]{1,0:T(8,128)(2,1)S(1)}, u32[]{:S(2)}, u32[]{:S(2)}) collective-permute-start(bf16[16,1536]{1,0:T(8,128)(2,1)S(1)} %collective-permute-done.2.p3.refs_3_.refs_8_), channel_id=1, source_target_pairs={{0,8},{8,16},{16,24},{14,6},{22,14},{30,22},{1,9},{9,17},{17,25},{... | collective-permute-start | bytes 147464 | tf_op jit(solution)/shard_map/ppermute | solution.py:58
  20.3 1.7 %collective-permute-done.7.refs_4_.refs_9_ = bf16[16,1536]{1,0:T(8,128)(2,1)S(1)} collective-permute-done((bf16[16,1536]{1,0:T(8,128)(2,1)S(1)}, bf16[16,1536]{1,0:T(8,128)(2,1)S(1)}, u32[]{:S(2)}, u32[]{:S(2)}) %collective-permute-start.7) | collective-permute-done | bytes 49184 | tf_op jit(solution)/shard_map/ppermute | solution.py:58
  22.1 6.5 %shard_map.124 = (f32[16,480]{1,0:T(8,128)S(1)}, f32[16,480]{1,0:T(8,128)S(1)}, bf16[7,8,2,240,240]{4,3,2,1,0:T(8,128)(2,1)S(1)}) custom-call(s32[8,8]{1,0:T(8,128)S(1)} %copy-done.3, s32[8]{0:T(128)S(1)} %copy-done.5, bf16[16,1536]{1,0:T(8,128)(2,1)S(1)} %get-tuple-element.27.p0.refs_0_.refs_5_.current, ...), custom_call_target="tpu_custom_call" | custom-call | flops 117964800 | bytes 14745600 | tf_op jit(solution)/shard_map/pallas_call | solution.py:420
  28.8 0.5 collective-permute-start.9
  29.3 0.8 %collective-permute-done.8.table_theirs = bf16[256,256]{1,0:T(8,128)(2,1)S(1)} collective-permute-done((bf16[256,256]{1,0:T(8,128)(2,1)S(1)}, bf16[256,256]{1,0:T(8,128)(2,1)S(1)}, u32[]{:S(2)}, u32[]{:S(2)}) %collective-permute-start.8) | collective-permute-done | bytes 131104 | tf_op jit(solution)/shard_map/ppermute | solution.py:509
  30.2 1.1 %shard_map.126.far = f32[16,480]{1,0:T(8,128)S(1)} custom-call(s32[8]{0:T(128)S(1)} %copy-done.6, s32[8,16]{1,0:T(8,128)S(1)} %copy-done.4, s32[8,16]{1,0:T(8,128)S(1)} %collective-permute-done.3.list_theirs, bf16[32,1024]{1,0:T(8,128)(2,1)S(1)} %get-tuple-element.34.z0, bf16[32,1024]{1,0:T(8,128)(2,1)S(1)} %collective-permute-done.4.z1, ...), custom_call_target="tpu_custom_call" | custom-call | bytes 6291456 | tf_op jit(solution)/shard_map/pallas_call | solution.py:232
  31.3 0.2 shard_map.127.p0.refs_0_.current
  31.4 2.8 %collective-permute-start.12 = (bf16[16,480]{1,0:T(8,128)(2,1)S(1)}, bf16[16,480]{1,0:T(8,128)(2,1)S(1)}, u32[]{:S(2)}, u32[]{:S(2)}) collective-permute-start(bf16[16,480]{1,0:T(8,128)(2,1)S(1)} %shard_map.127.p0.refs_0_.current), channel_id=1, source_target_pairs={{0,6},{2,4},{4,2},{6,0},{8,14},{10,12},{12,10},{14,8},{16,22},{18,... | collective-permute-start | bytes 46088 | tf_op jit(solution)/shard_map/ppermute | solution.py:21
  34.2 0.7 %collective-permute-start.10 = (bf16[16,480]{1,0:T(8,128)(2,1)S(1)}, bf16[16,480]{1,0:T(8,128)(2,1)S(1)}, u32[]{:S(2)}, u32[]{:S(2)}) collective-permute-start(bf16[16,480]{1,0:T(8,128)(2,1)S(1)} %shard_map.127.p0.refs_0_.current), channel_id=1, source_target_pairs={{0,2},{2,0},{4,6},{6,4},{8,10},{10,8},{12,14},{14,12},{16,18},{18,... | collective-permute-start | bytes 46088 | tf_op jit(solution)/shard_map/ppermute | solution.py:21
  34.9 1.1 %collective-permute-done.12.p3.refs_3_ = bf16[16,480]{1,0:T(8,128)(2,1)S(1)} collective-permute-done((bf16[16,480]{1,0:T(8,128)(2,1)S(1)}, bf16[16,480]{1,0:T(8,128)(2,1)S(1)}, u32[]{:S(2)}, u32[]{:S(2)}) %collective-permute-start.12) | collective-permute-done | bytes 15392 | tf_op jit(solution)/shard_map/ppermute | solution.py:21
  36.1 1.9 %collective-permute-done.11.p2.refs_2_ = bf16[16,480]{1,0:T(8,128)(2,1)S(1)} collective-permute-done((bf16[16,480]{1,0:T(8,128)(2,1)S(1)}, bf16[16,480]{1,0:T(8,128)(2,1)S(1)}, u32[]{:S(2)}, u32[]{:S(2)}) %collective-permute-start.11) | collective-permute-done | bytes 15392 | tf_op jit(solution)/shard_map/ppermute | solution.py:21
  38.0 0.3 shard_map.128
  38.3 3.1 %collective-permute-start.13 = (bf16[16,480]{1,0:T(8,128)(2,1)S(1)}, bf16[16,480]{1,0:T(8,128)(2,1)S(1)}, u32[]{:S(2)}, u32[]{:S(2)}) collective-permute-start(bf16[16,480]{1,0:T(8,128)(2,1)S(1)} %collective-permute-done.12.p3.refs_3_), channel_id=1, source_target_pairs={{0,8},{8,16},{16,24},{14,6},{22,14},{30,22},{1,9},{9,17},{17,25},{... | collective-permute-start | bytes 46088 | tf_op jit(solution)/shard_map/ppermute | solution.py:58
  41.4 1.4 %collective-permute-done.13.refs_4_ = bf16[16,480]{1,0:T(8,128)(2,1)S(1)} collective-permute-done((bf16[16,480]{1,0:T(8,128)(2,1)S(1)}, bf16[16,480]{1,0:T(8,128)(2,1)S(1)}, u32[]{:S(2)}, u32[]{:S(2)}) %collective-permute-start.13) | collective-permute-done | bytes 15392 | tf_op jit(solution)/shard_map/ppermute | solution.py:58
  42.8 4.5 %collective-permute-start.18 = (bf16[32,512]{1,0:T(8,128)(2,1)S(1)}, bf16[32,512]{1,0:T(8,128)(2,1)S(1)}, u32[]{:S(2)}, u32[]{:S(2)}) collective-permute-start(bf16[32,512]{1,0:T(8,128)(2,1)S(1)} %get-tuple-element.45.z0), channel_id=1, source_target_pairs={{0,24},{2,26},{4,28},{6,30},{8,16},{10,18},{12,20},{14,22},{16,8},... | collective-permute-start | bytes 98312 | tf_op jit(solution)/shard_map/ppermute | solution.py:21
  47.3 0.6 %collective-permute-start.16 = (bf16[32,512]{1,0:T(8,128)(2,1)S(1)}, bf16[32,512]{1,0:T(8,128)(2,1)S(1)}, u32[]{:S(2)}, u32[]{:S(2)}) collective-permute-start(bf16[32,512]{1,0:T(8,128)(2,1)S(1)} %get-tuple-element.45.z0), channel_id=1, source_target_pairs={{0,8},{2,10},{4,12},{6,14},{8,0},{10,2},{12,4},{14,6},{16,24},{18,... | collective-permute-start | bytes 98312 | tf_op jit(solution)/shard_map/ppermute | solution.py:21
  47.9 3.6 %shard_map.129 = (f32[16,480]{1,0:T(8,128)S(1)}, f32[16,480]{1,0:T(8,128)S(1)}, bf16[8,4,480]{2,1,0:T(4,128)(2,1)}) custom-call(s32[8,8]{1,0:T(8,128)S(1)} %copy-done.3, s32[8]{0:T(128)S(1)} %copy-done.5, bf16[16,480]{1,0:T(8,128)(2,1)S(1)} %shard_map.127.p0.refs_0_.current, bf16[16,480]{1,0:T(8,128)(2,1)S(1)} %collective-permute-done.10.p1.refs_1_, ...), custom_call_target="tpu_custom_call" | custom-call | flops 117964800 | bytes 12902400 | tf_op jit(solution)/shard_map/pallas_call | solution.py:420
  51.6 0.6 %collective-permute-done.17.z2 = bf16[32,512]{1,0:T(8,128)(2,1)S(1)} collective-permute-done((bf16[32,512]{1,0:T(8,128)(2,1)S(1)}, bf16[32,512]{1,0:T(8,128)(2,1)S(1)}, u32[]{:S(2)}, u32[]{:S(2)}) %collective-permute-start.17) | collective-permute-done | bytes 32800 | tf_op jit(solution)/shard_map/ppermute | solution.py:21
  52.2 1.1 %shard_map.130.far = f32[16,480]{1,0:T(8,128)S(1)} custom-call(s32[8]{0:T(128)S(1)} %copy-done.6, s32[8,16]{1,0:T(8,128)S(1)} %copy-done.4, s32[8,16]{1,0:T(8,128)S(1)} %collective-permute-done.3.list_theirs, bf16[32,512]{1,0:T(8,128)(2,1)S(1)} %get-tuple-element.45.z0, bf16[32,512]{1,0:T(8,128)(2,1)S(1)} %collective-permute-done.16.z1, ...), custom_call_target="tpu_custom_call" | custom-call | bytes 6291456 | tf_op jit(solution)/shard_map/pallas_call | solution.py:232
  53.3 0.2 shard_map.131.mine
  53.5 1.2 %collective-permute-done.20.theirs = bf16[16,480]{1,0:T(8,128)(2,1)S(1)} collective-permute-done((bf16[16,480]{1,0:T(8,128)(2,1)S(1)}, bf16[16,480]{1,0:T(8,128)(2,1)S(1)}, u32[]{:S(2)}, u32[]{:S(2)}) %collective-permute-start.20) | collective-permute-done | bytes 15392 | tf_op jit(solution)/shard_map/ppermute | solution.py:509
  54.6 0.7 %shard_map.132 = bf16[8,4,480]{2,1,0:T(4,128)(2,1)} custom-call(bf16[16,480]{1,0:T(8,128)(2,1)S(1)} %shard_map.131.mine, bf16[16,480]{1,0:T(8,128)(2,1)S(1)} %collective-permute-done.20.theirs), custom_call_target="tpu_custom_call" | custom-call | bytes 6291456 | tf_op jit(solution)/shard_map/pallas_call | solution.py:232
  (35 shorter events, 0.4 us)
Async XLA Ops:
  0.6 11.2 %copy-start = (bf16[480,512]{1,0:T(8,128)(2,1)S(1)}, bf16[480,512]{1,0:T(8,128)(2,1)}, u32[]{:S(2)}) copy-start(bf16[480,512]{1,0:T(8,128)(2,1)} %agg.3) | copy-start | bytes 1474564
  0.6 21.4 %copy-start.5 = (s32[8]{0:T(128)S(1)}, s32[8]{0:T(128)}, u32[]{:S(2)}) copy-start(s32[8]{0:T(128)} %live.3) | copy-start | bytes 100
  0.7 21.4 %copy-start.3 = (s32[8,8]{1,0:T(8,128)S(1)}, s32[8,8]{1,0:T(8,128)}, u32[]{:S(2)}) copy-start(s32[8,8]{1,0:T(8,128)} %neighbours.3) | copy-start | bytes 772
  0.7 7.3 %copy-start.4 = (s32[8,16]{1,0:T(8,128)S(1)}, s32[8,16]{1,0:T(8,128)}, u32[]{:S(2)}) copy-start(s32[8,16]{1,0:T(8,128)} %list_mine.3) | copy-start | bytes 1540
  0.7 29.5 %copy-start.1 = (bf16[512,480]{0,1:T(8,128)(2,1)S(1)}, bf16[512,480]{0,1:T(8,128)(2,1)}, u32[]{:S(2)}) copy-start(bf16[512,480]{0,1:T(8,128)(2,1)} %param.21) | copy-start | bytes 1474564
  0.7 29.5 %copy-start.6 = (s32[8]{0:T(128)S(1)}, s32[8]{0:T(128)}, u32[]{:S(2)}) copy-start(s32[8]{0:T(128)} %box.5) | copy-start | bytes 100
  3.3 28.0 %copy-start.2 = (f32[8,2,240]{2,1,0:T(2,128)S(1)}, f32[8,2,240]{2,1,0:T(2,128)}, u32[]{:S(2)}) copy-start(f32[8,2,240]{2,1,0:T(2,128)} %tmatrix.3) | copy-start | bytes 46084
  3.3 6.1 %collective-permute-start.2 = (bf16[16,1536]{1,0:T(8,128)(2,1)S(1)}, bf16[16,1536]{1,0:T(8,128)(2,1)S(1)}, u32[]{:S(2)}, u32[]{:S(2)}) collective-permute-start(bf16[16,1536]{1,0:T(8,128)(2,1)S(1)} %get-tuple-element.27.p0.refs_0_.refs_5_.current), channel_id=1, source_target_pairs={{0,6},{2,4},{4,2},{6,0},{8,14},{10,12},{12,10},{14,8},{16,22},{18,... | collective-permute-start | bytes 147464 | tf_op jit(solution)/shard_map/ppermute | solution.py:21
  7.3 4.1 %collective-permute-start.1 = (bf16[16,1536]{1,0:T(8,128)(2,1)S(1)}, bf16[16,1536]{1,0:T(8,128)(2,1)S(1)}, u32[]{:S(2)}, u32[]{:S(2)}) collective-permute-start(bf16[16,1536]{1,0:T(8,128)(2,1)S(1)} %get-tuple-element.27.p0.refs_0_.refs_5_.current), channel_id=1, source_target_pairs={{0,4},{2,6},{4,0},{6,2},{8,12},{10,14},{12,8},{14,10},{16,20},{18,... | collective-permute-start | bytes 147464 | tf_op jit(solution)/shard_map/ppermute | solution.py:21
  7.8 4.1 %collective-permute-start = (bf16[16,1536]{1,0:T(8,128)(2,1)S(1)}, bf16[16,1536]{1,0:T(8,128)(2,1)S(1)}, u32[]{:S(2)}, u32[]{:S(2)}) collective-permute-start(bf16[16,1536]{1,0:T(8,128)(2,1)S(1)} %get-tuple-element.27.p0.refs_0_.refs_5_.current), channel_id=1, source_target_pairs={{0,2},{2,0},{4,6},{6,4},{8,10},{10,8},{12,14},{14,12},{16,18},{18,... | collective-permute-start | bytes 147464 | tf_op jit(solution)/shard_map/ppermute | solution.py:21
  7.9 1.2 %collective-permute-start.3 = (s32[8,16]{1,0:T(8,128)S(1)}, s32[8,16]{1,0:T(8,128)S(1)}, u32[]{:S(2)}, u32[]{:S(2)}) collective-permute-start(s32[8,16]{1,0:T(8,128)S(1)} %copy-done.4), channel_id=1, source_target_pairs={{0,1},{1,0},{2,3},{3,2},{4,5},{5,4},{6,7},{7,6},{8,9},{9,8},{10,11... | collective-permute-start | bytes 1544 | tf_op jit(solution)/shard_map/ppermute | solution.py:509
  12.8 15.8 %collective-permute-start.6 = (bf16[32,1024]{1,0:T(8,128)(2,1)S(1)}, bf16[32,1024]{1,0:T(8,128)(2,1)S(1)}, u32[]{:S(2)}, u32[]{:S(2)}) collective-permute-start(bf16[32,1024]{1,0:T(8,128)(2,1)S(1)} %get-tuple-element.34.z0), channel_id=1, source_target_pairs={{0,24},{2,26},{4,28},{6,30},{8,16},{10,18},{12,20},{14,22},{16,8},... | collective-permute-start | bytes 196616 | tf_op jit(solution)/shard_map/ppermute | solution.py:21
  16.4 12.2 %collective-permute-start.5 = (bf16[32,1024]{1,0:T(8,128)(2,1)S(1)}, bf16[32,1024]{1,0:T(8,128)(2,1)S(1)}, u32[]{:S(2)}, u32[]{:S(2)}) collective-permute-start(bf16[32,1024]{1,0:T(8,128)(2,1)S(1)} %get-tuple-element.34.z0), channel_id=1, source_target_pairs={{0,16},{2,18},{4,20},{6,22},{8,24},{10,26},{12,28},{14,30},{16,0},... | collective-permute-start | bytes 196616 | tf_op jit(solution)/shard_map/ppermute | solution.py:21
  16.4 12.2 %collective-permute-start.4 = (bf16[32,1024]{1,0:T(8,128)(2,1)S(1)}, bf16[32,1024]{1,0:T(8,128)(2,1)S(1)}, u32[]{:S(2)}, u32[]{:S(2)}) collective-permute-start(bf16[32,1024]{1,0:T(8,128)(2,1)S(1)} %get-tuple-element.34.z0), channel_id=1, source_target_pairs={{0,8},{2,10},{4,12},{6,14},{8,0},{10,2},{12,4},{14,6},{16,24},{18,... | collective-permute-start | bytes 196616 | tf_op jit(solution)/shard_map/ppermute | solution.py:21
  17.2 4.9 %collective-permute-start.7 = (bf16[16,1536]{1,0:T(8,128)(2,1)S(1)}, bf16[16,1536]{1,0:T(8,128)(2,1)S(1)}, u32[]{:S(2)}, u32[]{:S(2)}) collective-permute-start(bf16[16,1536]{1,0:T(8,128)(2,1)S(1)} %collective-permute-done.2.p3.refs_3_.refs_8_), channel_id=1, source_target_pairs={{0,8},{8,16},{16,24},{14,6},{22,14},{30,22},{1,9},{9,17},{17,25},{... | collective-permute-start | bytes 147464 | tf_op jit(solution)/shard_map/ppermute | solution.py:58
  28.8 1.4 %collective-permute-start.8 = (bf16[256,256]{1,0:T(8,128)(2,1)S(1)}, bf16[256,256]{1,0:T(8,128)(2,1)S(1)}, u32[]{:S(2)}, u32[]{:S(2)}) collective-permute-start(bf16[256,256]{1,0:T(8,128)(2,1)S(1)} %shard_map.125.table_mine), channel_id=1, source_target_pairs={{0,1},{1,0},{2,3},{3,2},{4,5},{5,4},{6,7},{7,6},{8,9},{9,8},{10,11... | collective-permute-start | bytes 393224 | tf_op jit(solution)/shard_map/ppermute | solution.py:509
  28.8 2.4 %collective-permute-start.9 = (f32[16,480]{1,0:T(8,128)S(1)}, f32[16,480]{1,0:T(8,128)S(1)}, u32[]{:S(2)}, u32[]{:S(2)}) collective-permute-start(f32[16,480]{1,0:T(8,128)S(1)} %get-tuple-element.40), channel_id=1, source_target_pairs={{0,1},{1,0},{2,3},{3,2},{4,5},{5,4},{6,7},{7,6},{8,9},{9,8},{10,11... | collective-permute-start | bytes 92168 | tf_op jit(solution)/shard_map/ppermute | solution.py:509
  31.4 4.7 %collective-permute-start.12 = (bf16[16,480]{1,0:T(8,128)(2,1)S(1)}, bf16[16,480]{1,0:T(8,128)(2,1)S(1)}, u32[]{:S(2)}, u32[]{:S(2)}) collective-permute-start(bf16[16,480]{1,0:T(8,128)(2,1)S(1)} %shard_map.127.p0.refs_0_.current), channel_id=1, source_target_pairs={{0,6},{2,4},{4,2},{6,0},{8,14},{10,12},{12,10},{14,8},{16,22},{18,... | collective-permute-start | bytes 46088 | tf_op jit(solution)/shard_map/ppermute | solution.py:21
  34.2 3.7 %collective-permute-start.11 = (bf16[16,480]{1,0:T(8,128)(2,1)S(1)}, bf16[16,480]{1,0:T(8,128)(2,1)S(1)}, u32[]{:S(2)}, u32[]{:S(2)}) collective-permute-start(bf16[16,480]{1,0:T(8,128)(2,1)S(1)} %shard_map.127.p0.refs_0_.current), channel_id=1, source_target_pairs={{0,4},{2,6},{4,0},{6,2},{8,12},{10,14},{12,8},{14,10},{16,20},{18,... | collective-permute-start | bytes 46088 | tf_op jit(solution)/shard_map/ppermute | solution.py:21
  34.2 3.7 %collective-permute-start.10 = (bf16[16,480]{1,0:T(8,128)(2,1)S(1)}, bf16[16,480]{1,0:T(8,128)(2,1)S(1)}, u32[]{:S(2)}, u32[]{:S(2)}) collective-permute-start(bf16[16,480]{1,0:T(8,128)(2,1)S(1)} %shard_map.127.p0.refs_0_.current), channel_id=1, source_target_pairs={{0,2},{2,0},{4,6},{6,4},{8,10},{10,8},{12,14},{14,12},{16,18},{18,... | collective-permute-start | bytes 46088 | tf_op jit(solution)/shard_map/ppermute | solution.py:21
  38.3 9.6 %collective-permute-start.14 = (bf16[64,480]{1,0:T(8,128)(2,1)S(1)}, bf16[64,480]{1,0:T(8,128)(2,1)S(1)}, u32[]{:S(2)}, u32[]{:S(2)}) collective-permute-start(bf16[64,480]{1,0:T(8,128)(2,1)S(1)} %get-tuple-element.42), channel_id=1, source_target_pairs={{0,1},{1,0},{2,3},{3,2},{4,5},{5,4},{6,7},{7,6},{8,9},{9,8},{10,11... | collective-permute-start | bytes 184328 | tf_op jit(solution)/shard_map/ppermute | solution.py:509
  38.3 4.5 %collective-permute-start.13 = (bf16[16,480]{1,0:T(8,128)(2,1)S(1)}, bf16[16,480]{1,0:T(8,128)(2,1)S(1)}, u32[]{:S(2)}, u32[]{:S(2)}) collective-permute-start(bf16[16,480]{1,0:T(8,128)(2,1)S(1)} %collective-permute-done.12.p3.refs_3_), channel_id=1, source_target_pairs={{0,8},{8,16},{16,24},{14,6},{22,14},{30,22},{1,9},{9,17},{17,25},{... | collective-permute-start | bytes 46088 | tf_op jit(solution)/shard_map/ppermute | solution.py:58
  42.8 5.1 %collective-permute-start.15 = (bf16[16,480]{1,0:T(8,128)(2,1)S(1)}, bf16[16,480]{1,0:T(8,128)(2,1)S(1)}, u32[]{:S(2)}, u32[]{:S(2)}) collective-permute-start(bf16[16,480]{1,0:T(8,128)(2,1)S(1)} %collective-permute-done.13.refs_4_), channel_id=1, source_target_pairs={{0,1},{1,0},{2,3},{3,2},{4,5},{5,4},{6,7},{7,6},{8,9},{9,8},{10,11... | collective-permute-start | bytes 46088 | tf_op jit(solution)/shard_map/ppermute | solution.py:509
  42.8 8.7 %collective-permute-start.18 = (bf16[32,512]{1,0:T(8,128)(2,1)S(1)}, bf16[32,512]{1,0:T(8,128)(2,1)S(1)}, u32[]{:S(2)}, u32[]{:S(2)}) collective-permute-start(bf16[32,512]{1,0:T(8,128)(2,1)S(1)} %get-tuple-element.45.z0), channel_id=1, source_target_pairs={{0,24},{2,26},{4,28},{6,30},{8,16},{10,18},{12,20},{14,22},{16,8},... | collective-permute-start | bytes 98312 | tf_op jit(solution)/shard_map/ppermute | solution.py:21
  47.3 4.8 %collective-permute-start.17 = (bf16[32,512]{1,0:T(8,128)(2,1)S(1)}, bf16[32,512]{1,0:T(8,128)(2,1)S(1)}, u32[]{:S(2)}, u32[]{:S(2)}) collective-permute-start(bf16[32,512]{1,0:T(8,128)(2,1)S(1)} %get-tuple-element.45.z0), channel_id=1, source_target_pairs={{0,16},{2,18},{4,20},{6,22},{8,24},{10,26},{12,28},{14,30},{16,0},... | collective-permute-start | bytes 98312 | tf_op jit(solution)/shard_map/ppermute | solution.py:21
  47.3 4.8 %collective-permute-start.16 = (bf16[32,512]{1,0:T(8,128)(2,1)S(1)}, bf16[32,512]{1,0:T(8,128)(2,1)S(1)}, u32[]{:S(2)}, u32[]{:S(2)}) collective-permute-start(bf16[32,512]{1,0:T(8,128)(2,1)S(1)} %get-tuple-element.45.z0), channel_id=1, source_target_pairs={{0,8},{2,10},{4,12},{6,14},{8,0},{10,2},{12,4},{14,6},{16,24},{18,... | collective-permute-start | bytes 98312 | tf_op jit(solution)/shard_map/ppermute | solution.py:21
  51.5 1.7 %collective-permute-start.19 = (f32[16,480]{1,0:T(8,128)S(1)}, f32[16,480]{1,0:T(8,128)S(1)}, u32[]{:S(2)}, u32[]{:S(2)}) collective-permute-start(f32[16,480]{1,0:T(8,128)S(1)} %get-tuple-element.47), channel_id=1, source_target_pairs={{0,1},{1,0},{2,3},{3,2},{4,5},{5,4},{6,7},{7,6},{8,9},{9,8},{10,11... | collective-permute-start | bytes 92168 | tf_op jit(solution)/shard_map/ppermute | solution.py:509
  53.4 1.2 %collective-permute-start.20 = (bf16[16,480]{1,0:T(8,128)(2,1)S(1)}, bf16[16,480]{1,0:T(8,128)(2,1)S(1)}, u32[]{:S(2)}, u32[]{:S(2)}) collective-permute-start(bf16[16,480]{1,0:T(8,128)(2,1)S(1)} %shard_map.131.mine), channel_id=1, source_target_pairs={{0,1},{1,0},{2,3},{3,2},{4,5},{5,4},{6,7},{7,6},{8,9},{9,8},{10,11... | collective-permute-start | bytes 46088 | tf_op jit(solution)/shard_map/ppermute | solution.py:509
